TPU v7x, 32 devices: a whole 2x2x4 slice. The times are simulated.
32 devices in a mesh: ctx: 8 (over z, y), fsdp: 4 (over x, core).
Axes of the slice: x: 2, y: 2, z: 4, core: 2. Of those that a mesh axis runs over, the one named last changes fastest.
Arguments:
- hidden_in: float32 [4, 2048, 1024], P('fsdp', 'ctx'), may hold values from -6 to 6
- positions: int32 [4, 2048], P('fsdp', 'ctx'), may hold values from 0 to 1023, as said below
- mixer_gain: bfloat16 [1024], P('fsdp'), may hold values from 0.5 to 1.5
- attention_in: bfloat16 [1024, 768], P('fsdp'), may hold values from -16 to 16
- attention_out: bfloat16 [512, 1024], P('fsdp'), may hold values from -2 to 2
- mamba_in: bfloat16 [1024, 3352], P('fsdp'), may hold values from -0.1875 to 0.1875
- filter_taps: bfloat16 [4, 1792], P(None, 'fsdp'), may hold values from -3 to 3
- step_bias: bfloat16 [24], P('fsdp'), may hold values from -3 to -1
- decay_log: bfloat16 [24], P('fsdp')
- skip_gain: bfloat16 [24], P('fsdp'), may hold values from 0.5 to 2
- gated_gain: bfloat16 [1536], P('fsdp'), may hold values from 0.5 to 1.5
- mamba_out: bfloat16 [1536, 1024], P('fsdp'), may hold values from -0.15625 to 0.15625
- feed_gain: bfloat16 [1024], P('fsdp'), may hold values from 0.5 to 1.5
- gate_weight: bfloat16 [1024, 2048], P(None, 'fsdp'), may hold values from -0.1875 to 0.1875
- up_weight: bfloat16 [1024, 2048], P(None, 'fsdp'), may hold values from -0.1875 to 0.1875
- down_weight: bfloat16 [2048, 1024], P('fsdp'), may hold values from -0.125 to 0.125
- cotangent: float32 [4, 2048, 1024], P('fsdp', 'ctx'), may hold values from -6 to 6
Outputs:
- hidden_out: float32 [4, 2048, 1024], P('fsdp', 'ctx')
- input_gradient: float32 [4, 2048, 1024], P('fsdp', 'ctx')
- mixer_gain_gradient: float32 [1024], P('fsdp')
- attention_in_gradient: float32 [1024, 768], P('fsdp')
- attention_out_gradient: float32 [512, 1024], P('fsdp')
- mamba_in_gradient: float32 [1024, 3352], P('fsdp')
- filter_taps_gradient: float32 [4, 1792], P(None, 'fsdp')
- step_bias_gradient: float32 [24], P('fsdp')
- decay_log_gradient: float32 [24], P('fsdp')
- skip_gain_gradient: float32 [24], P('fsdp')
- gated_gain_gradient: float32 [1536], P('fsdp')
- mamba_out_gradient: float32 [1536, 1024], P('fsdp')
- feed_gain_gradient: float32 [1024], P('fsdp')
- gate_weight_gradient: float32 [1024, 2048], P(None, 'fsdp')
- up_weight_gradient: float32 [1024, 2048], P(None, 'fsdp')
- down_weight_gradient: float32 [2048, 1024], P('fsdp')
Inputs may be any that keep to these rules, and one draw needn't show every extreme that they name: `positions`: each row holds documents laid end to end: an entry is the token's offset from the first token of its document, 0 at a document's first token and rising by one within it. In each row one document spans exactly 1024 tokens and no document spans more.
All inputs are finite; a program needn't handle non-finite values.
Results may differ from a plain program's by a relative error of at most 0.028.
Values may be sent and summed in bfloat16 or wider, within the bound.
No kernel may reach another device: no remote copies, remote signals or barrier semaphores. Data moves between devices by JAX's collectives and lax.ppermute only.
A program may use at most 256 MiB of HBM per device.

v0:
```python
import math

import jax
import jax.numpy as jnp
from jax import lax
from jax.sharding import PartitionSpec as P

QHEADS = 8
KVHEADS = 2
HEAD = 64
MHEADS = 24
MHEAD = 64
STATE = 128
CONV = 4
DIN = 1536
XBC = 1792
QDIM = 512
KVDIM = 128


EPS = 1e-05
NEGATIVE = -1e30
ROPE_BASE = 10000.0
HIGH = lax.Precision.HIGHEST


def from_behind(value, axis, steps):
    count = lax.axis_size(axis)
    first, last = (max(0, -steps), min(count, count - steps))
    return lax.ppermute(value, axis, [(source, source + steps) for source in range(first, last)])


def prefix(shard, axis, combine, identity):
    size, mine = (lax.axis_size(axis), lax.axis_index(axis))
    everything = jax.tree.map(
        lambda part, kind: lax.all_gather(part.astype(kind), axis),
        shard,
        (jnp.bfloat16, jnp.bfloat16),
    )
    start = jax.tree.map(
        lambda part, zero: jnp.broadcast_to(jnp.asarray(zero, part.dtype), part.shape),
        shard,
        identity,
    )

    def step(k, before):
        reached = k < mine
        new = combine(
            before, jax.tree.map(lambda part, own: part[k].astype(own.dtype), everything, shard)
        )
        return jax.tree.map(lambda a, b: jnp.where(reached, a, b), new, before)

    return lax.fori_loop(0, size, step, start)


def entering(shard, axis, join, neutral):
    count = lax.axis_size(axis)
    place = lax.axis_index(axis)
    ahead = count - 1 - place
    gathered = jax.tree.map(
        lambda a, kind: lax.all_gather(a.astype(kind), axis),
        shard,
        jax.tree.map(lambda a: jnp.bfloat16 if a.dtype == jnp.float32 else a.dtype, shard),
    )
    state = jax.tree.map(lambda a, e: jnp.zeros_like(a) + jnp.asarray(e, a.dtype), shard, neutral)

    def one(step, state):
        source = count - 1 - step
        return join(
            state,
            jax.tree.map(
                lambda a, own: lax.dynamic_index_in_dim(a, source, 0, False).astype(own.dtype),
                gathered,
                shard,
            ),
        )

    return lax.fori_loop(0, ahead, one, state)


def matmul(left, right):
    return jnp.dot(left, right, preferred_element_type=jnp.float32)


def rms_forward(values, gain):
    inverse = lax.rsqrt(jnp.mean(values * values, axis=-1, keepdims=True) + EPS)
    return (values * inverse * gain, inverse)


def rms_backward(values, inverse, gain, upstream):
    scaled = gain * upstream
    inner = jnp.mean(scaled * values, axis=-1, keepdims=True)
    back = inverse * scaled - values * inverse**3 * inner
    return (back, jnp.sum(upstream * values * inverse, axis=0))


def rotary_tables(token_pos, half):
    exponent = jnp.arange(half, dtype=jnp.float32) * (2.0 / (2 * half))
    frequency = jnp.exp(-math.log(ROPE_BASE) * exponent)
    angle = token_pos.astype(jnp.float32)[:, None] * frequency[None, :]
    return (jnp.cos(angle), jnp.sin(angle))


def rotate(tensor, cosine, sine):
    half = tensor.shape[-1] // 2
    first = tensor[..., :half]
    second = tensor[..., half:]
    cos_part = cosine[:, None, :]
    sin_part = sine[:, None, :]
    return jnp.concatenate(
        [first * cos_part - second * sin_part, second * cos_part + first * sin_part], axis=-1
    )


def rotate_back(tensor, cosine, sine):
    half = tensor.shape[-1] // 2
    first = tensor[..., :half]
    second = tensor[..., half:]
    cos_part = cosine[:, None, :]
    sin_part = sine[:, None, :]
    return jnp.concatenate(
        [first * cos_part + second * sin_part, second * cos_part - first * sin_part], axis=-1
    )


def group_rows(tensor, groups):
    count, heads, width = tensor.shape
    members = heads // groups
    return (
        tensor.reshape(count, groups, members, width)
        .transpose(1, 2, 0, 3)
        .reshape(groups, members * count, width)
    )


def ungroup_rows(tensor, count):
    groups, rows, width = tensor.shape
    members = rows // count
    return (
        tensor.reshape(groups, members, count, width)
        .transpose(2, 0, 1, 3)
        .reshape(count, groups * members, width)
    )


def mixer_inputs(window, step_raw, taps, step_bias, decay_log):
    span = step_raw.shape[0]
    convolved = taps[0] * window[0:span]
    for tap in range(1, taps.shape[0]):
        convolved = convolved + taps[tap] * window[tap : tap + span]
    activated = jax.nn.silu(convolved)
    inner = activated[:, :DIN].reshape(span, MHEADS, MHEAD)
    basis = activated[:, DIN : DIN + STATE]
    reader = activated[:, DIN + STATE :]
    step = jax.nn.softplus(step_raw + step_bias)
    logdecay = -step * jnp.exp(decay_log)
    return (inner, basis, reader, step, logdecay)


def block_states(inner, basis, step, logdecay):
    cumulative = jnp.cumsum(logdecay, axis=0)
    weight = jnp.exp(cumulative[-1][None, :] - cumulative) * step
    state = jnp.einsum("thp,tn->hpn", inner * weight[:, :, None], basis, precision=HIGH)
    return (state, jnp.exp(cumulative[-1]))


def block_outputs(inner, basis, reader, step, logdecay, incoming, gate_z, skip):
    span = step.shape[0]
    cumulative = jnp.cumsum(logdecay, axis=0)
    intersection = jnp.dot(reader, basis.T, precision=HIGH)
    order = jnp.arange(span, dtype=jnp.int32)
    causal = (order[:, None] >= order[None, :])[:, :, None]
    gap = cumulative[:, None, :] - cumulative[None, :, :]
    decay = jnp.where(causal, jnp.exp(jnp.where(causal, gap, 0.0)), 0.0)
    mixing = intersection[:, :, None] * decay * step[None, :, :]
    within = jnp.einsum("tsh,shp->thp", mixing, inner, precision=HIGH)
    carried = jnp.exp(cumulative)[:, :, None] * jnp.einsum(
        "tn,hpn->thp", reader, incoming, precision=HIGH
    )
    output = within + carried + skip[None, :, None] * inner
    return output.reshape(span, -1) * jax.nn.silu(gate_z)


def combine_states(earlier, later):
    state_first, decay_first = earlier
    state_second, decay_second = later
    return (decay_second[:, None, None] * state_first + state_second, decay_first * decay_second)


def feed_forward(rows, gate_w, up_w):
    gate = matmul(rows, gate_w)
    up = matmul(rows, up_w)
    activated = (jax.nn.silu(gate) * up).astype(jnp.bfloat16)
    return (gate, up, activated)


def feed_backward(rows, gate, up, activated, upstream_b, gate_w, up_w, down_w):
    down_grad = matmul(activated.T, upstream_b)
    act_grad = matmul(upstream_b, down_w.T)
    sigma = jax.nn.sigmoid(gate)
    gate_part = (act_grad * up * sigma * (1.0 + gate * (1.0 - sigma))).astype(jnp.bfloat16)
    up_part = (act_grad * gate * sigma).astype(jnp.bfloat16)
    gate_grad = matmul(rows.T, gate_part)
    up_grad = matmul(rows.T, up_part)
    back = matmul(gate_part, gate_w.T) + matmul(up_part, up_w.T)
    return (gate_grad, up_grad, down_grad, back)


def masked_scores(query_rows, key_block, row_index, row_lowest, key_first, scale):
    scores = (
        jnp.einsum("grd,pgd->grp", query_rows, key_block, preferred_element_type=jnp.float32)
        * scale
    )
    key_index = key_first + jnp.arange(key_block.shape[0], dtype=jnp.int32)
    allowed = (key_index[None, :] <= row_index[:, None]) & (
        key_index[None, :] >= row_lowest[:, None]
    )
    return (scores, allowed[None])


def online_step(carry, scores, allowed, value_block):
    maximum, weight_sum, accum = carry
    block_max = jnp.max(jnp.where(allowed, scores, NEGATIVE), axis=-1)
    new_max = jnp.maximum(maximum, block_max)
    weights = jnp.where(allowed, jnp.exp(scores - new_max[..., None]), 0.0)
    factor = jnp.exp(maximum - new_max)
    weight_sum = weight_sum * factor + jnp.sum(weights, axis=-1)
    accum = accum * factor[..., None] + jnp.einsum(
        "grp,pgd->grd",
        weights.astype(jnp.bfloat16),
        value_block,
        preferred_element_type=jnp.float32,
    )
    return (new_max, weight_sum, accum)


def keep_same(state):
    return state


def body(
    hidden_in,
    positions,
    mixer_gain,
    attention_in,
    attention_out,
    mamba_in,
    filter_taps,
    step_bias,
    decay_log,
    skip_gain,
    gated_gain,
    mamba_out,
    feed_gain,
    gate_weight,
    up_weight,
    down_weight,
    cotangent,
):
    tokens = hidden_in[0]
    token_pos = positions[0]
    upstream = cotangent[0]
    length = tokens.shape[0]
    axis_count = lax.axis_size("ctx")
    seq_total = length * axis_count
    my_index = lax.axis_index("ctx")
    first_row = my_index * length
    members = QHEADS // KVHEADS
    rows_count = members * length
    scale = 1.0 / math.sqrt(HEAD)
    (
        mixer_full,
        attend_in,
        attend_out,
        mamba_proj,
        taps_full,
        bias_full,
        rate_full,
        skip_full,
        gated_full,
        mamba_back_w,
        feed_full,
    ) = (
        lax.all_gather(mixer_gain, "fsdp", axis=0, tiled=True),
        lax.all_gather(attention_in, "fsdp", axis=0, tiled=True),
        lax.all_gather(attention_out, "fsdp", axis=0, tiled=True),
        lax.all_gather(mamba_in, "fsdp", axis=0, tiled=True),
        lax.all_gather(filter_taps, "fsdp", axis=1, tiled=True),
        lax.all_gather(step_bias, "fsdp", axis=0, tiled=True),
        lax.all_gather(decay_log, "fsdp", axis=0, tiled=True),
        lax.all_gather(skip_gain, "fsdp", axis=0, tiled=True),
        lax.all_gather(gated_gain, "fsdp", axis=0, tiled=True),
        lax.all_gather(mamba_out, "fsdp", axis=0, tiled=True),
        lax.all_gather(feed_gain, "fsdp", axis=0, tiled=True),
    )
    mixer_f = mixer_full.astype(jnp.float32)
    gated_f = gated_full.astype(jnp.float32)
    feed_f = feed_full.astype(jnp.float32)
    normed, inverse_one = rms_forward(tokens, mixer_f)
    normed_b = normed.astype(jnp.bfloat16)
    projected = matmul(normed_b, attend_in)
    cosine, sine = rotary_tables(token_pos, HEAD // 2)
    queries = rotate(projected[:, :QDIM].reshape(length, QHEADS, HEAD), cosine, sine).astype(
        jnp.bfloat16
    )
    keys = rotate(
        projected[:, QDIM : QDIM + KVDIM].reshape(length, KVHEADS, HEAD), cosine, sine
    ).astype(jnp.bfloat16)
    values = projected[:, QDIM + KVDIM :].reshape(length, KVHEADS, HEAD).astype(jnp.bfloat16)
    query_rows = group_rows(queries, KVHEADS)
    row_index = jnp.tile(first_row + jnp.arange(length, dtype=jnp.int32), members)
    row_lowest = row_index - jnp.tile(token_pos, members)
    query_last = first_row + length - 1
    lowest_any = first_row - token_pos[0]
    start_state = (
        jnp.full((KVHEADS, rows_count), NEGATIVE, jnp.float32),
        jnp.zeros((KVHEADS, rows_count), jnp.float32),
        jnp.zeros((KVHEADS, rows_count, HEAD), jnp.float32),
    )
    start = jnp.int32(0)
    key_piece = lax.all_gather(keys, "ctx", axis=0, tiled=True)
    value_piece = lax.all_gather(values, "ctx", axis=0, tiled=True)
    size = key_piece.shape[0]
    block = math.gcd(size, 512)
    needed = (start <= query_last) & (start + size - 1 >= lowest_any)

    def attend_compute(state):

        def attend_one_block(index, inner_state):
            offset = index * block
            key_block = lax.dynamic_slice_in_dim(key_piece, offset, block, 0)
            value_block = lax.dynamic_slice_in_dim(value_piece, offset, block, 0)
            scores, allowed = masked_scores(
                query_rows, key_block, row_index, row_lowest, offset, scale
            )
            return online_step(inner_state, scores, allowed, value_block)

        return lax.fori_loop(0, size // block, attend_one_block, state)

    maximum, weight_sum, accum = lax.cond(needed, attend_compute, keep_same, start_state)
    attended = (
        ungroup_rows(accum / weight_sum[..., None], length)
        .reshape(length, QDIM)
        .astype(jnp.bfloat16)
    )
    log_total = maximum + jnp.log(weight_sum)
    attend_branch = matmul(attended, attend_out)
    mixed = matmul(normed_b, mamba_proj)
    gate_z = mixed[:, :DIN]
    conv_in = mixed[:, DIN : DIN + XBC].astype(jnp.bfloat16)
    step_raw = mixed[:, DIN + XBC :]
    edge = from_behind(conv_in[length - CONV + 1 :], "ctx", 1)
    window = jnp.concatenate([edge, lax.optimization_barrier(conv_in)], axis=0).astype(jnp.float32)
    prepared, prepare_back = jax.vjp(
        mixer_inputs,
        window,
        step_raw,
        taps_full.astype(jnp.float32),
        bias_full.astype(jnp.float32),
        rate_full.astype(jnp.float32),
    )
    inner, basis, reader, step, logdecay = prepared
    (local_state, decay), states_back = jax.vjp(block_states, inner, basis, step, logdecay)
    identity = (jnp.zeros_like(local_state), jnp.ones_like(decay))
    incoming, passed_decay = prefix((local_state, decay), "ctx", combine_states, identity)
    gated, outputs_back = jax.vjp(
        block_outputs,
        inner,
        basis,
        reader,
        step,
        logdecay,
        incoming,
        gate_z,
        skip_full.astype(jnp.float32),
    )
    mamba_normed, inverse_three = rms_forward(gated, gated_f)
    mamba_normed_b = mamba_normed.astype(jnp.bfloat16)
    middle = tokens + attend_branch + matmul(mamba_normed_b, mamba_back_w)
    feed_normed, inverse_two = rms_forward(middle, feed_f)
    feed_b = feed_normed.astype(jnp.bfloat16)
    upstream_b = upstream.astype(jnp.bfloat16)
    gate_full, up_full, down_full = (
        lax.all_gather(gate_weight, "fsdp", axis=1, tiled=True),
        lax.all_gather(up_weight, "fsdp", axis=1, tiled=True),
        lax.all_gather(down_weight, "fsdp", axis=0, tiled=True),
    )
    gate, up, activated = feed_forward(feed_b, gate_full, up_full)
    feed_out = matmul(activated, down_full)
    gate_whole, up_whole, down_whole, feed_grad = feed_backward(
        feed_b, gate, up, activated, upstream_b, gate_full, up_full, down_full
    )
    gate_grad, up_grad, down_grad = (
        lax.psum_scatter(
            gate_whole.astype(jnp.bfloat16), "fsdp", scatter_dimension=1, tiled=True
        ).astype(jnp.float32),
        lax.psum_scatter(
            up_whole.astype(jnp.bfloat16), "fsdp", scatter_dimension=1, tiled=True
        ).astype(jnp.float32),
        lax.psum_scatter(
            down_whole.astype(jnp.bfloat16), "fsdp", scatter_dimension=0, tiled=True
        ).astype(jnp.float32),
    )
    output = middle + feed_out
    back_two, feed_gain_grad = rms_backward(middle, inverse_two, feed_f, feed_grad)
    middle_grad = upstream + back_two
    middle_b = middle_grad.astype(jnp.bfloat16)
    mamba_out_grad = matmul(mamba_normed_b.T, middle_b)
    normed_mamba_grad = matmul(middle_b, mamba_back_w.T)
    gated_grad, gated_gain_grad = rms_backward(gated, inverse_three, gated_f, normed_mamba_grad)
    (
        grad_inner,
        grad_basis,
        grad_reader,
        grad_step,
        grad_logdecay,
        grad_incoming,
        grad_gate_z,
        skip_grad,
    ) = outputs_back(gated_grad)
    state_grad, suffix_decay = entering((grad_incoming, decay), "ctx", combine_states, identity)
    decay_grad = jnp.sum(state_grad * incoming, axis=(1, 2))
    more_inner, more_basis, more_step, more_logdecay = states_back((state_grad, decay_grad))
    window_grad, raw_grad, taps_grad, bias_grad, rate_grad = prepare_back(
        (
            grad_inner + more_inner,
            grad_basis + more_basis,
            grad_reader,
            grad_step + more_step,
            grad_logdecay + more_logdecay,
        )
    )
    returned = from_behind(window_grad[: CONV - 1], "ctx", -1)
    conv_grad = window_grad[CONV - 1 :]
    conv_grad = jnp.concatenate(
        [conv_grad[: length - CONV + 1], conv_grad[length - CONV + 1 :] + returned], axis=0
    )
    mixed_grad = jnp.concatenate([grad_gate_z, conv_grad, raw_grad], axis=1).astype(jnp.bfloat16)
    mamba_in_grad = matmul(normed_b.T, mixed_grad)
    normed_grad = matmul(mixed_grad, mamba_proj.T)
    attend_out_grad = matmul(attended.T, middle_b)
    attended_grad = matmul(middle_b, attend_out.T).astype(jnp.bfloat16)
    grad_rows = group_rows(attended_grad.reshape(length, QHEADS, HEAD), KVHEADS)
    out_rows = group_rows(attended.reshape(length, QHEADS, HEAD), KVHEADS)
    delta = jnp.sum(grad_rows.astype(jnp.float32) * out_rows.astype(jnp.float32), axis=-1)

    def block_grads(key_block, value_block, key_first):
        scores, allowed = masked_scores(
            query_rows, key_block, row_index, row_lowest, key_first, scale
        )
        probs = jnp.where(allowed, jnp.exp(scores - log_total[..., None]), 0.0)
        value_part = jnp.einsum(
            "grp,grd->pgd",
            probs.astype(jnp.bfloat16),
            grad_rows,
            preferred_element_type=jnp.float32,
        )
        prob_grad = jnp.einsum(
            "grd,pgd->grp", grad_rows, value_block, preferred_element_type=jnp.float32
        )
        score_grad = (probs * (prob_grad - delta[..., None])).astype(jnp.bfloat16)
        query_part = (
            jnp.einsum("grp,pgd->grd", score_grad, key_block, preferred_element_type=jnp.float32)
            * scale
        )
        key_part = (
            jnp.einsum("grp,grd->pgd", score_grad, query_rows, preferred_element_type=jnp.float32)
            * scale
        )
        return (query_part, key_part, value_part)

    query_zero = jnp.zeros((KVHEADS, rows_count, HEAD), jnp.float32)
    back_state = (
        query_zero,
        jnp.zeros((seq_total, KVHEADS, HEAD), jnp.float32),
        jnp.zeros((seq_total, KVHEADS, HEAD), jnp.float32),
    )
    start = jnp.int32(0)
    back_key_piece = lax.all_gather(keys, "ctx", axis=0, tiled=True)
    back_value_piece = lax.all_gather(values, "ctx", axis=0, tiled=True)
    back_size = back_key_piece.shape[0]
    back_block = math.gcd(back_size, 512)
    needed = (start <= query_last) & (start + back_size - 1 >= lowest_any)

    def back_compute(state):

        def back_one_block(index, inner_state):
            query_acc, key_acc, value_acc = inner_state
            offset = index * back_block
            key_block = lax.dynamic_slice_in_dim(back_key_piece, offset, back_block, 0)
            value_block = lax.dynamic_slice_in_dim(back_value_piece, offset, back_block, 0)
            query_part, key_part, value_part = block_grads(key_block, value_block, offset)
            key_acc = lax.dynamic_update_slice_in_dim(
                key_acc,
                lax.dynamic_slice_in_dim(key_acc, offset, back_block, 0) + key_part,
                offset,
                0,
            )
            value_acc = lax.dynamic_update_slice_in_dim(
                value_acc,
                lax.dynamic_slice_in_dim(value_acc, offset, back_block, 0) + value_part,
                offset,
                0,
            )
            return (query_acc + query_part, key_acc, value_acc)

        return lax.fori_loop(0, back_size // back_block, back_one_block, state)

    query_grad, key_grads, value_grads = lax.cond(needed, back_compute, keep_same, back_state)
    own_keys, own_values = (
        lax.psum_scatter(
            key_grads.astype(jnp.bfloat16), "ctx", scatter_dimension=0, tiled=True
        ).astype(jnp.float32),
        lax.psum_scatter(
            value_grads.astype(jnp.bfloat16), "ctx", scatter_dimension=0, tiled=True
        ).astype(jnp.float32),
    )
    query_grad = rotate_back(ungroup_rows(query_grad, length), cosine, sine)
    own_keys = rotate_back(own_keys, cosine, sine)
    projected_grad = jnp.concatenate(
        [
            query_grad.reshape(length, QDIM),
            own_keys.reshape(length, KVDIM),
            own_values.reshape(length, KVDIM),
        ],
        axis=1,
    ).astype(jnp.bfloat16)
    attend_in_grad = matmul(normed_b.T, projected_grad)
    normed_grad = normed_grad + matmul(projected_grad, attend_in.T)
    back_one, mixer_gain_grad = rms_backward(tokens, inverse_one, mixer_f, normed_grad)
    input_grad = middle_grad + back_one
    (
        shard_mixer,
        shard_attend_in,
        shard_attend_out,
        shard_mamba_in,
        shard_taps,
        shard_bias,
        shard_rate,
        shard_skip,
        shard_gated,
        shard_mamba_out,
        shard_feed,
    ) = (
        lax.psum_scatter(
            mixer_gain_grad.astype(jnp.bfloat16), "fsdp", scatter_dimension=0, tiled=True
        ).astype(jnp.float32),
        lax.psum_scatter(
            attend_in_grad.astype(jnp.bfloat16), "fsdp", scatter_dimension=0, tiled=True
        ).astype(jnp.float32),
        lax.psum_scatter(
            attend_out_grad.astype(jnp.bfloat16), "fsdp", scatter_dimension=0, tiled=True
        ).astype(jnp.float32),
        lax.psum_scatter(
            mamba_in_grad.astype(jnp.bfloat16), "fsdp", scatter_dimension=0, tiled=True
        ).astype(jnp.float32),
        lax.psum_scatter(
            taps_grad.astype(jnp.bfloat16), "fsdp", scatter_dimension=1, tiled=True
        ).astype(jnp.float32),
        lax.psum_scatter(
            bias_grad.astype(jnp.bfloat16), "fsdp", scatter_dimension=0, tiled=True
        ).astype(jnp.float32),
        lax.psum_scatter(
            rate_grad.astype(jnp.bfloat16), "fsdp", scatter_dimension=0, tiled=True
        ).astype(jnp.float32),
        lax.psum_scatter(
            skip_grad.astype(jnp.bfloat16), "fsdp", scatter_dimension=0, tiled=True
        ).astype(jnp.float32),
        lax.psum_scatter(
            gated_gain_grad.astype(jnp.bfloat16), "fsdp", scatter_dimension=0, tiled=True
        ).astype(jnp.float32),
        lax.psum_scatter(
            mamba_out_grad.astype(jnp.bfloat16), "fsdp", scatter_dimension=0, tiled=True
        ).astype(jnp.float32),
        lax.psum_scatter(
            feed_gain_grad.astype(jnp.bfloat16), "fsdp", scatter_dimension=0, tiled=True
        ).astype(jnp.float32),
    )
    (
        total_mixer,
        total_attend_in,
        total_attend_out,
        total_mamba_in,
        total_taps,
        total_bias,
        total_rate,
        total_skip,
        total_gated,
        total_mamba_out,
        total_feed,
        total_gate,
        total_up,
        total_down,
    ) = (
        lax.psum(shard_mixer.astype(jnp.bfloat16), "ctx").astype(jnp.float32),
        lax.psum(shard_attend_in.astype(jnp.bfloat16), "ctx").astype(jnp.float32),
        lax.psum(shard_attend_out.astype(jnp.bfloat16), "ctx").astype(jnp.float32),
        lax.psum(shard_mamba_in.astype(jnp.bfloat16), "ctx").astype(jnp.float32),
        lax.psum(shard_taps.astype(jnp.bfloat16), "ctx").astype(jnp.float32),
        lax.psum(shard_bias.astype(jnp.bfloat16), "ctx").astype(jnp.float32),
        lax.psum(shard_rate.astype(jnp.bfloat16), "ctx").astype(jnp.float32),
        lax.psum(shard_skip.astype(jnp.bfloat16), "ctx").astype(jnp.float32),
        lax.psum(shard_gated.astype(jnp.bfloat16), "ctx").astype(jnp.float32),
        lax.psum(shard_mamba_out.astype(jnp.bfloat16), "ctx").astype(jnp.float32),
        lax.psum(shard_feed.astype(jnp.bfloat16), "ctx").astype(jnp.float32),
        lax.psum(gate_grad.astype(jnp.bfloat16), "ctx").astype(jnp.float32),
        lax.psum(up_grad.astype(jnp.bfloat16), "ctx").astype(jnp.float32),
        lax.psum(down_grad.astype(jnp.bfloat16), "ctx").astype(jnp.float32),
    )
    return (
        output[None],
        input_grad[None],
        total_mixer,
        total_attend_in,
        total_attend_out,
        total_mamba_in,
        total_taps,
        total_bias,
        total_rate,
        total_skip,
        total_gated,
        total_mamba_out,
        total_feed,
        total_gate,
        total_up,
        total_down,
    )


def solution(mesh):
    return jax.shard_map(
        body,
        mesh=mesh,
        in_specs=(
            P("fsdp", "ctx", None),
            P("fsdp", "ctx"),
            P("fsdp"),
            P("fsdp", None),
            P("fsdp", None),
            P("fsdp", None),
            P(None, "fsdp"),
            P("fsdp"),
            P("fsdp"),
            P("fsdp"),
            P("fsdp"),
            P("fsdp", None),
            P("fsdp"),
            P(None, "fsdp"),
            P(None, "fsdp"),
            P("fsdp", None),
            P("fsdp", "ctx", None),
        ),
        out_specs=(
            P("fsdp", "ctx", None),
            P("fsdp", "ctx", None),
            P("fsdp"),
            P("fsdp", None),
            P("fsdp", None),
            P("fsdp", None),
            P(None, "fsdp"),
            P("fsdp"),
            P("fsdp"),
            P("fsdp"),
            P("fsdp"),
            P("fsdp", None),
            P("fsdp"),
            P(None, "fsdp"),
            P(None, "fsdp"),
            P("fsdp", None),
        ),
        check_vma=False,
    )
```

profile of v0, /device:TPU:0, one launch (start us, length us, event | category | flops | bytes accessed | tf_op | source)
XLA Modules:
  0.0 1146.5 jit_solution(10691900784060148970)
XLA Ops:
  12.6 8.4 all-reduce.25
  21.8 5.2 all-gather.2
  27.0 5.4 all-gather.3
  32.8 30.1 %all-gather.21.cloned.1.call-done = bf16[1024,3352]{0,1:T(8,128)(2,1)} async-done(((bf16[256,3352]{0,1:T(8,128)(2,1)}), bf16[1024,3352]{0,1:T(8,128)(2,1)}) %all-gather.21.cloned.1.call-update) | async-done | bytes 6864912 | tf_op jit(solution)/shard_map/all_gather | solution.py:287
  63.0 5.0 fusion.165
  71.0 3.4 collective-permute-start
  84.4 3.2 fusion.94
  92.2 5.2 all-gather.5
  98.1 5.1 all-gather.6
  111.1 36.7 %all_gather.70 = bf16[2048,2,64]{0,2,1:T(8,128)(2,1)} all-gather(bf16[256,2,64]{0,2,1:T(8,128)(2,1)S(1)} %pad_maximum_fusion.7), channel_id=1, replica_groups=mesh['ctx'=8,'fsdp'=4] {'ctx'}, dimensions={0}, use_global_device_ids=true | all-gather | bytes 589824 | tf_op jit(solution)/shard_map/all_gather | solution.py:321
  148.8 34.0 %all_gather.71 = bf16[2048,2,64]{0,2,1:T(8,128)(2,1)} all-gather(bf16[256,2,64]{0,2,1:T(8,128)(2,1)S(1)} %bitcast.405), channel_id=1, replica_groups=mesh['ctx'=8,'fsdp'=4] {'ctx'}, dimensions={0}, use_global_device_ids=true | all-gather | bytes 589824 | tf_op jit(solution)/shard_map/all_gather | solution.py:322
  182.8 54.2 %conditional.2 = (f32[2,1024]{1,0:T(2,128)}, f32[2,1024]{1,0:T(2,128)}, f32[2,1024,64]{1,2,0:T(8,128)}, f32[2,1024]{1,0:T(2,128)S(1)}) conditional(s32[]{:T(128)} %convert_element_type.298, () %tuple.92, (s32[4,256]{1,0:T(4,128)S(1)}, s32[1024]{0:T(1024)S(1)}, bf16[2048,2,64]{0,2,1:T(8,128)(2,1)}, bf16[2,1024,64]{1,2,0:T(8,128)(2,1)S(1)}, ...), branch_computations={%region_1.0_spmd, %region_2.7_spmd} | conditional | flops 281946624 | bytes 33198444 | solution.py:340
  183.0 53.3 %while.62 = (s32[]{:T(128)}, f32[2,1024]{1,0:T(2,128)}, f32[2,1024]{1,0:T(2,128)}, f32[2,1024,64]{1,2,0:T(8,128)}, s32[4,256]{1,0:T(4,128)S(1)}, /*index=5*/s32[...) while((s32[]{:T(128)}, f32[2,1024]{1,0:T(2,128)}, ...), condition=%wide.region_6.6_spmd.clone, body=%wide.region_3.5_spmd.clone.sunk | while | flops 281946624 | bytes 33181916 | solution.py:338
  183.5 4.0 fusion.273
  187.5 3.3 fusion.275
  195.4 4.0 fusion.273
  200.1 3.3 fusion.275
  209.0 4.0 fusion.273
  213.6 4.0 fusion.275
  223.2 4.0 fusion.273
  227.9 3.4 fusion.275
  239.2 18.7 %all-gather.4 = bf16[8,1,24]{2,1,0:T(2,128)(2,1)S(1)} all-gather(bf16[1,1,24]{2,1,0:T(2,128)(2,1)S(1)} %get-tuple-element.919), channel_id=1, replica_groups=mesh['ctx'=8,'fsdp'=4] {'ctx'}, dimensions={0}, use_global_device_ids=true | all-gather | bytes 432 | tf_op jit(solution)/shard_map/all_gather | solution.py:36
  260.4 9.8 while.65
  272.7 8.7 fusion.78
  287.9 3.9 fusion.154
  295.1 4.9 fusion.172
  300.1 4.8 fusion.173
  304.9 7.8 all-gather.29.cloned.1.call-done
  312.7 7.0 multiply_convert_fusion
  327.5 62.3 %conditional.3 = (f32[2,1024,64]{1,2,0:T(8,128)}, f32[2048,2,64]{0,2,1:T(8,128)}, f32[2048,2,64]{0,2,1:T(8,128)}) conditional(s32[]{:T(128)} %convert_element_type.298, () %tuple.96, (f32[2,1024]{1,0:T(2,128)}, f32[2,1024]{1,0:T(2,128)}, bf16[2,4,256,64]{2,3,1,0:T(8,128)(2,1)S(1)}, f32[2,4,256,64]{2,3,1,0:T(8,128)S(1)}, ...), branch_computations={%region_29.30_spmd, %region_30.34_spmd} | conditional | flops 684130816 | bytes 52261512 | solution.py:509
  334.3 55.2 %while.63 = (s32[]{:T(128)}, f32[2,1024,64]{1,2,0:T(8,128)}, f32[2048,2,64]{0,2,1:T(8,128)}, f32[2048,2,64]{0,2,1:T(8,128)}, s32[4,256]{1,0:T(4,128)S(1)}, /*ind...) while((s32[]{:T(128)}, f32[2,1024,64]{1,2,0:T(8,128)}, ...), condition=%wide.region_33.33_spmd.clone, body=%wide.region_32.32_spmd.clone.sunk | while | flops 683737600 | bytes 47198660 | solution.py:507
  343.9 4.1 fusion.269
  357.7 4.1 fusion.269
  371.6 4.1 fusion.269
  385.4 4.1 fusion.269
  394.4 3.9 multiply_reduce_fusion.5
  398.4 4.9 multiply_reduce_fusion.6
  406.3 3.6 fusion.97
  414.2 41.3 %reduce-scatter.13.cloned.1.call-done = bf16[256,2,64]{0,2,1:T(8,128)(2,1)} async-done(((bf16[2048,2,64]{0,2,1:T(8,128)(2,1)}), bf16[256,2,64]{0,2,1:T(8,128)(2,1)}) %reduce-scatter.13.cloned.1.call-update) | async-done | bytes 65552 | tf_op jit(solution)/shard_map/reduce_scatter | solution.py:511
  457.8 63.2 %reduce-scatter.15.cloned.1.call-done = bf16[256,2,64]{0,2,1:T(8,128)(2,1)} async-done(((bf16[2048,2,64]{0,2,1:T(8,128)(2,1)}), bf16[256,2,64]{0,2,1:T(8,128)(2,1)}) %reduce-scatter.15.cloned.1.call-update) | async-done | bytes 65552 | tf_op jit(solution)/shard_map/reduce_scatter | solution.py:514
  528.0 3.3 convolution_convert_fusion.4
  532.6 3.3 convolution_convert_fusion.3
  536.2 5.0 fusion.167
  541.3 11.2 fusion.58
  559.1 4.0 fusion.103
  565.1 17.7 %all-gather.33.cloned.1.call-done = bf16[192,64,128]{2,1,0:T(8,128)(2,1)} async-done(((bf16[24,64,128]{2,1,0:T(8,128)(2,1)}), bf16[192,64,128]{2,1,0:T(8,128)(2,1)}) %all-gather.33.cloned.1.call-update) | async-done | bytes 3145744 | tf_op jit(solution)/shard_map/all_gather | solution.py:61
  582.9 13.7 %while.64 = (s32[]{:T(128)}, f32[24,64,128]{2,1,0:T(8,128)S(1)}, s32[]{:T(128)}, bf16[8,24]{1,0:T(8,128)(2,1)}, bf16[8,24,64,128]{3,2,1,0:T(8,128)(2,1)}, /*index=5*/s32[]{:T(128)}, s32[]{:T(128)}, s32[]{:T(128)}, s32[]{:T(128)}) while((s32[]{:T(128)}, f32[24,64,128]{2,1,0:T(8,128)S(1)}, s32[]{:T(128)}, bf16[8,24]{1,0:T(8,128)(2,1)}, ...), condition=%wide.region_17.18_spmd, body=%wide.region_16.17_spmd.sunk | while | flops 589854 | bytes 1966467 | solution.py:78
  596.7 3.1 multiply_reduce_fusion.8
  599.8 6.9 fusion.77
  609.8 3.5 fusion.100
  614.8 3.6 multiply_reduce_fusion.4
  629.5 3.3 pad_add_fusion
  636.0 4.9 convolution_convert_fusion
  642.8 37.2 %reduce-scatter.23.cloned.1.call-done = bf16[384,1024]{1,0:T(8,128)(2,1)} async-done(((bf16[1536,1024]{1,0:T(8,128)(2,1)}), bf16[384,1024]{1,0:T(8,128)(2,1)}) %reduce-scatter.23.cloned.1.call-update) | async-done | bytes 786448 | tf_op jit(solution)/shard_map/reduce_scatter | solution.py:572
  680.1 46.8 %reduce-scatter.25.cloned.1.call-done = bf16[1024,512]{1,0:T(8,128)(2,1)} async-done(((bf16[1024,2048]{1,0:T(8,128)(2,1)}), bf16[1024,512]{1,0:T(8,128)(2,1)}) %reduce-scatter.25.cloned.1.call-update) | async-done | bytes 1048592 | tf_op jit(solution)/shard_map/reduce_scatter | solution.py:394
  726.9 46.8 %reduce-scatter.27.cloned.1.call-done = bf16[1024,512]{1,0:T(8,128)(2,1)} async-done(((bf16[1024,2048]{1,0:T(8,128)(2,1)}), bf16[1024,512]{1,0:T(8,128)(2,1)}) %reduce-scatter.27.cloned.1.call-update) | async-done | bytes 1048592 | tf_op jit(solution)/shard_map/reduce_scatter | solution.py:397
  773.7 47.0 %reduce-scatter.29.cloned.1.call-done = bf16[512,1024]{1,0:T(8,128)(2,1)} async-done(((bf16[2048,1024]{1,0:T(8,128)(2,1)}), bf16[512,1024]{1,0:T(8,128)(2,1)}) %reduce-scatter.29.cloned.1.call-update) | async-done | bytes 1048592 | tf_op jit(solution)/shard_map/reduce_scatter | solution.py:400
  820.7 64.0 %reduce-scatter.21.cloned.1.call-done = bf16[256,3352]{0,1:T(8,128)(2,1)} async-done(((bf16[1024,3352]{0,1:T(8,128)(2,1)}), bf16[256,3352]{0,1:T(8,128)(2,1)}) %reduce-scatter.21.cloned.1.call-update) | async-done | bytes 1716240 | tf_op jit(solution)/shard_map/reduce_scatter | solution.py:554
  887.1 4.5 fusion.93
  893.5 6.4 fusion.115
  899.9 6.0 all-reduce.24
  910.2 22.4 %all-reduce.22 = (bf16[256]{0:T(256)(128)(2,1)S(1)}, bf16[4,448]{1,0:T(4,128)(2,1)S(1)}, bf16[6]{0:T(256)(128)(2,1)S(1)}, bf16[6]{0:T(256)(128)(2,1)S(1)}, bf16[...) all-reduce(bf16[256]{0:T(256)(128)(2,1)S(1)} %dynamic-slice.4, ...), channel_id=1, replica_groups=mesh['ctx'=8,'fsdp'=4] {'ctx'}, use_global_device_ids=true, to_apply=%region_39.40 | all-reduce | flops 2706 | bytes 10824 | tf_op jit(solution)/shard_map/psum | solution.py:595
  936.4 191.3 %all-reduce.28.cloned.1.call-done = (bf16[256,768]{1,0:T(8,128)(2,1)}, bf16[128,1024]{1,0:T(8,128)(2,1)}, bf16[256,3352]{0,1:T(8,128)(2,1)}, bf16[384,1024]{1,0:...) async-done(((bf16[256,768]{1,0:T(8,128)(2,1)}, bf16[128,1024]{1,0:T(8,128)(2,1)}, bf16[256,3352]{0,1:T(8,128)(2,1)}, ...) | async-done | bytes 6303760 | tf_op jit(solution)/shard_map/psum | solution.py:596
  1127.7 3.6 convert_element_type.337
  (638 shorter events, 218.1 us)
Async XLA Ops:
  7.2 13.9 %copy-start.17 = (f32[1,256,1024]{2,1,0:T(8,128)S(1)}, f32[1,256,1024]{2,1,0:T(8,128)}, u32[]{:S(2)}) copy-start(f32[1,256,1024]{2,1,0:T(8,128)} %param.29) | copy-start | bytes 3145732
  7.2 14.6 %copy-start.129 = (bf16[256]{0:T(256)(128)(2,1)S(1)}, bf16[256]{0:T(256)(128)(2,1)}, u32[]{:S(2)}) copy-start(bf16[256]{0:T(256)(128)(2,1)} %param.31) | copy-start | bytes 1540
  7.2 19.8 %copy-start.119 = (bf16[4,448]{1,0:T(4,128)(2,1)S(1)}, bf16[4,448]{1,0:T(4,128)(2,1)}, u32[]{:S(2)}) copy-start(bf16[4,448]{1,0:T(4,128)(2,1)} %param.35) | copy-start | bytes 10756
  7.2 55.8 %all-gather.21.cloned.1.call-start = ((), (), s32[]{:S(2)}) async-start(), calls=%async_computation.12 | async-start | bytes 8581120 | tf_op jit(solution)/shard_map/all_gather | solution.py:287
  7.9 96.1 %all-gather.17.cloned.1.call-start = ((), (), s32[]{:S(2)}) async-start(), calls=%async_computation.10 | async-start | bytes 1966080 | tf_op jit(solution)/shard_map/all_gather | solution.py:285
  12.6 247.8 %all-gather.31.cloned.1.call-start = ((), (), s32[]{:S(2)}) async-start(), calls=%async_computation.26 | async-start | bytes 3538944 | tf_op jit(solution)/shard_map/all_gather | solution.py:36
  21.0 47.0 %copy-start.131 = (bf16[24]{0:T(256)(128)(2,1)}, bf16[24]{0:T(256)(128)(2,1)S(1)}, u32[]{:S(2)}) copy-start(bf16[24]{0:T(256)(128)(2,1)S(1)} %get-tuple-element.878) | copy-start | bytes 148
  21.0 47.1 %copy-start.122 = (f32[24]{0:T(128)}, f32[24]{0:T(128)S(1)}, u32[]{:S(2)}) copy-start(f32[24]{0:T(128)S(1)} %convert_exponential_fusion) | copy-start | bytes 292
  21.0 47.0 %copy-start.124 = (f32[24]{0:T(128)}, f32[24]{0:T(128)S(1)}, u32[]{:S(2)}) copy-start(f32[24]{0:T(128)S(1)} %convert_element_type.309) | copy-start | bytes 292
  21.8 46.2 %copy-start.109 = (f32[256]{0:T(256)}, f32[256]{0:T(256)S(1)}, u32[]{:S(2)}) copy-start(f32[256]{0:T(256)S(1)} %get-tuple-element.923) | copy-start | bytes 3076
  27.0 41.0 %copy-start.93 = (f32[4,1,256]{2,1,0:T(1,128)}, f32[4,1,256]{2,1,0:T(1,128)S(1)}, u32[]{:S(2)}) copy-start(f32[4,1,256]{2,1,0:T(1,128)S(1)} %convert_element_type.363) | copy-start | bytes 12292
  32.6 44.9 %copy-start.80 = (f32[1792]{0:T(1024)}, f32[1792]{0:T(1024)S(1)}, u32[]{:S(2)}) copy-start(f32[1792]{0:T(1024)S(1)} %get-tuple-element.791) | copy-start | bytes 21508
  32.6 44.9 %copy-start.82 = (f32[1792]{0:T(1024)}, f32[1792]{0:T(1024)S(1)}, u32[]{:S(2)}) copy-start(f32[1792]{0:T(1024)S(1)} %get-tuple-element.792) | copy-start | bytes 21508
  32.6 44.9 %copy-start.84 = (f32[1792]{0:T(1024)}, f32[1792]{0:T(1024)S(1)}, u32[]{:S(2)}) copy-start(f32[1792]{0:T(1024)S(1)} %get-tuple-element.793) | copy-start | bytes 21508
  32.6 44.9 %copy-start.86 = (f32[1792]{0:T(1024)}, f32[1792]{0:T(1024)S(1)}, u32[]{:S(2)}) copy-start(f32[1792]{0:T(1024)S(1)} %get-tuple-element.794) | copy-start | bytes 21508
  32.8 35.2 %copy-start.27 = (bf16[256,1024]{1,0:T(8,128)(2,1)}, bf16[256,1024]{1,0:T(8,128)(2,1)S(1)}, u32[]{:S(2)}) copy-start(bf16[256,1024]{1,0:T(8,128)(2,1)S(1)} %fusion.108) | copy-start | bytes 1572868
  69.9 169.3 %copy-start.41 = (f32[256,24]{1,0:T(8,128)}, f32[256,24]{1,0:T(8,128)S(1)}, u32[]{:S(2)}) copy-start(f32[256,24]{1,0:T(8,128)S(1)} %get-tuple-element.894) | copy-start | bytes 73732
  71.0 5.2 collective-permute-start
  76.1 8.3 copy-start.72
  84.4 188.2 %copy-start.12 = (f32[256,1536]{0,1:T(8,128)}, f32[256,1536]{0,1:T(8,128)S(1)}, u32[]{:S(2)}) copy-start(f32[256,1536]{0,1:T(8,128)S(1)} %copy.281) | copy-start | bytes 4718596
  87.7 200.2 %all-gather.23.cloned.1.call-start = ((), (), s32[]{:S(2)}) async-start(), calls=%async_computation.13 | async-start | bytes 3932160 | tf_op jit(solution)/shard_map/all_gather | solution.py:293
  88.3 9.9 copy-start.130
  88.3 15.8 %copy-start.28 = (bf16[256,1024]{1,0:T(8,128)(2,1)S(1)}, bf16[256,1024]{1,0:T(8,128)(2,1)}, u32[]{:S(2)}) copy-start(bf16[256,1024]{1,0:T(8,128)(2,1)} %copy-done.27) | copy-start | bytes 1572868
  88.3 203.5 %all-gather.19.cloned.1.call-start = ((), (), s32[]{:S(2)}) async-start(), calls=%async_computation.11 | async-start | bytes 1310720 | tf_op jit(solution)/shard_map/all_gather | solution.py:286
  88.9 206.3 %all-gather.25.cloned.1.call-start = ((), (), s32[]{:S(2)}) async-start(), calls=%async_computation.14 | async-start | bytes 5242880 | tf_op jit(solution)/shard_map/all_gather | solution.py:384
  89.4 210.6 %all-gather.27.cloned.1.call-start = ((), (), s32[]{:S(2)}) async-start(), calls=%async_computation.15 | async-start | bytes 5242880 | tf_op jit(solution)/shard_map/all_gather | solution.py:385
  90.2 222.5 %all-gather.29.cloned.1.call-start = ((), (), s32[]{:S(2)}) async-start(), calls=%async_computation.16 | async-start | bytes 5242880 | tf_op jit(solution)/shard_map/all_gather | solution.py:386
  90.9 364.6 %reduce-scatter.13.cloned.1.call-start = ((), (), s32[]{:S(2)}) async-start(), calls=%async_computation.17 | async-start | bytes 589824 | tf_op jit(solution)/shard_map/reduce_scatter | solution.py:511
  92.2 180.4 %copy-start.133 = (f32[24]{0:T(128)}, f32[24]{0:T(128)S(1)}, u32[]{:S(2)}) copy-start(f32[24]{0:T(128)S(1)} %convert_element_type.313) | copy-start | bytes 292
  104.0 7.1 copy-start.56
  104.0 7.1 copy-start.57
  213.6 5.4 copy-start.3
  237.0 23.4 %copy-start.99 = (f32[2,1024]{1,0:T(2,128)}, f32[2,1024]{1,0:T(2,128)S(1)}, u32[]{:S(2)}) copy-start(f32[2,1024]{1,0:T(2,128)S(1)} %get-tuple-element.615) | copy-start | bytes 24580
  238.3 22.1 %copy-start.47 = (bf16[2,4,256,64]{2,1,3,0:T(4,128)(2,1)}, bf16[2,4,256,64]{2,1,3,0:T(4,128)(2,1)S(1)}, u32[]{:S(2)}) copy-start(bf16[2,4,256,64]{2,1,3,0:T(4,128)(2,1)S(1)} %convert_element_type.304) | copy-start | bytes 786436
  239.2 33.4 %copy-start.102 = (f32[256,24]{0,1:T(8,128)}, f32[256,24]{0,1:T(8,128)S(1)}, u32[]{:S(2)}) copy-start(f32[256,24]{0,1:T(8,128)S(1)} %copy.285) | copy-start | bytes 73732
  239.2 33.4 %copy-start.105 = (f32[256,24]{0,1:T(8,128)}, f32[256,24]{0,1:T(8,128)S(1)}, u32[]{:S(2)}) copy-start(f32[256,24]{0,1:T(8,128)S(1)} %copy.287) | copy-start | bytes 73732
  258.9 13.7 %copy-start.74 = (f32[256,24]{0,1:T(8,128)}, f32[256,24]{0,1:T(8,128)S(1)}, u32[]{:S(2)}) copy-start(f32[256,24]{0,1:T(8,128)S(1)} %copy.288) | copy-start | bytes 73732
  260.3 12.3 %copy-start.67 = (f32[256,256]{1,0:T(8,128)}, f32[256,256]{1,0:T(8,128)S(1)}, u32[]{:S(2)}) copy-start(f32[256,256]{1,0:T(8,128)S(1)} %fusion.139) | copy-start | bytes 786436
  270.2 11.3 copy-start.126
  272.7 8.8 copy-start.33
  294.3 30.4 %copy-start.19 = (f32[256,1024]{1,0:T(8,128)}, f32[256,1024]{1,0:T(8,128)S(1)}, u32[]{:S(2)}) copy-start(f32[256,1024]{1,0:T(8,128)S(1)} %get-tuple-element.933) | copy-start | bytes 3145732
  294.9 5.1 copy-start.91
  312.7 7.0 copy-start.128
  392.2 128.8 %reduce-scatter.15.cloned.1.call-start = ((), (), s32[]{:S(2)}) async-start(), calls=%async_computation.18 | async-start | bytes 589824 | tf_op jit(solution)/shard_map/reduce_scatter | solution.py:514
  394.3 188.4 %all-gather.33.cloned.1.call-start = ((), (), s32[]{:S(2)}) async-start(), calls=%async_computation.27 | async-start | bytes 3538944 | tf_op jit(solution)/shard_map/all_gather | solution.py:61
  409.9 232.9 %reduce-scatter.19.cloned.1.call-start = ((), (), s32[]{:S(2)}) async-start(), calls=%async_computation.20 | async-start | bytes 1310720 | tf_op jit(solution)/shard_map/reduce_scatter | solution.py:551
  411.4 109.5 %copy-start.29 = (bf16[256,1024]{1,0:T(8,128)(2,1)S(1)}, bf16[256,1024]{1,0:T(8,128)(2,1)}, u32[]{:S(2)}) copy-start(bf16[256,1024]{1,0:T(8,128)(2,1)} %copy-done.27) | copy-start | bytes 1572868
  411.4 231.4 %reduce-scatter.17.cloned.1.call-start = ((), (), s32[]{:S(2)}) async-start(), calls=%async_computation.19 | async-start | bytes 1966080 | tf_op jit(solution)/shard_map/reduce_scatter | solution.py:548
  523.8 156.3 %reduce-scatter.23.cloned.1.call-start = ((), (), s32[]{:S(2)}) async-start(), calls=%async_computation.22 | async-start | bytes 3932160 | tf_op jit(solution)/shard_map/reduce_scatter | solution.py:572
  526.7 200.3 %reduce-scatter.25.cloned.1.call-start = ((), (), s32[]{:S(2)}) async-start(), calls=%async_computation.23 | async-start | bytes 5242880 | tf_op jit(solution)/shard_map/reduce_scatter | solution.py:394
  531.4 242.4 %reduce-scatter.27.cloned.1.call-start = ((), (), s32[]{:S(2)}) async-start(), calls=%async_computation.24 | async-start | bytes 5242880 | tf_op jit(solution)/shard_map/reduce_scatter | solution.py:397
  536.0 284.8 %reduce-scatter.29.cloned.1.call-start = ((), (), s32[]{:S(2)}) async-start(), calls=%async_computation.25 | async-start | bytes 5242880 | tf_op jit(solution)/shard_map/reduce_scatter | solution.py:400
  536.2 5.1 copy-start.13
  536.2 5.1 copy-start.68
  552.5 6.6 copy-start.76
  552.5 332.2 %reduce-scatter.21.cloned.1.call-start = ((), (), s32[]{:S(2)}) async-start(), calls=%async_computation.21 | async-start | bytes 8581120 | tf_op jit(solution)/shard_map/reduce_scatter | solution.py:554
  557.7 25.1 %copy-start.77 = (f32[24,2,128]{2,0,1:T(8,128)}, f32[24,2,128]{2,0,1:T(8,128)S(1)}, u32[]{:S(2)}) copy-start(f32[24,2,128]{2,0,1:T(8,128)S(1)} %reduce-window.24) | copy-start | bytes 73732
  621.5 12.9 %collective-permute-start.1 = (f32[3,1792]{1,0:T(4,128)}, f32[3,1792]{1,0:T(4,128)}, u32[]{:S(2)}, u32[]{:S(2)}) collective-permute-start(f32[3,1792]{1,0:T(4,128)} %pad_add_fusion.2), channel_id=1, source_target_pairs={{4,0},{8,4},{12,8},{16,12},{20,16},{24,20},{28,24},{5,1},{9,5},{13... | collective-permute-start | bytes 64520 | tf_op jit(solution)/shard_map/ppermute | solution.py:30
  640.9 268.2 %reduce-scatter.31.cloned.1.call-start = ((), (), s32[]{:S(2)}) async-start(), calls=%async_computation.28 | async-start | bytes 573440
  642.7 485.0 %all-reduce.28.cloned.1.call-start = ((), (), s32[]{:S(2)}) async-start(), calls=%async_computation.29 | async-start | bytes 12607488 | tf_op jit(solution)/shard_map/psum | solution.py:596
  893.5 6.4 copy-start.108
  893.5 6.4 copy-start.114
  893.5 12.9 %copy-start.37 = (f32[256,1024]{1,0:T(8,128)S(1)}, f32[256,1024]{1,0:T(8,128)}, u32[]{:S(2)}) copy-start(f32[256,1024]{1,0:T(8,128)} %get-tuple-element.890) | copy-start | bytes 3145732
  893.5 12.9 %copy-start.117 = (f32[256]{0:T(256)S(1)}, f32[256]{0:T(256)}, u32[]{:S(2)}) copy-start(f32[256]{0:T(256)} %get-tuple-element.922) | copy-start | bytes 3076
  (121 other events, 339.3 us)
Sparse Core Ops, SparseCore 0:
  9.6 53.3 all-gather.20
  64.5 19.6 all-gather.16
  87.8 70.0 all-gather.30
  159.3 27.2 all-gather.22
  188.0 16.6 all-gather.18
  206.1 34.4 all-gather.24
  242.2 34.4 all-gather.26
  278.2 34.4 all-gather.28
  392.3 63.1 reduce-scatter.12
  458.7 62.1 reduce-scatter.14
  523.7 59.0 all-gather.32
  585.2 23.4 reduce-scatter.18
  611.2 27.9 reduce-scatter.16
  642.2 37.8 reduce-scatter.22
  682.5 44.4 reduce-scatter.24
  729.3 44.3 reduce-scatter.26
  776.1 44.5 reduce-scatter.28
  823.1 61.5 reduce-scatter.20
  887.8 21.3 reduce-scatter.30
  914.5 213.2 all-reduce.27
where the time goes:
time: 1160 us; the launch traced here: 1150 us
  waiting for transfers between devices  598 us (52%)
  matrix products  205 us (18%)
  blocking collectives  147 us (13%)
  other arithmetic  116 us (10%)
  local copies, waits for them, and re-layouts  53.3 us (5%)
  between operations  19.9 us (2%)
    psum x1, waiting for transfers between devices, body(): lax.psum(shard_attend_in.astype(jnp.bfloat16), 'ctx').astype(jnp.float32)  191 us
    dot_general x21, matrix products, matmul(): return jnp.dot(left, right, preferred_element_type=jnp.float32)  73.1 us
    reduce_scatter x1, waiting for transfers between devices, body(): lax.psum_scatter(mamba_in_grad.astype(jnp.bfloat16), 'fsdp', scatter_dime...  64 us
    reduce_scatter x1, waiting for transfers between devices, body(): lax.psum_scatter(value_grads.astype(jnp.bfloat16), 'ctx', scatter_dimensi...  63.2 us
    reduce_scatter x1, waiting for transfers between devices, body(): lax.psum_scatter(down_whole.astype(jnp.bfloat16), 'fsdp', scatter_dimensi...  47 us
    reduce_scatter x1, waiting for transfers between devices, body(): lax.psum_scatter(gate_whole.astype(jnp.bfloat16), 'fsdp', scatter_dimensi...  46.8 us
    reduce_scatter x1, waiting for transfers between devices, body(): lax.psum_scatter(up_whole.astype(jnp.bfloat16), 'fsdp', scatter_dimension...  46.8 us
    reduce_scatter x1, waiting for transfers between devices, body(): lax.psum_scatter(key_grads.astype(jnp.bfloat16), 'ctx', scatter_dimension...  41.3 us
  transfers between devices with their start and end apart: 22, of which 12 were waited for; matrix products, arithmetic and copies ran while one was open for 24% of the time, Pallas kernels for 0%

commit v1 on v0

v1 whole, which is shorter than its diff:
```python
import functools
import math

import jax
import jax.numpy as jnp
from jax import lax
from jax.experimental import pallas as pl
from jax.experimental.pallas import tpu as pltpu
from jax.sharding import PartitionSpec as P

QHEADS = 8
KVHEADS = 2
HEAD = 64
MHEADS = 24
MHEAD = 64
STATE = 128
CONV = 4
DIN = 1536
XBC = 1792
QDIM = 512
KVDIM = 128


EPS = 1e-05
NEGATIVE = -1e30
ROPE_BASE = 10000.0
HIGH = lax.Precision.HIGHEST


BF = jnp.bfloat16
F32 = jnp.float32


def shift(value, axis, steps):
    count = lax.axis_size(axis)
    first, last = (max(0, -steps), min(count, count - steps))
    return lax.ppermute(value, axis, [(source, source + steps) for source in range(first, last)])


def swap(value, axis, bit):
    count = lax.axis_size(axis)
    return lax.ppermute(value, axis, [(source, source ^ bit) for source in range(count)])


def xor_gather(block, axis):
    held = {0: block}
    bit = lax.axis_size(axis) // 2
    while bit >= 1:
        held.update({d | bit: swap(part, axis, bit) for d, part in sorted(held.items())})
        bit //= 2
    return [held[d] for d in range(len(held))]


def xor_scatter(blocks, axis):
    held = dict(enumerate(blocks))
    bit = 1
    while bit < len(blocks):
        got = {d ^ bit: swap(held[d].astype(BF), axis, bit) for d in held if d & bit}
        held = {d: held[d].astype(F32) + got[d].astype(F32) for d in held if not d & bit}
        bit *= 2
    return held[0]


def ordered(blocks, axis):
    mine = lax.axis_index(axis)
    stack = jnp.stack(blocks)
    return [lax.dynamic_index_in_dim(stack, mine ^ j, 0, False) for j in range(len(blocks))]


def column_blocks(array, axis):
    count, mine = (lax.axis_size(axis), lax.axis_index(axis))
    width = array.shape[1] // count
    return [
        lax.dynamic_slice_in_dim(array, (mine ^ d) * width, width, 1) for d in range(count)
    ]


def carried(state, decay, axis, direction):
    count = lax.axis_size(axis)
    own_state, own_decay = (state, decay)
    out_state, out_decay = (jnp.zeros_like(state), jnp.ones_like(decay))
    step = 1
    while step < count:
        got_state = shift(own_state.astype(BF), axis, direction * step).astype(F32)
        got_decay = shift(own_decay, axis, direction * step)
        out_state = out_decay[:, None, None] * got_state + out_state
        out_decay = out_decay * got_decay
        own_state = own_decay[:, None, None] * got_state + own_state
        own_decay = own_decay * got_decay
        step *= 2
    return out_state


def matmul(left, right):
    return jnp.dot(left, right, preferred_element_type=jnp.float32)


def rms_forward(values, gain):
    inverse = lax.rsqrt(jnp.mean(values * values, axis=-1, keepdims=True) + EPS)
    return (values * inverse * gain, inverse)


def rms_backward(values, inverse, gain, upstream):
    scaled = gain * upstream
    inner = jnp.mean(scaled * values, axis=-1, keepdims=True)
    back = inverse * scaled - values * inverse**3 * inner
    return (back, jnp.sum(upstream * values * inverse, axis=0))


def mixer_inputs(window, step_raw, taps, step_bias, decay_log):
    span = step_raw.shape[0]
    convolved = taps[0] * window[0:span]
    for tap in range(1, taps.shape[0]):
        convolved = convolved + taps[tap] * window[tap : tap + span]
    activated = jax.nn.silu(convolved)
    inner = activated[:, :DIN].reshape(span, MHEADS, MHEAD)
    basis = activated[:, DIN : DIN + STATE]
    reader = activated[:, DIN + STATE :]
    step = jax.nn.softplus(step_raw + step_bias)
    logdecay = -step * jnp.exp(decay_log)
    return (inner, basis, reader, step, logdecay)


def block_states(inner, basis, step, logdecay):
    cumulative = jnp.cumsum(logdecay, axis=0)
    weight = jnp.exp(cumulative[-1][None, :] - cumulative) * step
    state = jnp.einsum("thp,tn->hpn", inner * weight[:, :, None], basis, precision=HIGH)
    return (state, jnp.exp(cumulative[-1]))


def block_outputs(inner, basis, reader, step, logdecay, incoming, gate_z, skip):
    span = step.shape[0]
    cumulative = jnp.cumsum(logdecay, axis=0)
    intersection = jnp.dot(reader, basis.T, precision=HIGH)
    order = jnp.arange(span, dtype=jnp.int32)
    causal = (order[:, None] >= order[None, :])[:, :, None]
    gap = cumulative[:, None, :] - cumulative[None, :, :]
    decay = jnp.where(causal, jnp.exp(jnp.where(causal, gap, 0.0)), 0.0)
    mixing = intersection[:, :, None] * decay * step[None, :, :]
    within = jnp.einsum("tsh,shp->thp", mixing, inner, precision=HIGH)
    carried = jnp.exp(cumulative)[:, :, None] * jnp.einsum(
        "tn,hpn->thp", reader, incoming, precision=HIGH
    )
    output = within + carried + skip[None, :, None] * inner
    return output.reshape(span, -1) * jax.nn.silu(gate_z)


def feed_forward(rows, gate_w, up_w):
    gate = matmul(rows, gate_w)
    up = matmul(rows, up_w)
    activated = (jax.nn.silu(gate) * up).astype(jnp.bfloat16)
    return (gate, up, activated)


def turned(value, lane_low):
    return jnp.where(lane_low, -pltpu.roll(value, 96, 1), pltpu.roll(value, 32, 1))


def lanes_low(rows):
    return lax.broadcasted_iota(jnp.int32, (rows, 128), 1) % HEAD < HEAD // 2


def rope_kernel(proj_ref, cos_ref, sin_ref, q_ref, kv_ref):
    rows = proj_ref.shape[0]
    low = lanes_low(rows)
    cosine, sine = (cos_ref[...], sin_ref[...])
    for j in range(QDIM // 128):
        part = proj_ref[:, j * 128 : (j + 1) * 128]
        out = part * cosine + turned(part, low) * sine
        q_ref[:, j * 128 : (j + 1) * 128] = (out.astype(BF).astype(F32) * HEAD**-0.5).astype(BF)
    part = proj_ref[:, QDIM : QDIM + KVDIM]
    keys = (part * cosine + turned(part, low) * sine).astype(BF)
    vals = proj_ref[:, QDIM + KVDIM :].astype(BF)
    for g in range(KVHEADS):
        kv_ref[:, g * 128 : g * 128 + HEAD] = keys[:, g * HEAD : (g + 1) * HEAD]
        kv_ref[:, g * 128 + HEAD : (g + 1) * 128] = vals[:, g * HEAD : (g + 1) * HEAD]


def window_bias(pos_ref, rows, span):
    row = lax.broadcasted_iota(jnp.int32, (rows, span), 0) + (span - rows)
    col = lax.broadcasted_iota(jnp.int32, (rows, span), 1)
    return (col <= row) & (col >= row - pos_ref[...])


def nt(left, right):
    return lax.dot_general(left, right, (((1,), (1,)), ((), ())), preferred_element_type=F32)


def tn(left, right):
    return lax.dot_general(left, right, (((0,), (0,)), ((), ())), preferred_element_type=F32)


def nn(left, right):
    return lax.dot_general(left, right, (((1,), (0,)), ((), ())), preferred_element_type=F32)


def attend_kernel(q_ref, kv_ref, pos_ref, o_ref, lse_ref):
    rows, span = (q_ref.shape[0], kv_ref.shape[0])
    allowed = window_bias(pos_ref, rows, span)
    keys, vals = (kv_ref[:, :HEAD], kv_ref[:, HEAD:])
    for h in range(2):
        scores = jnp.where(allowed, nt(q_ref[:, h * HEAD : (h + 1) * HEAD], keys), NEGATIVE)
        peak = jnp.max(scores, axis=1, keepdims=True)
        weights = jnp.exp(scores - peak)
        total = jnp.sum(weights, axis=1, keepdims=True)
        accum = nn(weights.astype(BF), vals)
        o_ref[:, h * HEAD : (h + 1) * HEAD] = (accum / total).astype(BF)
        lse_ref[0, :, h : h + 1] = peak + jnp.log(total)


def attend_back_kernel(q_ref, kv_ref, pos_ref, o_ref, g_ref, lse_ref, cos_ref, sin_ref, dq_ref, dkv_ref, acc_ref):
    rows, span = (q_ref.shape[0], kv_ref.shape[0])
    step = pl.program_id(0)
    per_group = QHEADS // KVHEADS // 2
    allowed = window_bias(pos_ref, rows, span)
    keys, vals = (kv_ref[:, :HEAD], kv_ref[:, HEAD:])
    out = o_ref[...].astype(F32)
    grad = g_ref[...].astype(F32)
    both = out * grad
    parts = []
    dk, dv = (None, None)
    for h in range(2):
        lanes = slice(h * HEAD, (h + 1) * HEAD)
        query, upstream = (q_ref[:, lanes], g_ref[:, lanes])
        delta = jnp.sum(both[:, lanes], axis=1, keepdims=True)
        scores = nt(query, keys)
        probs = jnp.where(allowed, jnp.exp(jnp.where(allowed, scores - lse_ref[0, :, h : h + 1], 0.0)), 0.0)
        dp = nt(upstream, vals)
        ds = (probs * (dp - delta)).astype(BF)
        parts.append(nn(ds, keys) * HEAD**-0.5)
        dk_h, dv_h = (tn(ds, query), tn(probs.astype(BF), upstream))
        dk = dk_h if dk is None else dk + dk_h
        dv = dv_h if dv is None else dv + dv_h
    low = lanes_low(rows)
    dq = jnp.concatenate(parts, axis=1)
    dq_ref[...] = (dq * cos_ref[...] - turned(dq, low) * sin_ref[...]).astype(BF)
    dkv = jnp.concatenate([dk, dv], axis=1)

    @pl.when(step % per_group == 0)
    def _():
        acc_ref[...] = dkv

    @pl.when(step % per_group != 0)
    def _():
        acc_ref[...] = acc_ref[...] + dkv

    @pl.when(step % per_group == per_group - 1)
    def _():
        dkv_ref[...] = acc_ref[...].astype(BF)


def attend(query, window, pos):
    rows, span = (query.shape[0], window.shape[0])
    pairs = QHEADS // 2
    per_group = pairs // KVHEADS
    return pl.pallas_call(
        attend_kernel,
        grid=(pairs,),
        in_specs=[
            pl.BlockSpec((rows, 128), lambda p: (0, p)),
            pl.BlockSpec((span, 128), lambda p: (0, p // per_group)),
            pl.BlockSpec((rows, 1), lambda p: (0, 0)),
        ],
        out_specs=[
            pl.BlockSpec((rows, 128), lambda p: (0, p)),
            pl.BlockSpec((1, rows, 2), lambda p: (p, 0, 0)),
        ],
        out_shape=[
            jax.ShapeDtypeStruct((rows, QDIM), BF),
            jax.ShapeDtypeStruct((pairs, rows, 2), F32),
        ],
        name="attend",
    )(query, window, pos)


def attend_back(query, window, pos, out, grad, lse, cosine, sine):
    rows, span = (query.shape[0], window.shape[0])
    pairs = QHEADS // 2
    per_group = pairs // KVHEADS
    tile = pl.BlockSpec((rows, 128), lambda p: (0, p))
    table = pl.BlockSpec((rows, 128), lambda p: (0, 0))
    wide = pl.BlockSpec((span, 128), lambda p: (0, p // per_group))
    return pl.pallas_call(
        attend_back_kernel,
        grid=(pairs,),
        in_specs=[
            tile,
            wide,
            pl.BlockSpec((rows, 1), lambda p: (0, 0)),
            tile,
            tile,
            pl.BlockSpec((1, rows, 2), lambda p: (p, 0, 0)),
            table,
            table,
        ],
        out_specs=[tile, wide],
        out_shape=[
            jax.ShapeDtypeStruct((rows, QDIM), BF),
            jax.ShapeDtypeStruct(window.shape, BF),
        ],
        scratch_shapes=[pltpu.VMEM((span, 128), F32)],
        name="attend_back",
    )(query, window, pos, out, grad, lse, cosine, sine)


def join_kernel(count, *refs):
    own_ref, rest = (refs[0], refs[1 : 1 + count])
    cos_ref, sin_ref, out_ref = refs[1 + count :]
    total = own_ref[...].astype(F32)
    for ref in rest:
        total = total + ref[...].astype(F32)
    keys = jnp.concatenate([total[:, g * 128 : g * 128 + HEAD] for g in range(KVHEADS)], axis=1)
    vals = jnp.concatenate([total[:, g * 128 + HEAD : (g + 1) * 128] for g in range(KVHEADS)], axis=1)
    back = keys * cos_ref[...] - turned(keys, lanes_low(keys.shape[0])) * sin_ref[...]
    out_ref[:, :KVDIM] = back.astype(BF)
    out_ref[:, KVDIM:] = vals.astype(BF)


def body(
    hidden_in,
    positions,
    mixer_gain,
    attention_in,
    attention_out,
    mamba_in,
    filter_taps,
    step_bias,
    decay_log,
    skip_gain,
    gated_gain,
    mamba_out,
    feed_gain,
    gate_weight,
    up_weight,
    down_weight,
    cotangent,
):
    tokens = hidden_in[0]
    token_pos = positions[0]
    upstream = cotangent[0]
    length = tokens.shape[0]
    ctx_count = lax.axis_size("ctx")
    group = lax.axis_size("fsdp")
    longest = length * ctx_count // 2
    reach = min(ctx_count - 1, (longest - 1 + length - 1) // length)

    small_parts = (
        mixer_gain,
        feed_gain,
        gated_gain,
        filter_taps.reshape(-1),
        step_bias,
        decay_log,
        skip_gain,
    )
    sizes = [part.shape[0] for part in small_parts]
    bounds = [sum(sizes[:k]) for k in range(len(sizes) + 1)]
    small = jnp.stack(ordered(xor_gather(jnp.concatenate(small_parts), "fsdp"), "fsdp"))
    mixer_f, feed_f, gated_f, taps_f, bias_f, rate_f, skip_f = (
        small[:, bounds[k] : bounds[k + 1]].astype(F32) for k in range(len(sizes))
    )
    taps_f = taps_f.reshape(group, CONV, -1).transpose(1, 0, 2).reshape(CONV, -1)
    mixer_f, feed_f, gated_f, bias_f, rate_f, skip_f = (
        part.reshape(-1) for part in (mixer_f, feed_f, gated_f, bias_f, rate_f, skip_f)
    )
    attend_in = jnp.concatenate(ordered(xor_gather(attention_in, "fsdp"), "fsdp"), axis=0)
    mamba_proj = lax.all_gather(mamba_in, "fsdp", axis=0, tiled=True)
    attend_rows = attention_out.shape[0]
    outs = lax.all_gather(jnp.concatenate([attention_out, mamba_out], axis=0), "fsdp", axis=0)
    attend_out = outs[:, :attend_rows].reshape(-1, outs.shape[-1])
    mamba_back_w = outs[:, attend_rows:].reshape(-1, outs.shape[-1])

    normed, inverse_one = rms_forward(tokens, mixer_f)
    normed_b = normed.astype(BF)
    projected = matmul(normed_b, attend_in)
    lane = jnp.arange(128, dtype=jnp.int32) % (HEAD // 2)
    frequency = jnp.exp(-math.log(ROPE_BASE) * lane.astype(F32) * (2.0 / HEAD))
    angle = token_pos.astype(F32)[:, None] * frequency[None, :]
    cosine, sine = (jnp.cos(angle), jnp.sin(angle))
    query, kv_own = pl.pallas_call(
        rope_kernel,
        out_shape=[
            jax.ShapeDtypeStruct((length, QDIM), BF),
            jax.ShapeDtypeStruct((length, 2 * KVDIM), BF),
        ],
        name="rope",
    )(projected, cosine, sine)
    window = jnp.concatenate(
        [shift(kv_own, "ctx", k) for k in range(reach, 0, -1)] + [kv_own], axis=0
    )
    pos_column = token_pos[:, None]
    attended, log_total = attend(query, window, pos_column)
    attend_branch = matmul(attended, attend_out)
    mixed = matmul(normed_b, mamba_proj)
    gate_z = mixed[:, :DIN]
    conv_in = mixed[:, DIN : DIN + XBC].astype(BF)
    step_raw = mixed[:, DIN + XBC :]
    edge = shift(conv_in[length - CONV + 1 :], "ctx", 1)
    conv_window = jnp.concatenate([edge, lax.optimization_barrier(conv_in)], axis=0).astype(F32)
    prepared, prepare_back = jax.vjp(mixer_inputs, conv_window, step_raw, taps_f, bias_f, rate_f)
    inner, basis, reader, step, logdecay = prepared
    (local_state, decay), states_back = jax.vjp(block_states, inner, basis, step, logdecay)
    incoming = carried(local_state, decay, "ctx", 1)
    gated, outputs_back = jax.vjp(
        block_outputs, inner, basis, reader, step, logdecay, incoming, gate_z, skip_f
    )
    mamba_normed, inverse_three = rms_forward(gated, gated_f)
    mamba_normed_b = mamba_normed.astype(BF)
    middle = tokens + attend_branch + matmul(mamba_normed_b, mamba_back_w)
    feed_normed, inverse_two = rms_forward(middle, feed_f)
    feed_b = feed_normed.astype(BF)
    upstream_all = jnp.concatenate(xor_gather(upstream.astype(BF), "fsdp"), axis=0)
    rows_all = jnp.concatenate(xor_gather(feed_b, "fsdp"), axis=0)

    gate, up, activated = feed_forward(rows_all, gate_weight, up_weight)
    act_grad = matmul(upstream_all, down_weight.T)
    sigma = jax.nn.sigmoid(gate)
    gate_part = (act_grad * up * sigma * (1.0 + gate * (1.0 - sigma))).astype(BF)
    up_part = (act_grad * gate * sigma).astype(BF)
    feed_back = matmul(gate_part, gate_weight.T) + matmul(up_part, up_weight.T)
    feed_grad = xor_scatter(jnp.split(feed_back, group, axis=0), "fsdp")
    feed_out = xor_scatter(jnp.split(matmul(activated, down_weight), group, axis=0), "fsdp")
    output = middle + feed_out
    feed_totals = lax.psum(
        (
            matmul(rows_all.T, gate_part).astype(BF),
            matmul(rows_all.T, up_part).astype(BF),
            matmul(activated.T, upstream_all).astype(BF),
        ),
        "ctx",
    )

    back_two, feed_gain_grad = rms_backward(middle, inverse_two, feed_f, feed_grad)
    middle_grad = upstream + back_two
    middle_b = middle_grad.astype(BF)
    out_columns = jnp.concatenate(
        [
            part
            for pair in zip(column_blocks(attended, "fsdp"), column_blocks(mamba_normed_b, "fsdp"))
            for part in pair
        ],
        axis=1,
    )
    out_grads = xor_scatter(jnp.split(matmul(out_columns.T, middle_b), group, axis=0), "fsdp")
    out_grads, feed_totals = lax.optimization_barrier((out_grads.astype(BF), feed_totals))
    out_totals = lax.psum(out_grads, "ctx")

    normed_mamba_grad = matmul(middle_b, mamba_back_w.T)
    gated_grad, gated_gain_grad = rms_backward(gated, inverse_three, gated_f, normed_mamba_grad)
    (
        grad_inner,
        grad_basis,
        grad_reader,
        grad_step,
        grad_logdecay,
        grad_incoming,
        grad_gate_z,
        skip_grad,
    ) = outputs_back(gated_grad)
    state_grad = carried(grad_incoming, decay, "ctx", -1)
    decay_grad = jnp.sum(state_grad * incoming, axis=(1, 2))
    more_inner, more_basis, more_step, more_logdecay = states_back((state_grad, decay_grad))
    window_grad, raw_grad, taps_grad, bias_grad, rate_grad = prepare_back(
        (
            grad_inner + more_inner,
            grad_basis + more_basis,
            grad_reader,
            grad_step + more_step,
            grad_logdecay + more_logdecay,
        )
    )
    returned = shift(window_grad[: CONV - 1], "ctx", -1)
    conv_grad = window_grad[CONV - 1 :]
    conv_grad = jnp.concatenate(
        [conv_grad[: length - CONV + 1], conv_grad[length - CONV + 1 :] + returned], axis=0
    )
    mixed_grad = jnp.concatenate([grad_gate_z, conv_grad, raw_grad], axis=1).astype(BF)
    normed_columns = jnp.concatenate(column_blocks(normed_b, "fsdp"), axis=1)
    mamba_in_grad = xor_scatter(
        jnp.split(matmul(normed_columns.T, mixed_grad), group, axis=0), "fsdp"
    )
    mamba_in_grad, out_totals = lax.optimization_barrier((mamba_in_grad.astype(BF), out_totals))
    mamba_in_total = lax.psum(mamba_in_grad, "ctx")
    normed_grad = matmul(mixed_grad, mamba_proj.T)

    attended_grad = matmul(middle_b, attend_out.T).astype(BF)
    query_grad, window_back = attend_back(
        query, window, pos_column, attended, attended_grad, log_total, cosine, sine
    )
    pieces = jnp.split(window_back, reach + 1, axis=0)
    kv_grad = pl.pallas_call(
        functools.partial(join_kernel, reach),
        out_shape=jax.ShapeDtypeStruct((length, 2 * KVDIM), BF),
        name="join",
    )(
        pieces[reach],
        *[shift(pieces[reach - k], "ctx", -k) for k in range(1, reach + 1)],
        cosine,
        sine,
    )
    projected_grad = jnp.concatenate([query_grad, kv_grad], axis=1)
    attend_in_grad = xor_scatter(
        jnp.split(matmul(normed_columns.T, projected_grad), group, axis=0), "fsdp"
    )
    normed_grad = normed_grad + matmul(projected_grad, attend_in.T)
    back_one, mixer_gain_grad = rms_backward(tokens, inverse_one, mixer_f, normed_grad)
    input_grad = middle_grad + back_one

    small_grads = jnp.concatenate(
        [
            mixer_gain_grad.reshape(group, -1),
            feed_gain_grad.reshape(group, -1),
            gated_gain_grad.reshape(group, -1),
            taps_grad.reshape(CONV, group, -1).transpose(1, 0, 2).reshape(group, -1),
            bias_grad.reshape(group, -1),
            rate_grad.reshape(group, -1),
            skip_grad.reshape(group, -1),
        ],
        axis=1,
    )
    mine = lax.axis_index("fsdp")
    small_own = xor_scatter(
        [lax.dynamic_index_in_dim(small_grads, mine ^ d, 0, False) for d in range(group)], "fsdp"
    )
    last, mamba_in_total = lax.optimization_barrier(
        ((attend_in_grad.astype(BF), small_own.astype(BF)), mamba_in_total)
    )
    attend_in_total, small_total = lax.psum(last, "ctx")
    total_mixer, total_feed, total_gated, total_taps, total_bias, total_rate, total_skip = (
        small_total[bounds[k] : bounds[k + 1]].astype(F32) for k in range(len(sizes))
    )
    return (
        output[None],
        input_grad[None],
        total_mixer,
        attend_in_total.astype(F32),
        out_totals[:attend_rows].astype(F32),
        mamba_in_total.astype(F32),
        total_taps.reshape(CONV, -1),
        total_bias,
        total_rate,
        total_skip,
        total_gated,
        out_totals[attend_rows:].astype(F32),
        total_feed,
        *(part.astype(F32) for part in feed_totals),
    )


def solution(mesh):
    return jax.shard_map(
        body,
        mesh=mesh,
        in_specs=(
            P("fsdp", "ctx", None),
            P("fsdp", "ctx"),
            P("fsdp"),
            P("fsdp", None),
            P("fsdp", None),
            P("fsdp", None),
            P(None, "fsdp"),
            P("fsdp"),
            P("fsdp"),
            P("fsdp"),
            P("fsdp"),
            P("fsdp", None),
            P("fsdp"),
            P(None, "fsdp"),
            P(None, "fsdp"),
            P("fsdp", None),
            P("fsdp", "ctx", None),
        ),
        out_specs=(
            P("fsdp", "ctx", None),
            P("fsdp", "ctx", None),
            P("fsdp"),
            P("fsdp", None),
            P("fsdp", None),
            P("fsdp", None),
            P(None, "fsdp"),
            P("fsdp"),
            P("fsdp"),
            P("fsdp"),
            P("fsdp"),
            P("fsdp", None),
            P("fsdp"),
            P(None, "fsdp"),
            P(None, "fsdp"),
            P("fsdp", None),
        ),
        check_vma=False,
    )
```

time: 1160 us -> 826 us (0.71)
  waiting for transfers between devices: 598 us -> 403 us
  blocking collectives: 147 us -> 20 us
  matrix products: 205 us -> 113 us
  starting transfers between devices: 5.89 us -> 75.1 us
  other arithmetic: 116 us -> 90 us
  Pallas kernels: 0 us -> 25.1 us
  local copies, waits for them, and re-layouts: 53.3 us -> 72.2 us
    reduce_scatter x9 -> x0, waiting for transfers between devices: 346 us -> none  [the longest x1 64 us: body(): lax.psum_scatter(mamba_in_grad.astype(jnp.bfloat16), 'fsdp', scatter_dime...]
    all_gather x7 -> x0, blocking collectives: 110 us -> none  [the longest x1 36.7 us: body(): key_piece = lax.all_gather(keys, 'ctx', axis=0, tiled=True)]
    ppermute x2 -> x50, waiting for transfers between devices: 0.01 us -> 109 us  [the longest x30 83.3 us: swap(): lax.ppermute(value, axis, [(source, source ^ bit) for source in range(cou...]
    dot_general x28 -> x0, matrix products: 80.8 us -> none  [the longest x8 22.6 us: masked_scores(): jnp.einsum('grd,pgd->grp', query_rows, key_block, preferred_element_type=...]
    ppermute x2 -> x50, starting transfers between devices: 4.91 us -> 74.6 us  [the longest x20 57.3 us: shift(): lax.ppermute(value, axis, [(source, source + steps) for source in range(f...]
    psum x1 -> x4, waiting for transfers between devices: 191 us -> 261 us  [the longest x1 76.9 us: body(): mamba_in_total = lax.psum(mamba_in_grad, 'ctx')]
    pallas_call x0 -> x4, Pallas kernels: none -> 25.1 us  [the longest x1 12 us: attend_back(): pl.pallas_call(attend_back_kernel, grid=(pairs,), in_specs=[tile, wide, p...]
    all_gather x9 -> x2, waiting for transfers between devices: 55.7 us -> 32.6 us  [the longest x1 32.6 us: body(): mamba_proj = lax.all_gather(mamba_in, 'fsdp', axis=0, tiled=True)]
  transfers between devices with their start and end apart: 22 -> 56, of which waited for: 12 -> 18; matrix products, arithmetic and copies ran while one was open for 24% -> 31% of each run, Pallas kernels for 0% -> 2%
where the time goes in v1:
time: 826 us; the launch traced here: 815 us
  waiting for transfers between devices  403 us (49%)
  matrix products  113 us (14%)
  other arithmetic  90 us (11%)
  starting transfers between devices  75.1 us (9%)
  local copies, waits for them, and re-layouts  72.2 us (9%)
  Pallas kernels  25.1 us (3%)
  blocking collectives  20 us (2%)
  between operations  16.6 us (2%)
    ppermute x30, waiting for transfers between devices, swap(): lax.ppermute(value, axis, [(source, source ^ bit) for source in range(cou...  83.3 us
    psum x1, waiting for transfers between devices, body(): mamba_in_total = lax.psum(mamba_in_grad, 'ctx')  76.9 us
    psum x1, waiting for transfers between devices, body(): out_totals = lax.psum(out_grads, 'ctx')  76.4 us
    psum x1, waiting for transfers between devices, body(): attend_in_total, small_total = lax.psum(last, 'ctx')  63.7 us
    ppermute x20, starting transfers between devices, shift(): lax.ppermute(value, axis, [(source, source + steps) for source in range(f...  57.3 us
    dot_general x20, matrix products, matmul(): return jnp.dot(left, right, preferred_element_type=jnp.float32)  55.1 us
    psum x1, waiting for transfers between devices, body(): lax.psum((matmul(rows_all.T, gate_part).astype(BF), matmul(rows_all.T, up...  43.6 us
    all_gather x1, waiting for transfers between devices, body(): mamba_proj = lax.all_gather(mamba_in, 'fsdp', axis=0, tiled=True)  32.6 us
  transfers between devices with their start and end apart: 56, of which 18 were waited for; matrix products, arithmetic and copies ran while one was open for 31% of the time, Pallas kernels for 2%

profile of v1, /device:TPU:0, one launch (start us, length us, event | category | flops | bytes accessed | tf_op | source)
XLA Modules:
  0.0 815.1 jit_solution(10375029066807186799)
XLA Ops:
  8.8 4.1 concatenate.41
  12.9 3.0 collective-permute-start.1
  26.1 6.5 collective-permute-done.4
  37.9 2.3 rope.1
  40.3 5.3 collective-permute-start.6
  45.6 32.6 %all-gather.4.cloned.1.call-done = bf16[1024,3352]{0,1:T(8,128)(2,1)} async-done(((bf16[256,3352]{0,1:T(8,128)(2,1)}), bf16[1024,3352]{0,1:T(8,128)(2,1)}) %all-gather.4.cloned.1.call-update) | async-done | bytes 6864912 | tf_op jit(solution)/shard_map/all_gather | solution.py:367
  78.2 5.0 fusion.167
  83.3 3.4 collective-permute-start.10
  92.4 2.3 fusion.30
  97.3 3.1 copy.203
  100.3 3.9 fusion.168
  104.2 3.4 collective-permute-start.13
  110.9 3.4 collective-permute-start.9
  114.3 3.4 collective-permute-start.8
  117.8 3.3 collective-permute-start.7
  128.8 4.5 collective-permute-start.11
  136.2 10.4 %collective-permute-start.15 = (bf16[24,64,128]{2,1,0:T(8,128)(2,1)}, bf16[24,64,128]{2,1,0:T(8,128)(2,1)}, u32[]{:S(2)}, u32[]{:S(2)}) collective-permute-start(bf16[24,64,128]{2,1,0:T(8,128)(2,1)} %fusion.81), channel_id=1, source_target_pairs={{0,16},{4,20},{8,24},{12,28},{1,17},{5,21},{9,25},{13,29},{2,18},{... | collective-permute-start | bytes 1179656 | tf_op jit(solution)/shard_map/ppermute | solution.py:37
  147.9 8.7 %attend.1 = (bf16[256,512]{1,0:T(8,128)(2,1)}, f32[4,256,2]{2,1,0:T(8,128)}) custom-call(bf16[256,512]{1,0:T(8,128)(2,1)} %get-tuple-element.31.q_ref, bf16[1280,256]{1,0:T(8,128)(2,1)} %constant_dynamic-update-slice_fusion.kv_ref, s32[256,1]{1,0:T(8,128)} %copy.201.pos_ref), custom_call_target="tpu_custom_call" | custom-call | tf_op jit(solution)/shard_map/attend/pallas_call | solution.py:256
  156.6 2.3 slice.183
  158.8 3.9 slice.202
  165.0 4.2 collective-permute-start.12
  173.0 2.7 fusion.114
  175.7 9.3 %fusion.35 = f32[256,24,64]{0,2,1:T(8,128)} fusion(f32[256,24,64]{0,2,1:T(8,128)S(1)} %bitcast.196, f32[256,24,64]{0,2,1:T(8,128)S(1)} %fusion.114, f32[256,24]{0,1:T(8,128)S(1)} %copy-done.99, f32[256,24]{0,1:T(8,128)S(1)} %copy-done.102, f32[256,256]{1,0:T(8,128)S(1)} %fusion.120, pred[256,256]{1,0:T(8,128)(4,1)S(1)} %copy-done.89, f32[24]{0:T(128)} %reshape.323, ...), kind=kOutput, calls=%fused_computation.64 | convolution fusion | flops 1217396736 | bytes 5120096 | tf_op jit(solution)/shard_map/jvp(tsh,shp->thp)/dot_general | solution.py:140
  185.0 3.0 copy.213
  188.0 2.6 multiply_reduce_fusion.10
  200.3 3.9 collective-permute-done.29
  208.3 2.5 fusion.153
  210.7 2.4 fusion.154
  213.2 3.7 multiply_convert_fusion
  222.1 3.5 convolution_convert_fusion.1
  228.0 3.5 convolution_convert_fusion.2
  231.5 9.1 %collective-permute-done.27 = bf16[256,1024]{1,0:T(8,128)(2,1)S(1)} collective-permute-done((bf16[256,1024]{1,0:T(8,128)(2,1)S(1)}, bf16[256,1024]{1,0:T(8,128)(2,1)S(1)}, u32[]{:S(2)}, u32[]{:S(2)}) %collective-permute-start.27) | collective-permute-done | bytes 524320 | tf_op jit(solution)/shard_map/ppermute | solution.py:42
  241.7 9.3 %collective-permute-done.21 = bf16[256,1024]{1,0:T(8,128)(2,1)S(1)} collective-permute-done((bf16[256,1024]{1,0:T(8,128)(2,1)S(1)}, bf16[256,1024]{1,0:T(8,128)(2,1)S(1)}, u32[]{:S(2)}, u32[]{:S(2)}) %collective-permute-start.21) | collective-permute-done | bytes 524320 | tf_op jit(solution)/shard_map/ppermute | solution.py:42
  253.8 2.9 multiply_reduce_fusion.6
  258.4 12.0 %attend_back.1 = (bf16[256,512]{1,0:T(8,128)(2,1)}, bf16[1280,256]{1,0:T(8,128)(2,1)}) custom-call(bf16[256,512]{1,0:T(8,128)(2,1)} %get-tuple-element.31.q_ref, bf16[1280,256]{1,0:T(8,128)(2,1)} %constant_dynamic-update-slice_fusion.kv_ref, s32[256,1]{1,0:T(8,128)} %copy.201.pos_ref, bf16[256,512]{1,0:T(8,128)(2,1)} %get-tuple-element.33.o_ref, ...), custom_call_target="tpu_custom_call" | custom-call | tf_op jit(solution)/shard_map/attend_back/pallas_call | solution.py:283
  277.5 6.6 multiply_reduce_fusion.5
  284.1 3.1 copy.215
  287.2 12.7 %fusion.12 = (f32[256,24]{0,1:T(8,128)}, f32[256,24]{0,1:T(8,128)}, f32[256,24]{0,1:T(8,128)}, f32[256,256]{1,0:T(8,128)}) fusion(f32[256,24]{0,1:T(8,128)S(1)} %copy-done.100, f32[256,24]{0,1:T(8,128)} %copy.207, f32[256,256]{1,0:T(8,128)S(1)} %copy-done.75, pred[256,256]{1,0:T(8,128)(4,1)S(1)} %copy-done.90, f32[24,64,256]{2,1,0:T(8,128)} %bitcast.198, ...), kind=kOutput, calls=%fused_computation.17 | convolution fusion | flops 1231468544 | bytes 3858432 | tf_op jit(solution)/shard_map/transpose(jvp(tsh,shp->thp))/dot_general | solution.py:140
  300.0 3.4 fusion.171
  313.7 3.8 reduce-window.24
  324.4 9.2 %collective-permute-done.31 = bf16[24,64,128]{2,1,0:T(8,128)(2,1)S(1)} collective-permute-done((bf16[24,64,128]{2,1,0:T(8,128)(2,1)S(1)}, bf16[24,64,128]{2,1,0:T(8,128)(2,1)S(1)}, u32[]{:S(2)}, u32[]{:S(2)}) %collective-permute-start.31) | collective-permute-done | bytes 393248 | tf_op jit(solution)/shard_map/ppermute | solution.py:37
  341.4 5.3 fusion.56
  346.8 10.4 %collective-permute-done.32 = bf16[24,64,128]{2,1,0:T(8,128)(2,1)} collective-permute-done((bf16[24,64,128]{2,1,0:T(8,128)(2,1)}, bf16[24,64,128]{2,1,0:T(8,128)(2,1)}, u32[]{:S(2)}, u32[]{:S(2)}) %collective-permute-start.32) | collective-permute-done | bytes 393248 | tf_op jit(solution)/shard_map/ppermute | solution.py:37
  357.2 3.1 multiply_reduce_fusion.8
  360.3 7.1 fusion.34
  367.5 3.0 copy.216
  370.5 4.5 fusion.59
  375.1 3.3 multiply_reduce_fusion.4
  386.7 2.5 reduce-window.26
  397.3 6.9 fusion.173
  406.2 3.6 convolution_convert_fusion
  422.5 3.6 fusion.8
  428.9 3.1 fusion.100
  435.9 55.4 %collective-permute-done.49 = bf16[512,1024]{1,0:T(8,128)(2,1)S(1)} collective-permute-done((bf16[512,1024]{1,0:T(8,128)(2,1)S(1)}, bf16[512,1024]{1,0:T(8,128)(2,1)S(1)}, u32[]{:S(2)}, u32[]{:S(2)}) %collective-permute-start.49) | collective-permute-done | bytes 1048608 | tf_op jit(solution)/shard_map/ppermute | solution.py:42
  491.3 3.3 fusion.27
  494.7 43.6 %all-reduce.25.cloned.1.call-done = (bf16[1024,512]{1,0:T(8,128)(2,1)}, bf16[1024,512]{1,0:T(8,128)(2,1)}, bf16[512,1024]{1,0:T(8,128)(2,1)}) async-done(((bf16[1024,512]{1,0:T(8,128)(2,1)}, bf16[1024,512]{1,0:T(8,128)(2,1)}, bf16[512,1024]{1,0:T(8,128)(2,1)}), (bf16[1024,512]{1,0:T(8,128)(2,1)}, bf16[1024,512]{1,0:T(8,128)(2,1)}, bf16[512,1024]{1,0:T(8,128)(2,1)})) %all-reduce.25.cloned.1.call-update) | async-done | bytes 3145744 | tf_op jit(solution)/shard_map/psum | solution.py:424
  538.5 4.8 fusion.10
  543.3 76.4 %all-reduce.19.cloned.1.call-done = bf16[512,1024]{1,0:T(8,128)(2,1)} async-done(((bf16[512,1024]{1,0:T(8,128)(2,1)}), bf16[512,1024]{1,0:T(8,128)(2,1)}) %all-reduce.19.cloned.1.call-update) | async-done | bytes 1048592 | tf_op jit(solution)/shard_map/psum | solution.py:446
  620.1 6.6 fusion.77
  629.6 2.6 fusion.74
  639.1 76.9 %all-reduce.21.cloned.1.call-done = bf16[256,3352]{0,1:T(8,128)(2,1)} async-done(((bf16[256,3352]{0,1:T(8,128)(2,1)}), bf16[256,3352]{0,1:T(8,128)(2,1)}) %all-reduce.21.cloned.1.call-update) | async-done | bytes 1716240 | tf_op jit(solution)/shard_map/psum | solution.py:483
  716.0 20.0 %psum.54 = bf16[2706]{0:T(1024)(128)(2,1)S(1)} all-reduce(bf16[2706]{0:T(1024)(128)(2,1)S(1)} %add_convert_fusion), channel_id=1, replica_groups=mesh['ctx'=8,'fsdp'=4] {'ctx'}, use_global_device_ids=true, to_apply=%region_36.37 | all-reduce | flops 2706 | bytes 10824 | tf_op jit(solution)/shard_map/psum | solution.py:528
  737.3 3.6 convert_element_type.319
  742.1 63.7 %all-reduce.23.cloned.1.call-done = bf16[256,768]{1,0:T(8,128)(2,1)} async-done(((bf16[256,768]{1,0:T(8,128)(2,1)}), bf16[256,768]{1,0:T(8,128)(2,1)}) %all-reduce.23.cloned.1.call-update) | async-done | bytes 393232 | tf_op jit(solution)/shard_map/psum | solution.py:528
  (538 shorter events, 156.8 us)
Async XLA Ops:
  7.2 206.0 %copy-start = (bf16[512,1024]{1,0:T(8,128)(2,1)S(1)}, bf16[512,1024]{1,0:T(8,128)(2,1)}, u32[]{:S(2)}) copy-start(bf16[512,1024]{1,0:T(8,128)(2,1)} %param.32) | copy-start | bytes 3145732
  7.2 71.0 %all-gather.4.cloned.1.call-start = ((), (), s32[]{:S(2)}) async-start(), calls=%async_computation | async-start | bytes 8581120 | tf_op jit(solution)/shard_map/all_gather | solution.py:367
  8.0 148.6 %all-gather.6.cloned.1.call-start = ((), (), s32[]{:S(2)}) async-start(), calls=%async_computation.4 | async-start | bytes 5242880 | tf_op jit(solution)/shard_map/all_gather | solution.py:369
  12.9 10.2 %collective-permute-start.1 = (bf16[2706]{0:T(1024)(128)(2,1)S(1)}, bf16[2706]{0:T(1024)(128)(2,1)S(1)}, u32[]{:S(2)}, u32[]{:S(2)}) collective-permute-start(bf16[2706]{0:T(1024)(128)(2,1)S(1)} %concatenate.41), channel_id=1, source_target_pairs={{0,2},{1,3},{2,0},{3,1},{4,6},{5,7},{6,4},{7,5},{8,10},{9,11},{10,... | collective-permute-start | bytes 16244 | tf_op jit(solution)/shard_map/ppermute | solution.py:42
  15.8 8.7 %collective-permute-start = (bf16[2706]{0:T(1024)(128)(2,1)S(1)}, bf16[2706]{0:T(1024)(128)(2,1)S(1)}, u32[]{:S(2)}, u32[]{:S(2)}) collective-permute-start(bf16[2706]{0:T(1024)(128)(2,1)S(1)} %concatenate.41), channel_id=1, source_target_pairs={{0,1},{1,0},{2,3},{3,2},{4,5},{5,4},{6,7},{7,6},{8,9},{9,8},{10,11... | collective-permute-start | bytes 16244 | tf_op jit(solution)/shard_map/ppermute | solution.py:42
  15.9 16.8 %collective-permute-start.4 = (bf16[256,768]{1,0:T(8,128)(2,1)}, bf16[256,768]{1,0:T(8,128)(2,1)S(1)}, u32[]{:S(2)}, u32[]{:S(2)}) collective-permute-start(bf16[256,768]{1,0:T(8,128)(2,1)} %param.20), channel_id=1, source_target_pairs={{0,2},{1,3},{2,0},{3,1},{4,6},{5,7},{6,4},{7,5},{8,10},{9,11},{10,... | collective-permute-start | bytes 1179656 | tf_op jit(solution)/shard_map/ppermute | solution.py:42
  16.0 18.8 %collective-permute-start.3 = (bf16[256,768]{1,0:T(8,128)(2,1)}, bf16[256,768]{1,0:T(8,128)(2,1)}, u32[]{:S(2)}, u32[]{:S(2)}) collective-permute-start(bf16[256,768]{1,0:T(8,128)(2,1)} %param.20), channel_id=1, source_target_pairs={{0,1},{1,0},{2,3},{3,2},{4,5},{5,4},{6,7},{7,6},{8,9},{9,8},{10,11... | collective-permute-start | bytes 1179656 | tf_op jit(solution)/shard_map/ppermute | solution.py:42
  17.2 181.0 %collective-permute-start.23 = (bf16[256,1024]{1,0:T(8,128)(2,1)}, bf16[256,1024]{1,0:T(8,128)(2,1)}, u32[]{:S(2)}, u32[]{:S(2)}) collective-permute-start(bf16[256,1024]{1,0:T(8,128)(2,1)} %bitcast_convert_fusion), channel_id=1, source_target_pairs={{0,2},{1,3},{2,0},{3,1},{4,6},{5,7},{6,4},{7,5},{8,10},{9,11},{10,... | collective-permute-start | bytes 1572872 | tf_op jit(solution)/shard_map/ppermute | solution.py:42
  21.0 517.3 %all-reduce.25.cloned.1.call-start = ((), (), s32[]{:S(2)}) async-start(), calls=%async_computation.5 | async-start | bytes 6291456 | tf_op jit(solution)/shard_map/psum | solution.py:424
  23.1 1.5 collective-permute-start.2
  32.6 2.2 collective-permute-start.5
  33.2 59.1 %copy-start.82 = (f32[1792]{0:T(1024)}, f32[1792]{0:T(1024)S(1)}, u32[]{:S(2)}) copy-start(f32[1792]{0:T(1024)S(1)} %mul.640) | copy-start | bytes 21508
  40.3 77.5 %collective-permute-start.6 = (bf16[256,256]{1,0:T(8,128)(2,1)}, bf16[256,256]{1,0:T(8,128)(2,1)}, u32[]{:S(2)}, u32[]{:S(2)}) collective-permute-start(bf16[256,256]{1,0:T(8,128)(2,1)} %get-tuple-element.32), channel_id=1, source_target_pairs={{0,16},{4,20},{8,24},{12,28},{1,17},{5,21},{9,25},{13,29},{2,18},{... | collective-permute-start | bytes 393224 | tf_op jit(solution)/shard_map/ppermute | solution.py:37
  83.3 7.6 collective-permute-start.10
  104.2 18.5 %collective-permute-start.13 = (bf16[24,64,128]{2,1,0:T(8,128)(2,1)}, bf16[24,64,128]{2,1,0:T(8,128)(2,1)S(1)}, u32[]{:S(2)}, u32[]{:S(2)}) collective-permute-start(bf16[24,64,128]{2,1,0:T(8,128)(2,1)} %get-tuple-element.145), channel_id=1, source_target_pairs={{0,4},{4,8},{8,12},{12,16},{16,20},{20,24},{24,28},{1,5},{5,9},{9,... | collective-permute-start | bytes 1179656 | tf_op jit(solution)/shard_map/ppermute | solution.py:37
  110.9 35.6 %collective-permute-start.9 = (bf16[256,256]{1,0:T(8,128)(2,1)}, bf16[256,256]{1,0:T(8,128)(2,1)S(1)}, u32[]{:S(2)}, u32[]{:S(2)}) collective-permute-start(bf16[256,256]{1,0:T(8,128)(2,1)} %get-tuple-element.32), channel_id=1, source_target_pairs={{0,4},{4,8},{8,12},{12,16},{16,20},{20,24},{24,28},{1,5},{5,9},{9,... | collective-permute-start | bytes 393224 | tf_op jit(solution)/shard_map/ppermute | solution.py:37
  114.3 12.5 %collective-permute-start.8 = (bf16[256,256]{1,0:T(8,128)(2,1)}, bf16[256,256]{1,0:T(8,128)(2,1)S(1)}, u32[]{:S(2)}, u32[]{:S(2)}) collective-permute-start(bf16[256,256]{1,0:T(8,128)(2,1)} %get-tuple-element.32), channel_id=1, source_target_pairs={{0,8},{4,12},{8,16},{12,20},{16,24},{20,28},{1,9},{5,13},{9,17},{1... | collective-permute-start | bytes 393224 | tf_op jit(solution)/shard_map/ppermute | solution.py:37
  117.8 8.3 %collective-permute-start.7 = (bf16[256,256]{1,0:T(8,128)(2,1)}, bf16[256,256]{1,0:T(8,128)(2,1)S(1)}, u32[]{:S(2)}, u32[]{:S(2)}) collective-permute-start(bf16[256,256]{1,0:T(8,128)(2,1)} %get-tuple-element.32), channel_id=1, source_target_pairs={{0,12},{4,16},{8,20},{12,24},{16,28},{1,13},{5,17},{9,21},{13,25},... | collective-permute-start | bytes 393224 | tf_op jit(solution)/shard_map/ppermute | solution.py:37
  124.2 10.9 %collective-permute-start.14 = (bf16[24,64,128]{2,1,0:T(8,128)(2,1)S(1)}, bf16[24,64,128]{2,1,0:T(8,128)(2,1)S(1)}, u32[]{:S(2)}, u32[]{:S(2)}) collective-permute-start(bf16[24,64,128]{2,1,0:T(8,128)(2,1)S(1)} %fusion.95), channel_id=1, source_target_pairs={{0,8},{4,12},{8,16},{12,20},{16,24},{20,28},{1,9},{5,13},{9,17},{1... | collective-permute-start | bytes 1179656 | tf_op jit(solution)/shard_map/ppermute | solution.py:37
  127.5 5.8 collective-permute-start.28
  128.8 5.8 collective-permute-start.11
  136.2 36.8 %collective-permute-start.15 = (bf16[24,64,128]{2,1,0:T(8,128)(2,1)}, bf16[24,64,128]{2,1,0:T(8,128)(2,1)}, u32[]{:S(2)}, u32[]{:S(2)}) collective-permute-start(bf16[24,64,128]{2,1,0:T(8,128)(2,1)} %fusion.81), channel_id=1, source_target_pairs={{0,16},{4,20},{8,24},{12,28},{1,17},{5,21},{9,25},{13,29},{2,18},{... | collective-permute-start | bytes 1179656 | tf_op jit(solution)/shard_map/ppermute | solution.py:37
  165.0 5.8 collective-permute-start.12
  195.6 10.6 %collective-permute-start.17 = (bf16[256,1024]{1,0:T(8,128)(2,1)}, bf16[256,1024]{1,0:T(8,128)(2,1)}, u32[]{:S(2)}, u32[]{:S(2)}) collective-permute-start(bf16[256,1024]{1,0:T(8,128)(2,1)} %multiply_convert_fusion.4), channel_id=1, source_target_pairs={{0,2},{1,3},{2,0},{3,1},{4,6},{5,7},{6,4},{7,5},{8,10},{9,11},{10,... | collective-permute-start | bytes 1572872 | tf_op jit(solution)/shard_map/ppermute | solution.py:42
  196.2 16.9 %collective-permute-start.22 = (bf16[256,1024]{1,0:T(8,128)(2,1)}, bf16[256,1024]{1,0:T(8,128)(2,1)}, u32[]{:S(2)}, u32[]{:S(2)}) collective-permute-start(bf16[256,1024]{1,0:T(8,128)(2,1)} %bitcast_convert_fusion), channel_id=1, source_target_pairs={{0,1},{1,0},{2,3},{3,2},{4,5},{5,4},{6,7},{7,6},{8,9},{9,8},{10,11... | collective-permute-start | bytes 1572872 | tf_op jit(solution)/shard_map/ppermute | solution.py:42
  198.3 14.9 %collective-permute-start.24 = (bf16[256,1024]{1,0:T(8,128)(2,1)}, bf16[256,1024]{1,0:T(8,128)(2,1)S(1)}, u32[]{:S(2)}, u32[]{:S(2)}) collective-permute-start(bf16[256,1024]{1,0:T(8,128)(2,1)} %collective-permute-done.23), channel_id=1, source_target_pairs={{0,1},{1,0},{2,3},{3,2},{4,5},{5,4},{6,7},{7,6},{8,9},{9,8},{10,11... | collective-permute-start | bytes 1572872 | tf_op jit(solution)/shard_map/ppermute | solution.py:42
  198.8 5.5 collective-permute-start.29
  204.8 2.8 collective-permute-start.16
  206.1 2.1 collective-permute-start.18
  219.6 11.9 %collective-permute-start.25 = (bf16[256,1024]{1,0:T(8,128)(2,1)S(1)}, bf16[256,1024]{1,0:T(8,128)(2,1)S(1)}, u32[]{:S(2)}, u32[]{:S(2)}) collective-permute-start(bf16[256,1024]{1,0:T(8,128)(2,1)S(1)} %get-tuple-element.92), channel_id=1, source_target_pairs={{0,1},{1,0},{2,3},{3,2},{4,5},{5,4},{6,7},{7,6},{8,9},{9,8},{10,11... | collective-permute-start | bytes 1572872 | tf_op jit(solution)/shard_map/ppermute | solution.py:42
  219.9 5.7 collective-permute-start.26
  221.5 20.2 %collective-permute-start.19 = (bf16[256,1024]{1,0:T(8,128)(2,1)S(1)}, bf16[256,1024]{1,0:T(8,128)(2,1)S(1)}, u32[]{:S(2)}, u32[]{:S(2)}) collective-permute-start(bf16[256,1024]{1,0:T(8,128)(2,1)S(1)} %get-tuple-element.94), channel_id=1, source_target_pairs={{0,1},{1,0},{2,3},{3,2},{4,5},{5,4},{6,7},{7,6},{8,9},{9,8},{10,11... | collective-permute-start | bytes 1572872 | tf_op jit(solution)/shard_map/ppermute | solution.py:42
  221.8 5.2 collective-permute-start.20
  225.7 14.9 %collective-permute-start.27 = (bf16[256,1024]{1,0:T(8,128)(2,1)S(1)}, bf16[256,1024]{1,0:T(8,128)(2,1)S(1)}, u32[]{:S(2)}, u32[]{:S(2)}) collective-permute-start(bf16[256,1024]{1,0:T(8,128)(2,1)S(1)} %fusion.62), channel_id=1, source_target_pairs={{0,2},{1,3},{2,0},{3,1},{4,6},{5,7},{6,4},{7,5},{8,10},{9,11},{10,... | collective-permute-start | bytes 1572872 | tf_op jit(solution)/shard_map/ppermute | solution.py:42
  227.1 23.9 %collective-permute-start.21 = (bf16[256,1024]{1,0:T(8,128)(2,1)S(1)}, bf16[256,1024]{1,0:T(8,128)(2,1)S(1)}, u32[]{:S(2)}, u32[]{:S(2)}) collective-permute-start(bf16[256,1024]{1,0:T(8,128)(2,1)S(1)} %fusion.64), channel_id=1, source_target_pairs={{0,2},{1,3},{2,0},{3,1},{4,6},{5,7},{6,4},{7,5},{8,10},{9,11},{10,... | collective-permute-start | bytes 1572872 | tf_op jit(solution)/shard_map/ppermute | solution.py:42
  272.4 137.5 %collective-permute-start.37 = (bf16[256,256]{1,0:T(8,128)(2,1)}, bf16[256,256]{1,0:T(8,128)(2,1)}, u32[]{:S(2)}, u32[]{:S(2)}) collective-permute-start(bf16[256,256]{1,0:T(8,128)(2,1)} %get-tuple-element.108), channel_id=1, source_target_pairs={{16,0},{20,4},{24,8},{28,12},{17,1},{21,5},{25,9},{29,13},{18,2},{... | collective-permute-start | bytes 393224 | tf_op jit(solution)/shard_map/ppermute | solution.py:37
  273.6 136.2 %collective-permute-start.36 = (bf16[256,256]{1,0:T(8,128)(2,1)}, bf16[256,256]{1,0:T(8,128)(2,1)}, u32[]{:S(2)}, u32[]{:S(2)}) collective-permute-start(bf16[256,256]{1,0:T(8,128)(2,1)} %get-tuple-element.109), channel_id=1, source_target_pairs={{12,0},{16,4},{20,8},{24,12},{28,16},{13,1},{17,5},{21,9},{25,13},... | collective-permute-start | bytes 393224 | tf_op jit(solution)/shard_map/ppermute | solution.py:37
  274.9 134.9 %collective-permute-start.35 = (bf16[256,256]{1,0:T(8,128)(2,1)}, bf16[256,256]{1,0:T(8,128)(2,1)}, u32[]{:S(2)}, u32[]{:S(2)}) collective-permute-start(bf16[256,256]{1,0:T(8,128)(2,1)} %get-tuple-element.110), channel_id=1, source_target_pairs={{8,0},{12,4},{16,8},{20,12},{24,16},{28,20},{9,1},{13,5},{17,9},{2... | collective-permute-start | bytes 393224 | tf_op jit(solution)/shard_map/ppermute | solution.py:37
  276.2 133.6 %collective-permute-start.34 = (bf16[256,256]{1,0:T(8,128)(2,1)}, bf16[256,256]{1,0:T(8,128)(2,1)}, u32[]{:S(2)}, u32[]{:S(2)}) collective-permute-start(bf16[256,256]{1,0:T(8,128)(2,1)} %get-tuple-element.111), channel_id=1, source_target_pairs={{4,0},{8,4},{12,8},{16,12},{20,16},{24,20},{28,24},{5,1},{9,5},{13... | collective-permute-start | bytes 393224 | tf_op jit(solution)/shard_map/ppermute | solution.py:37
  303.4 14.1 %collective-permute-start.30 = (bf16[24,64,128]{2,1,0:T(8,128)(2,1)}, bf16[24,64,128]{2,1,0:T(8,128)(2,1)S(1)}, u32[]{:S(2)}, u32[]{:S(2)}) collective-permute-start(bf16[24,64,128]{2,1,0:T(8,128)(2,1)} %get-tuple-element.154), channel_id=1, source_target_pairs={{4,0},{8,4},{12,8},{16,12},{20,16},{24,20},{28,24},{5,1},{9,5},{13... | collective-permute-start | bytes 1179656 | tf_op jit(solution)/shard_map/ppermute | solution.py:37
  318.9 14.7 %collective-permute-start.31 = (bf16[24,64,128]{2,1,0:T(8,128)(2,1)S(1)}, bf16[24,64,128]{2,1,0:T(8,128)(2,1)S(1)}, u32[]{:S(2)}, u32[]{:S(2)}) collective-permute-start(bf16[24,64,128]{2,1,0:T(8,128)(2,1)S(1)} %fusion.94), channel_id=1, source_target_pairs={{8,0},{12,4},{16,8},{20,12},{24,16},{28,20},{9,1},{13,5},{17,9},{2... | collective-permute-start | bytes 1179656 | tf_op jit(solution)/shard_map/ppermute | solution.py:37
  335.3 21.9 %collective-permute-start.32 = (bf16[24,64,128]{2,1,0:T(8,128)(2,1)}, bf16[24,64,128]{2,1,0:T(8,128)(2,1)}, u32[]{:S(2)}, u32[]{:S(2)}) collective-permute-start(bf16[24,64,128]{2,1,0:T(8,128)(2,1)} %fusion.85), channel_id=1, source_target_pairs={{16,0},{20,4},{24,8},{28,12},{17,1},{21,5},{25,9},{29,13},{18,2},{... | collective-permute-start | bytes 1179656 | tf_op jit(solution)/shard_map/ppermute | solution.py:37
  390.2 6.1 collective-permute-start.33
  406.1 16.4 %collective-permute-start.45 = (bf16[256,3352]{0,1:T(8,128)(2,1)}, bf16[256,3352]{0,1:T(8,128)(2,1)S(1)}, u32[]{:S(2)}, u32[]{:S(2)}) collective-permute-start(bf16[256,3352]{0,1:T(8,128)(2,1)} %get-tuple-element.85), channel_id=1, source_target_pairs={{0,1},{1,0},{2,3},{3,2},{4,5},{5,4},{6,7},{7,6},{8,9},{9,8},{10,11... | collective-permute-start | bytes 5148680 | tf_op jit(solution)/shard_map/ppermute | solution.py:42
  409.8 209.9 %all-reduce.19.cloned.1.call-start = ((), (), s32[]{:S(2)}) async-start(), calls=%async_computation.1 | async-start | bytes 2097152 | tf_op jit(solution)/shard_map/psum | solution.py:446
  413.7 5.7 collective-permute-start.39
  418.4 17.5 %collective-permute-start.47 = (bf16[512,1024]{1,0:T(8,128)(2,1)}, bf16[512,1024]{1,0:T(8,128)(2,1)}, u32[]{:S(2)}, u32[]{:S(2)}) collective-permute-start(bf16[512,1024]{1,0:T(8,128)(2,1)} %get-tuple-element.87), channel_id=1, source_target_pairs={{0,1},{1,0},{2,3},{3,2},{4,5},{5,4},{6,7},{7,6},{8,9},{9,8},{10,11... | collective-permute-start | bytes 3145736 | tf_op jit(solution)/shard_map/ppermute | solution.py:42
  418.9 7.2 collective-permute-start.48
  418.9 8.0 collective-permute-start.38
  420.9 12.3 %collective-permute-start.40 = (bf16[256,768]{1,0:T(8,128)(2,1)}, bf16[256,768]{1,0:T(8,128)(2,1)}, u32[]{:S(2)}, u32[]{:S(2)}) collective-permute-start(bf16[256,768]{1,0:T(8,128)(2,1)} %fusion.86), channel_id=1, source_target_pairs={{0,2},{1,3},{2,0},{3,1},{4,6},{5,7},{6,4},{7,5},{8,10},{9,11},{10,... | collective-permute-start | bytes 1179656 | tf_op jit(solution)/shard_map/ppermute | solution.py:42
  422.5 115.9 %collective-permute-start.44 = (bf16[256,3352]{0,1:T(8,128)(2,1)}, bf16[256,3352]{0,1:T(8,128)(2,1)}, u32[]{:S(2)}, u32[]{:S(2)}) collective-permute-start(bf16[256,3352]{0,1:T(8,128)(2,1)} %get-tuple-element.84), channel_id=1, source_target_pairs={{0,1},{1,0},{2,3},{3,2},{4,5},{5,4},{6,7},{7,6},{8,9},{9,8},{10,11... | collective-permute-start | bytes 5148680 | tf_op jit(solution)/shard_map/ppermute | solution.py:42
  426.1 112.4 %collective-permute-start.46 = (bf16[256,3352]{0,1:T(8,128)(2,1)}, bf16[256,3352]{0,1:T(8,128)(2,1)}, u32[]{:S(2)}, u32[]{:S(2)}) collective-permute-start(bf16[256,3352]{0,1:T(8,128)(2,1)} %fusion.8), channel_id=1, source_target_pairs={{0,2},{1,3},{2,0},{3,1},{4,6},{5,7},{6,4},{7,5},{8,10},{9,11},{10,... | collective-permute-start | bytes 5148680 | tf_op jit(solution)/shard_map/ppermute | solution.py:42
  426.9 64.4 %collective-permute-start.49 = (bf16[512,1024]{1,0:T(8,128)(2,1)S(1)}, bf16[512,1024]{1,0:T(8,128)(2,1)S(1)}, u32[]{:S(2)}, u32[]{:S(2)}) collective-permute-start(bf16[512,1024]{1,0:T(8,128)(2,1)S(1)} %fusion.25), channel_id=1, source_target_pairs={{0,2},{1,3},{2,0},{3,1},{4,6},{5,7},{6,4},{7,5},{8,10},{9,11},{10,... | collective-permute-start | bytes 3145736 | tf_op jit(solution)/shard_map/ppermute | solution.py:42
  538.3 81.7 %copy-start.16 = (f32[1,256,1024]{2,1,0:T(8,128)S(1)}, f32[1,256,1024]{2,1,0:T(8,128)}, u32[]{:S(2)}) copy-start(f32[1,256,1024]{2,1,0:T(8,128)} %param.17) | copy-start | bytes 3145732
  538.4 81.7 %copy-start.42 = (bf16[253,1792]{1,0:T(8,128)(2,1)S(1)}, bf16[253,1792]{1,0:T(8,128)(2,1)}, u32[]{:S(2)}) copy-start(bf16[253,1792]{1,0:T(8,128)(2,1)} %copy-done.41) | copy-start | bytes 2720260
  538.4 81.7 %copy-start.73 = (bf16[256,24]{1,0:T(8,128)(2,1)S(1)}, bf16[256,24]{1,0:T(8,128)(2,1)}, u32[]{:S(2)}) copy-start(bf16[256,24]{1,0:T(8,128)(2,1)} %copy-done.72) | copy-start | bytes 36868
  538.4 81.7 %copy-start.93 = (f32[1,2,4,128]{3,1,2,0:T(2,128)S(1)}, f32[1,2,4,128]{3,1,2,0:T(2,128)}, u32[]{:S(2)}) copy-start(f32[1,2,4,128]{3,1,2,0:T(2,128)} %copy-done.92) | copy-start | bytes 12292
  538.4 81.7 %copy-start.106 = (f32[256]{0:T(256)S(1)}, f32[256]{0:T(256)}, u32[]{:S(2)}) copy-start(f32[256]{0:T(256)} %copy-done.105) | copy-start | bytes 3076
  538.4 177.6 %all-reduce.21.cloned.1.call-start = ((), (), s32[]{:S(2)}) async-start(), calls=%async_computation.2 | async-start | bytes 3432448 | tf_op jit(solution)/shard_map/psum | solution.py:483
  619.7 186.1 %all-reduce.23.cloned.1.call-start = ((), (), s32[]{:S(2)}) async-start(), calls=%async_computation.3 | async-start | bytes 786432 | tf_op jit(solution)/shard_map/psum | solution.py:528
  626.9 1.2 collective-permute-start.42
  627.0 5.2 collective-permute-start.41
  628.1 4.0 collective-permute-start.43
  737.3 70.4 %copy-start.1 = (bf16[512,1024]{1,0:T(8,128)(2,1)S(1)}, bf16[512,1024]{1,0:T(8,128)(2,1)}, u32[]{:S(2)}) copy-start(bf16[512,1024]{1,0:T(8,128)(2,1)} %param.32) | copy-start | bytes 3145732
  (128 other events, 930.9 us)
Sparse Core Ops, SparseCore 0:
  9.6 68.6 all-gather.3
  80.4 34.7 all-gather.5
  409.9 128.3 all-reduce.24
  542.3 77.3 all-reduce.18
  623.7 92.2 all-reduce.20
  736.8 68.9 all-reduce.22

commit v2 on v1

--- a/solution.py
+++ b/solution.py
@@ -75,6 +75,25 @@
     ]
 
 
+def all_sum(array, axis, turn=0):
+    mine = lax.axis_index(axis)
+    bits = [1 << k for k in range((lax.axis_size(axis) - 1).bit_length())]
+    bits = bits[turn:] + bits[:turn]
+    for bit in bits:
+        high = (mine & bit) != 0
+        low_half, high_half = jnp.split(array, 2, axis=0)
+        got = swap(jnp.where(high, low_half, high_half).astype(BF), axis, bit)
+        array = jnp.where(high, high_half, low_half).astype(F32) + got.astype(F32)
+    array = array.astype(BF)
+    for bit in reversed(bits):
+        high = (mine & bit) != 0
+        got = swap(array, axis, bit)
+        array = jnp.where(
+            high, jnp.concatenate([got, array], axis=0), jnp.concatenate([array, got], axis=0)
+        )
+    return array
+
+
 def carried(state, decay, axis, direction):
     count = lax.axis_size(axis)
     own_state, own_decay = (state, decay)
@@ -83,9 +102,9 @@
     while step < count:
         got_state = shift(own_state.astype(BF), axis, direction * step).astype(F32)
         got_decay = shift(own_decay, axis, direction * step)
-        out_state = out_decay[:, None, None] * got_state + out_state
+        out_state = jnp.repeat(out_decay, MHEAD)[:, None] * got_state + out_state
         out_decay = out_decay * got_decay
-        own_state = own_decay[:, None, None] * got_state + own_state
+        own_state = jnp.repeat(own_decay, MHEAD)[:, None] * got_state + own_state
         own_decay = own_decay * got_decay
         step *= 2
     return out_state
@@ -105,44 +124,6 @@
     inner = jnp.mean(scaled * values, axis=-1, keepdims=True)
     back = inverse * scaled - values * inverse**3 * inner
     return (back, jnp.sum(upstream * values * inverse, axis=0))
-
-
-def mixer_inputs(window, step_raw, taps, step_bias, decay_log):
-    span = step_raw.shape[0]
-    convolved = taps[0] * window[0:span]
-    for tap in range(1, taps.shape[0]):
-        convolved = convolved + taps[tap] * window[tap : tap + span]
-    activated = jax.nn.silu(convolved)
-    inner = activated[:, :DIN].reshape(span, MHEADS, MHEAD)
-    basis = activated[:, DIN : DIN + STATE]
-    reader = activated[:, DIN + STATE :]
-    step = jax.nn.softplus(step_raw + step_bias)
-    logdecay = -step * jnp.exp(decay_log)
-    return (inner, basis, reader, step, logdecay)
-
-
-def block_states(inner, basis, step, logdecay):
-    cumulative = jnp.cumsum(logdecay, axis=0)
-    weight = jnp.exp(cumulative[-1][None, :] - cumulative) * step
-    state = jnp.einsum("thp,tn->hpn", inner * weight[:, :, None], basis, precision=HIGH)
-    return (state, jnp.exp(cumulative[-1]))
-
-
-def block_outputs(inner, basis, reader, step, logdecay, incoming, gate_z, skip):
-    span = step.shape[0]
-    cumulative = jnp.cumsum(logdecay, axis=0)
-    intersection = jnp.dot(reader, basis.T, precision=HIGH)
-    order = jnp.arange(span, dtype=jnp.int32)
-    causal = (order[:, None] >= order[None, :])[:, :, None]
-    gap = cumulative[:, None, :] - cumulative[None, :, :]
-    decay = jnp.where(causal, jnp.exp(jnp.where(causal, gap, 0.0)), 0.0)
-    mixing = intersection[:, :, None] * decay * step[None, :, :]
-    within = jnp.einsum("tsh,shp->thp", mixing, inner, precision=HIGH)
-    carried = jnp.exp(cumulative)[:, :, None] * jnp.einsum(
-        "tn,hpn->thp", reader, incoming, precision=HIGH
-    )
-    output = within + carried + skip[None, :, None] * inner
-    return output.reshape(span, -1) * jax.nn.silu(gate_z)
 
 
 def feed_forward(rows, gate_w, up_w):
@@ -316,6 +297,449 @@
     out_ref[:, KVDIM:] = vals.astype(BF)
 
 
+def sigmoid(value):
+    return 1.0 / (1.0 + jnp.exp(-value))
+
+
+def pick(array, lane):
+    lanes = lax.broadcasted_iota(jnp.int32, array.shape, 1)
+    return jnp.sum(jnp.where(lanes == lane, array, 0.0), axis=1, keepdims=True)
+
+
+def spread(pair, rows):
+    lanes = lax.broadcasted_iota(jnp.int32, (rows, 128), 1)
+    return jnp.where(lanes < MHEAD, pair[0], pair[1])
+
+
+def halves(value):
+    return [jnp.sum(value[:, h * MHEAD : (h + 1) * MHEAD], axis=1, keepdims=True) for h in range(2)]
+
+
+def triangle(rows, lower):
+    row = lax.broadcasted_iota(jnp.int32, (rows, rows), 0)
+    col = lax.broadcasted_iota(jnp.int32, (rows, rows), 1)
+    return row >= col if lower else row <= col
+
+
+def exact(left, right, dims):
+    return lax.dot_general(left, right, ((dims[0], dims[1]), ((), ())), precision=HIGH, preferred_element_type=F32)
+
+
+def prep_kernel(raw_ref, bias_ref, rate_ref, step_ref, cum_ref, cum_rows_ref):
+    rows = raw_ref.shape[0]
+    value = raw_ref[...] + bias_ref[...]
+    step = jnp.maximum(value, 0.0) + jnp.log1p(jnp.exp(-jnp.abs(value)))
+    logdecay = -step * jnp.exp(rate_ref[...])
+    step_ref[...] = step
+    cum_ref[...] = exact(triangle(rows, True).astype(F32), logdecay, ((1,), (0,)))
+    cum_rows_ref[...] = exact(logdecay, triangle(rows, False).astype(F32), ((0,), (0,)))
+
+
+def shifted_rows(mixed_ref, edge_ref):
+    rows = mixed_ref.shape[0]
+    full = jnp.concatenate([edge_ref[...].astype(F32), mixed_ref[...].astype(BF).astype(F32)], axis=0)
+    first = edge_ref.shape[0] - CONV + 1
+    return [full[first + k : first + k + rows] for k in range(CONV)]
+
+
+def convolve(views, taps_ref):
+    total = taps_ref[0:1, :] * views[0]
+    for k in range(1, CONV):
+        total = total + taps_ref[k : k + 1, :] * views[k]
+    return total
+
+
+def conv_kernel(mixed_ref, edge_ref, taps_ref, act_ref):
+    value = convolve(shifted_rows(mixed_ref, edge_ref), taps_ref)
+    act_ref[...] = value * sigmoid(value)
+
+
+def decay_matrix(cum, cum_rows_ref, head):
+    rows = cum.shape[0]
+    causal = triangle(rows, True)
+    gap = pick(cum, head) - cum_rows_ref[pl.ds(head, 1), :]
+    return jnp.where(causal, jnp.exp(jnp.where(causal, gap, 0.0)), 0.0)
+
+
+def scan_kernel(x_ref, b_ref, c_ref, step_ref, cum_ref, cum_rows_ref, skip_ref, y_ref, state_ref, mix_ref):
+    pair = pl.program_id(0)
+    rows = x_ref.shape[0]
+    basis = b_ref[...].astype(BF)
+
+    @pl.when(pair == 0)
+    def _():
+        mix_ref[...] = nt(c_ref[...].astype(BF), basis)
+
+    cum, step = (cum_ref[...], step_ref[...])
+    inner = x_ref[...]
+    steps = [pick(step, 2 * pair + h) for h in range(2)]
+    cums = [pick(cum, 2 * pair + h) for h in range(2)]
+    last = cum_ref[rows - 1 : rows, :]
+    lasts = [pick(last, 2 * pair + h) for h in range(2)]
+    scaled = inner * spread(steps, rows)
+    scaled_b = scaled.astype(BF)
+    weighted = scaled * spread([jnp.exp(lasts[h] - cums[h]) for h in range(2)], rows)
+    state_ref[...] = tn(weighted.astype(BF), basis)
+    parts = []
+    for h in range(2):
+        mixing = mix_ref[...] * decay_matrix(cum, cum_rows_ref, 2 * pair + h)
+        parts.append(nn(mixing.astype(BF), scaled_b[:, h * MHEAD : (h + 1) * MHEAD]))
+    y_ref[...] = jnp.concatenate(parts, axis=1) + skip_ref[...] * inner
+
+
+def finish_kernel(y_ref, z_ref, c_ref, cum_ref, in_ref, gain_ref, out_y_ref, out_ref, inverse_ref):
+    rows = y_ref.shape[0]
+    reader = c_ref[...].astype(BF)
+    growth = jnp.exp(cum_ref[...])
+    square = jnp.zeros((rows, 1), F32)
+    pairs = y_ref.shape[1] // 128
+    for j in range(pairs):
+        cols = slice(j * 128, (j + 1) * 128)
+        carry = nt(reader, in_ref[cols, :].astype(BF))
+        grow = spread([growth[:, 2 * j + h : 2 * j + h + 1] for h in range(2)], rows)
+        total = y_ref[:, cols] + grow * carry
+        out_y_ref[:, cols] = total
+        gate = z_ref[:, cols]
+        gated = total * (gate * sigmoid(gate))
+        square = square + jnp.sum(gated * gated, axis=1, keepdims=True)
+    inverse = lax.rsqrt(square / y_ref.shape[1] + EPS)
+    inverse_ref[...] = inverse
+    for j in range(pairs):
+        cols = slice(j * 128, (j + 1) * 128)
+        gate = z_ref[:, cols]
+        gated = out_y_ref[:, cols] * (gate * sigmoid(gate))
+        out_ref[:, cols] = (gated * inverse * gain_ref[:, cols]).astype(BF)
+
+
+def gate_back_kernel(up_ref, y_ref, z_ref, c_ref, cum_ref, gain_ref, inverse_ref, dy_ref, dz_ref, din_ref, dgain_ref):
+    rows = y_ref.shape[0]
+    reader = c_ref[...].astype(BF)
+    growth = jnp.exp(cum_ref[...])
+    inverse = inverse_ref[...]
+    pairs = y_ref.shape[1] // 128
+    inside = jnp.zeros((rows, 1), F32)
+    for j in range(pairs):
+        cols = slice(j * 128, (j + 1) * 128)
+        gate = z_ref[:, cols]
+        gated = y_ref[:, cols] * (gate * sigmoid(gate))
+        product = up_ref[:, cols] * gated
+        dgain_ref[:, cols] = jnp.sum(product * inverse, axis=0, keepdims=True)
+        inside = inside + jnp.sum(product * gain_ref[:, cols], axis=1, keepdims=True)
+    factor = inverse * inverse * inverse * (inside / y_ref.shape[1])
+    for j in range(pairs):
+        cols = slice(j * 128, (j + 1) * 128)
+        gate = z_ref[:, cols]
+        sigma = sigmoid(gate)
+        scan = y_ref[:, cols]
+        back = inverse * gain_ref[:, cols] * up_ref[:, cols] - scan * (gate * sigma) * factor
+        dy = back * (gate * sigma)
+        dy_ref[:, cols] = dy
+        dz_ref[:, cols] = (back * scan * sigma * (1.0 + gate * (1.0 - sigma))).astype(BF)
+        grow = spread([growth[:, 2 * j + h : 2 * j + h + 1] for h in range(2)], rows)
+        din_ref[cols, :] = tn((dy * grow).astype(BF), reader)
+
+
+def scan_back_kernel(
+    x_ref, b_ref, c_ref, step_ref, cum_ref, cum_rows_ref, skip_ref, y_ref, dy_ref, in_ref,
+    dx_ref, dbc_ref, dstep_ref, dcum_ref, dskip_ref, mix_ref, dmix_ref, dc_ref,
+):
+    pair = pl.program_id(0)
+    rows = x_ref.shape[0]
+
+    @pl.when(pair == 0)
+    def _():
+        mix_ref[...] = nt(c_ref[...].astype(BF), b_ref[...].astype(BF))
+        dmix_ref[...] = jnp.zeros(dmix_ref.shape, F32)
+        dc_ref[...] = jnp.zeros(dc_ref.shape, F32)
+        dstep_ref[...] = jnp.zeros(dstep_ref.shape, F32)
+        dcum_ref[...] = jnp.zeros(dcum_ref.shape, F32)
+
+    cum, step = (cum_ref[...], step_ref[...])
+    inner, dy, skip = (x_ref[...], dy_ref[...], skip_ref[...])
+    steps = spread([pick(step, 2 * pair + h) for h in range(2)], rows)
+    grow = spread([jnp.exp(pick(cum, 2 * pair + h)) for h in range(2)], rows)
+    scaled_b, dy_b = ((inner * steps).astype(BF), dy.astype(BF))
+    dc_ref[...] += nn((dy * grow).astype(BF), in_ref[...].astype(BF))
+    parts = []
+    for h in range(2):
+        lanes = slice(h * MHEAD, (h + 1) * MHEAD)
+        decay = decay_matrix(cum, cum_rows_ref, 2 * pair + h)
+        parts.append(tn((mix_ref[...] * decay).astype(BF), dy_b[:, lanes]))
+        dmix_ref[...] += nt(dy_b[:, lanes], scaled_b[:, lanes]) * decay
+    back = jnp.concatenate(parts, axis=1)
+    dx_ref[...] = back * steps + skip * dy
+    dsteps = halves(back * inner)
+    stays = halves(dy * (y_ref[...] - skip * inner))
+    lane = lax.broadcasted_iota(jnp.int32, dstep_ref.shape, 1)
+    for h in range(2):
+        here = lane == 2 * pair + h
+        column = pick(step, 2 * pair + h)
+        dstep_ref[...] += jnp.where(here, dsteps[h], 0.0)
+        dcum_ref[...] += jnp.where(here, stays[h] - column * dsteps[h], 0.0)
+    dskip_ref[...] = jnp.sum(dy * inner, axis=0, keepdims=True)
+
+    @pl.when(pair == pl.num_programs(0) - 1)
+    def _():
+        dmix = dmix_ref[...].astype(BF)
+        dbc_ref[:, :STATE] = tn(dmix, c_ref[...].astype(BF))
+        dbc_ref[:, STATE:] = dc_ref[...] + nn(dmix, b_ref[...].astype(BF))
+
+
+def conv_back_kernel(
+    mixed_ref, edge_ref, taps_ref, x_ref, b_ref, dx_ref, dbc_ref, dstate_ref, in_ref, step_ref, cum_ref,
+    dstep_in_ref, dcum_in_ref,
+    dconv_ref, head_ref, dtaps_ref, dstep_ref, dcum_ref, dact_ref, db_ref,
+):
+    block = pl.program_id(0)
+    rows = x_ref.shape[0]
+    pairs = pl.num_programs(0) - 2
+
+    @pl.when(block == 0)
+    def _():
+        db_ref[...] = dbc_ref[:, :STATE]
+        dstep_ref[...] = dstep_in_ref[...]
+        dcum_ref[...] = dcum_in_ref[...]
+
+    @pl.when(block < pairs)
+    def _():
+        cum, step = (cum_ref[...], step_ref[...])
+        inner = x_ref[...]
+        last = cum_ref[rows - 1 : rows, :]
+        lane = lax.broadcasted_iota(jnp.int32, step.shape, 1)
+        row = lax.broadcasted_iota(jnp.int32, step.shape, 0)
+        fades = [jnp.exp(pick(last, 2 * block + h) - pick(cum, 2 * block + h)) for h in range(2)]
+        steps = [pick(step, 2 * block + h) for h in range(2)]
+        weight = spread([fades[h] * steps[h] for h in range(2)], rows)
+        dstate = dstate_ref[...]
+        dstate_b = dstate.astype(BF)
+        back = nt(b_ref[...].astype(BF), dstate_b)
+        db_ref[...] += nn((inner * weight).astype(BF), dstate_b)
+        dact_ref[...] = dx_ref[...] + weight * back
+        dweights = halves(inner * back)
+        passed = dstate * in_ref[...]
+        for h in range(2):
+            here = lane == 2 * block + h
+            moved = fades[h] * steps[h] * dweights[h]
+            decay = jnp.exp(pick(last, 2 * block + h))
+            lanes = slice(h * MHEAD, (h + 1) * MHEAD)
+            end = jnp.sum(moved) + jnp.sum(passed[lanes, :]) * decay
+            dstep_ref[...] += jnp.where(here, fades[h] * dweights[h], 0.0)
+            dcum_ref[...] += jnp.where(here, jnp.where(row == rows - 1, end, 0.0) - moved, 0.0)
+
+    @pl.when(block == pairs)
+    def _():
+        dact_ref[...] = db_ref[...]
+
+    @pl.when(block == pairs + 1)
+    def _():
+        dact_ref[...] = dbc_ref[:, STATE:]
+
+    views = shifted_rows(mixed_ref, edge_ref)
+    value = convolve(views, taps_ref)
+    sigma = sigmoid(value)
+    dvalue = dact_ref[...] * sigma * (1.0 + value * (1.0 - sigma))
+    for k in range(CONV):
+        dtaps_ref[k : k + 1, :] = jnp.sum(dvalue * views[k], axis=0, keepdims=True)
+    pad = head_ref.shape[0]
+    padding = jnp.zeros((pad, 128), F32)
+    padded = jnp.concatenate([padding, dvalue, padding], axis=0)
+    total = None
+    for k in range(CONV):
+        term = taps_ref[k : k + 1, :] * padded[CONV - 1 - k : CONV - 1 - k + rows + pad]
+        total = term if total is None else total + term
+    head_ref[...] = total[:pad]
+    dconv_ref[...] = total[pad:]
+
+
+def step_back_kernel(raw_ref, bias_ref, rate_ref, step_ref, dstep_ref, dcum_ref, draw_ref, dbias_ref, drate_ref):
+    rows = raw_ref.shape[0]
+    rate = jnp.exp(rate_ref[...])
+    dlog = exact(triangle(rows, False).astype(F32), dcum_ref[...], ((1,), (0,)))
+    draw = (dstep_ref[...] - dlog * rate) * sigmoid(raw_ref[...] + bias_ref[...])
+    draw_ref[...] = draw
+    dbias_ref[...] = jnp.sum(draw, axis=0, keepdims=True)
+    drate_ref[...] = jnp.sum(-dlog * step_ref[...] * rate, axis=0, keepdims=True)
+
+
+def whole(shape):
+    return pl.BlockSpec(shape, lambda j: (0,) * len(shape))
+
+
+def columns(rows, first=0):
+    return pl.BlockSpec((rows, 128), lambda j: (0, first + j))
+
+
+def fixed(rows, index):
+    return pl.BlockSpec((rows, 128), lambda j: (0, index))
+
+
+PAIRS = DIN // 128
+BLOCKS = XBC // 128
+
+
+def struct(*shape, dtype=F32):
+    return jax.ShapeDtypeStruct(shape, dtype)
+
+
+def mamba_prep(raw, bias, rate):
+    rows = raw.shape[0]
+    return pl.pallas_call(
+        prep_kernel,
+        out_shape=[struct(rows, MHEADS), struct(rows, MHEADS), struct(MHEADS, rows)],
+        name="prep",
+    )(raw, bias, rate)
+
+
+def mamba_conv(mixed, edge, taps):
+    rows = mixed.shape[0]
+    return pl.pallas_call(
+        conv_kernel,
+        grid=(BLOCKS,),
+        in_specs=[columns(rows, PAIRS), columns(edge.shape[0]), columns(CONV)],
+        out_specs=columns(rows),
+        out_shape=struct(rows, XBC),
+        name="conv",
+    )(mixed, edge, taps)
+
+
+def mamba_scan(act, step, cum, cum_rows, skip):
+    rows = act.shape[0]
+    return pl.pallas_call(
+        scan_kernel,
+        grid=(PAIRS,),
+        in_specs=[
+            columns(rows),
+            fixed(rows, PAIRS),
+            fixed(rows, PAIRS + 1),
+            whole(step.shape),
+            whole(cum.shape),
+            whole(cum_rows.shape),
+            columns(1),
+        ],
+        out_specs=[columns(rows), pl.BlockSpec((128, STATE), lambda j: (j, 0))],
+        out_shape=[struct(rows, DIN), struct(DIN, STATE)],
+        scratch_shapes=[pltpu.VMEM((rows, rows), F32)],
+        name="scan",
+    )(act, act, act, step, cum, cum_rows, skip)
+
+
+def mamba_finish(y_local, mixed, act, cum, incoming, gain):
+    rows = act.shape[0]
+    return pl.pallas_call(
+        finish_kernel,
+        grid=(1,),
+        in_specs=[
+            whole(y_local.shape),
+            whole((rows, DIN)),
+            fixed(rows, PAIRS + 1),
+            whole(cum.shape),
+            whole(incoming.shape),
+            whole(gain.shape),
+        ],
+        out_specs=[whole((rows, DIN)), whole((rows, DIN)), whole((rows, 1))],
+        out_shape=[struct(rows, DIN), struct(rows, DIN, dtype=BF), struct(rows, 1)],
+        name="finish",
+    )(y_local, mixed, act, cum, incoming, gain)
+
+
+def mamba_gate_back(grad, y, mixed, act, cum, gain, inverse):
+    rows = act.shape[0]
+    return pl.pallas_call(
+        gate_back_kernel,
+        grid=(1,),
+        in_specs=[
+            whole((rows, DIN)),
+            whole((rows, DIN)),
+            whole((rows, DIN)),
+            fixed(rows, PAIRS + 1),
+            whole(cum.shape),
+            whole(gain.shape),
+            whole((rows, 1)),
+        ],
+        out_specs=[whole((rows, DIN)), whole((rows, DIN)), whole((DIN, STATE)), whole((1, DIN))],
+        out_shape=[struct(rows, DIN), struct(rows, DIN, dtype=BF), struct(DIN, STATE), struct(1, DIN)],
+        name="gate_back",
+    )(grad, y, mixed, act, cum, gain, inverse)
+
+
+def mamba_scan_back(act, step, cum, cum_rows, skip, y, dy, incoming):
+    rows = act.shape[0]
+    return pl.pallas_call(
+        scan_back_kernel,
+        grid=(PAIRS,),
+        in_specs=[
+            columns(rows),
+            fixed(rows, PAIRS),
+            fixed(rows, PAIRS + 1),
+            whole(step.shape),
+            whole(cum.shape),
+            whole(cum_rows.shape),
+            columns(1),
+            columns(rows),
+            columns(rows),
+            pl.BlockSpec((128, STATE), lambda j: (j, 0)),
+        ],
+        out_specs=[columns(rows), whole((rows, 2 * STATE)), whole(step.shape), whole(step.shape), columns(1)],
+        out_shape=[
+            struct(rows, DIN),
+            struct(rows, 2 * STATE),
+            struct(*step.shape),
+            struct(*step.shape),
+            struct(1, DIN),
+        ],
+        scratch_shapes=[
+            pltpu.VMEM((rows, rows), F32),
+            pltpu.VMEM((rows, rows), F32),
+            pltpu.VMEM((rows, STATE), F32),
+        ],
+        name="scan_back",
+    )(act, act, act, step, cum, cum_rows, skip, y, dy, incoming)
+
+
+def mamba_conv_back(mixed, edge, taps, act, dx, dbc, dstate, incoming, step, cum, dstep, dcum):
+    rows = act.shape[0]
+    pad = edge.shape[0]
+    clipped = pl.BlockSpec((rows, 128), lambda j: (0, jnp.minimum(j, PAIRS - 1)))
+    states = pl.BlockSpec((128, STATE), lambda j: (jnp.minimum(j, PAIRS - 1), 0))
+    return pl.pallas_call(
+        conv_back_kernel,
+        grid=(BLOCKS,),
+        in_specs=[
+            columns(rows, PAIRS),
+            columns(pad),
+            columns(CONV),
+            clipped,
+            fixed(rows, PAIRS),
+            clipped,
+            whole(dbc.shape),
+            states,
+            states,
+            whole(step.shape),
+            whole(step.shape),
+            whole(step.shape),
+            whole(step.shape),
+        ],
+        out_specs=[columns(rows), columns(pad), columns(CONV), whole(step.shape), whole(step.shape)],
+        out_shape=[
+            struct(rows, XBC),
+            struct(pad, XBC),
+            struct(CONV, XBC),
+            struct(*step.shape),
+            struct(*step.shape),
+        ],
+        scratch_shapes=[pltpu.VMEM((rows, 128), F32), pltpu.VMEM((rows, STATE), F32)],
+        name="conv_back",
+    )(mixed, edge, taps, act, act, dx, dbc, dstate, incoming, step, cum, dstep, dcum)
+
+
+def mamba_step_back(raw, bias, rate, step, dstep, dcum):
+    return pl.pallas_call(
+        step_back_kernel,
+        out_shape=[struct(*raw.shape), struct(1, MHEADS), struct(1, MHEADS)],
+        name="step_back",
+    )(raw, bias, rate, step, dstep, dcum)
+
+
 def body(
     hidden_in,
     positions,
@@ -389,27 +813,27 @@
         [shift(kv_own, "ctx", k) for k in range(reach, 0, -1)] + [kv_own], axis=0
     )
     pos_column = token_pos[:, None]
+    upstream_all = jnp.concatenate(xor_gather(upstream.astype(BF), "fsdp"), axis=0)
+    mixer_b, window, upstream_all = lax.optimization_barrier((normed_b, window, upstream_all))
+    mixed = matmul(mixer_b, mamba_proj)
     attended, log_total = attend(query, window, pos_column)
     attend_branch = matmul(attended, attend_out)
-    mixed = matmul(normed_b, mamba_proj)
-    gate_z = mixed[:, :DIN]
-    conv_in = mixed[:, DIN : DIN + XBC].astype(BF)
-    step_raw = mixed[:, DIN + XBC :]
-    edge = shift(conv_in[length - CONV + 1 :], "ctx", 1)
-    conv_window = jnp.concatenate([edge, lax.optimization_barrier(conv_in)], axis=0).astype(F32)
-    prepared, prepare_back = jax.vjp(mixer_inputs, conv_window, step_raw, taps_f, bias_f, rate_f)
-    inner, basis, reader, step, logdecay = prepared
-    (local_state, decay), states_back = jax.vjp(block_states, inner, basis, step, logdecay)
+    raw = mixed[:, DIN + XBC :]
+    last_rows = mixed[length - 8 :, DIN : DIN + XBC].astype(BF)
+    edge = shift(last_rows, "ctx", 1)
+    bias_row, rate_row, gated_row = (bias_f[None], rate_f[None], gated_f[None])
+    skip_row = jnp.repeat(skip_f, MHEAD)[None]
+    step, cum, cum_rows = mamba_prep(raw, bias_row, rate_row)
+    decay = jnp.exp(cum[length - 1])
+    act = mamba_conv(mixed, edge, taps_f)
+    y_local, local_state = mamba_scan(act, step, cum, cum_rows, skip_row)
     incoming = carried(local_state, decay, "ctx", 1)
-    gated, outputs_back = jax.vjp(
-        block_outputs, inner, basis, reader, step, logdecay, incoming, gate_z, skip_f
-    )
-    mamba_normed, inverse_three = rms_forward(gated, gated_f)
-    mamba_normed_b = mamba_normed.astype(BF)
+    scan_out, mamba_normed_b, inverse_three = mamba_finish(
+        y_local, mixed, act, cum, incoming, gated_row
+    )
     middle = tokens + attend_branch + matmul(mamba_normed_b, mamba_back_w)
     feed_normed, inverse_two = rms_forward(middle, feed_f)
     feed_b = feed_normed.astype(BF)
-    upstream_all = jnp.concatenate(xor_gather(upstream.astype(BF), "fsdp"), axis=0)
     rows_all = jnp.concatenate(xor_gather(feed_b, "fsdp"), axis=0)
 
     gate, up, activated = feed_forward(rows_all, gate_weight, up_weight)
@@ -418,17 +842,16 @@
     gate_part = (act_grad * up * sigma * (1.0 + gate * (1.0 - sigma))).astype(BF)
     up_part = (act_grad * gate * sigma).astype(BF)
     feed_back = matmul(gate_part, gate_weight.T) + matmul(up_part, up_weight.T)
+    feed_grads = (
+        matmul(rows_all.T, gate_part).astype(BF),
+        matmul(rows_all.T, up_part).astype(BF),
+        matmul(activated.T, upstream_all).astype(BF),
+    )
+    feed_totals = lax.psum(feed_grads, "ctx")
     feed_grad = xor_scatter(jnp.split(feed_back, group, axis=0), "fsdp")
+    feed_grad, feed_grads = lax.optimization_barrier((feed_grad, feed_grads))
     feed_out = xor_scatter(jnp.split(matmul(activated, down_weight), group, axis=0), "fsdp")
     output = middle + feed_out
-    feed_totals = lax.psum(
-        (
-            matmul(rows_all.T, gate_part).astype(BF),
-            matmul(rows_all.T, up_part).astype(BF),
-            matmul(activated.T, upstream_all).astype(BF),
-        ),
-        "ctx",
-    )
 
     back_two, feed_gain_grad = rms_backward(middle, inverse_two, feed_f, feed_grad)
     middle_grad = upstream + back_two
@@ -442,45 +865,34 @@
         axis=1,
     )
     out_grads = xor_scatter(jnp.split(matmul(out_columns.T, middle_b), group, axis=0), "fsdp")
-    out_grads, feed_totals = lax.optimization_barrier((out_grads.astype(BF), feed_totals))
-    out_totals = lax.psum(out_grads, "ctx")
+    out_totals = all_sum(out_grads, "ctx")
 
     normed_mamba_grad = matmul(middle_b, mamba_back_w.T)
-    gated_grad, gated_gain_grad = rms_backward(gated, inverse_three, gated_f, normed_mamba_grad)
-    (
-        grad_inner,
-        grad_basis,
-        grad_reader,
-        grad_step,
-        grad_logdecay,
-        grad_incoming,
-        grad_gate_z,
-        skip_grad,
-    ) = outputs_back(gated_grad)
+    dy, gate_z_grad, grad_incoming, gated_gain_grad = mamba_gate_back(
+        normed_mamba_grad, scan_out, mixed, act, cum, gated_row, inverse_three
+    )
+    normed_columns = jnp.concatenate(column_blocks(normed_b, "fsdp"), axis=1)
+
+    def input_weight_grad(grad):
+        return jnp.split(matmul(normed_columns.T, grad), group, axis=0)
+
+    gate_columns = all_sum(xor_scatter(input_weight_grad(gate_z_grad), "fsdp"), "ctx", 1)
     state_grad = carried(grad_incoming, decay, "ctx", -1)
-    decay_grad = jnp.sum(state_grad * incoming, axis=(1, 2))
-    more_inner, more_basis, more_step, more_logdecay = states_back((state_grad, decay_grad))
-    window_grad, raw_grad, taps_grad, bias_grad, rate_grad = prepare_back(
-        (
-            grad_inner + more_inner,
-            grad_basis + more_basis,
-            grad_reader,
-            grad_step + more_step,
-            grad_logdecay + more_logdecay,
-        )
-    )
-    returned = shift(window_grad[: CONV - 1], "ctx", -1)
-    conv_grad = window_grad[CONV - 1 :]
+    dx, dbc, dstep, dcum, dskip = mamba_scan_back(
+        act, step, cum, cum_rows, skip_row, scan_out, dy, incoming
+    )
+    conv_grad, head_rows, taps_grad, dstep, dcum = mamba_conv_back(
+        mixed, edge, taps_f, act, dx, dbc, state_grad, incoming, step, cum, dstep, dcum
+    )
+    raw_grad, bias_grad, rate_grad = mamba_step_back(raw, bias_row, rate_row, step, dstep, dcum)
+    skip_grad = jnp.sum(dskip.reshape(MHEADS, MHEAD), axis=1)
+    returned = shift(head_rows, "ctx", -1)
     conv_grad = jnp.concatenate(
-        [conv_grad[: length - CONV + 1], conv_grad[length - CONV + 1 :] + returned], axis=0
-    )
-    mixed_grad = jnp.concatenate([grad_gate_z, conv_grad, raw_grad], axis=1).astype(BF)
-    normed_columns = jnp.concatenate(column_blocks(normed_b, "fsdp"), axis=1)
-    mamba_in_grad = xor_scatter(
-        jnp.split(matmul(normed_columns.T, mixed_grad), group, axis=0), "fsdp"
-    )
-    mamba_in_grad, out_totals = lax.optimization_barrier((mamba_in_grad.astype(BF), out_totals))
-    mamba_in_total = lax.psum(mamba_in_grad, "ctx")
+        [conv_grad[: length - 8], conv_grad[length - 8 :] + returned], axis=0
+    )
+    rest_grad = jnp.concatenate([conv_grad.astype(BF), raw_grad.astype(BF)], axis=1)
+    rest_columns = all_sum(xor_scatter(input_weight_grad(rest_grad), "fsdp"), "ctx")
+    mixed_grad = jnp.concatenate([gate_z_grad, rest_grad], axis=1)
     normed_grad = matmul(mixed_grad, mamba_proj.T)
 
     attended_grad = matmul(middle_b, attend_out.T).astype(BF)
@@ -499,9 +911,6 @@
         sine,
     )
     projected_grad = jnp.concatenate([query_grad, kv_grad], axis=1)
-    attend_in_grad = xor_scatter(
-        jnp.split(matmul(normed_columns.T, projected_grad), group, axis=0), "fsdp"
-    )
     normed_grad = normed_grad + matmul(projected_grad, attend_in.T)
     back_one, mixer_gain_grad = rms_backward(tokens, inverse_one, mixer_f, normed_grad)
     input_grad = middle_grad + back_one
@@ -519,13 +928,26 @@
         axis=1,
     )
     mine = lax.axis_index("fsdp")
-    small_own = xor_scatter(
-        [lax.dynamic_index_in_dim(small_grads, mine ^ d, 0, False) for d in range(group)], "fsdp"
-    )
-    last, mamba_in_total = lax.optimization_barrier(
-        ((attend_in_grad.astype(BF), small_own.astype(BF)), mamba_in_total)
-    )
-    attend_in_total, small_total = lax.psum(last, "ctx")
+    width = projected_grad.shape[1]
+    spare = -(-small_grads.shape[1] // (ctx_count * width)) * ctx_count
+    small_grads = jnp.pad(
+        small_grads, ((0, 0), (0, spare * width - small_grads.shape[1]))
+    ).reshape(group, spare, width)
+    last = all_sum(
+        xor_scatter(
+            [
+                jnp.concatenate(
+                    [part, lax.dynamic_index_in_dim(small_grads, mine ^ d, 0, False)], axis=0
+                )
+                for d, part in enumerate(input_weight_grad(projected_grad))
+            ],
+            "fsdp",
+        ),
+        "ctx",
+        1,
+    )
+    attend_in_total, small_total = (last[: attention_in.shape[0]], last[attention_in.shape[0] :])
+    small_total = small_total.reshape(-1)
     total_mixer, total_feed, total_gated, total_taps, total_bias, total_rate, total_skip = (
         small_total[bounds[k] : bounds[k + 1]].astype(F32) for k in range(len(sizes))
     )
@@ -535,7 +957,7 @@
         total_mixer,
         attend_in_total.astype(F32),
         out_totals[:attend_rows].astype(F32),
-        mamba_in_total.astype(F32),
+        jnp.concatenate([gate_columns, rest_columns], axis=1).astype(F32),
         total_taps.reshape(CONV, -1),
         total_bias,
         total_rate,

time: 826 us -> 641 us (0.78)
  waiting for transfers between devices: 403 us -> 213 us
  Pallas kernels: 25.1 us -> 97.4 us
  matrix products: 113 us -> 61.7 us
  starting transfers between devices: 75.1 us -> 98.8 us
  blocking collectives: 20 us -> 0 us
  other arithmetic: 90 us -> 78.9 us
    psum x4 -> x1, waiting for transfers between devices: 261 us -> 0.02 us  [body(): feed_totals = lax.psum(feed_grads, 'ctx')]
    pallas_call x0 -> x8, Pallas kernels: none -> 72.2 us  [the longest x1 20.2 us: mamba_scan_back(): pl.pallas_call(scan_back_kernel, grid=(PAIRS,), in_specs=[columns(rows),...]
    ppermute x30 -> x54, waiting for transfers between devices: 83.3 us -> 150 us  [swap(): lax.ppermute(value, axis, [(source, source ^ bit) for source in range(cou...]
    dot_general x12 -> x0, matrix products: 57.6 us -> none  [the longest x3 29.1 us: block_outputs(): within = jnp.einsum('tsh,shp->thp', mixing, inner, precision=HIGH)]
    ppermute x20, waiting for transfers between devices: 26.1 us -> 54.2 us  [shift(): lax.ppermute(value, axis, [(source, source + steps) for source in range(f...]
    ppermute x30 -> x54, starting transfers between devices: 17.3 us -> 43.4 us  [swap(): lax.ppermute(value, axis, [(source, source ^ bit) for source in range(cou...]
    all_gather x1, waiting for transfers between devices: 32.6 us -> 8.04 us  [body(): mamba_proj = lax.all_gather(mamba_in, 'fsdp', axis=0, tiled=True)]
    psum x1 -> x0, blocking collectives: 20 us -> none  [body(): attend_in_total, small_total = lax.psum(last, 'ctx')]
  transfers between devices with their start and end apart: 56 -> 77, of which waited for: 18 -> 31; matrix products, arithmetic and copies ran while one was open for 31% -> 27% of each run, Pallas kernels for 2% -> 15%
where the time goes in v2:
time: 641 us; the launch traced here: 631 us
  waiting for transfers between devices  213 us (33%)
  starting transfers between devices  98.8 us (15%)
  Pallas kernels  97.4 us (15%)
  other arithmetic  78.9 us (12%)
  local copies, waits for them, and re-layouts  64.9 us (10%)
  matrix products  61.7 us (10%)
  between operations  15.9 us (2%)
    ppermute x54, waiting for transfers between devices, swap(): lax.ppermute(value, axis, [(source, source ^ bit) for source in range(cou...  150 us
    dot_general x21, matrix products, matmul(): return jnp.dot(left, right, preferred_element_type=jnp.float32)  61.7 us
    ppermute x20, starting transfers between devices, shift(): lax.ppermute(value, axis, [(source, source + steps) for source in range(f...  55.2 us
    ppermute x20, waiting for transfers between devices, shift(): lax.ppermute(value, axis, [(source, source + steps) for source in range(f...  54.2 us
    ppermute x54, starting transfers between devices, swap(): lax.ppermute(value, axis, [(source, source ^ bit) for source in range(cou...  43.4 us
    pallas_call x1, Pallas kernels, mamba_scan_back(): pl.pallas_call(scan_back_kernel, grid=(PAIRS,), in_specs=[columns(rows),...  20.2 us
    pallas_call x1, Pallas kernels, mamba_conv_back(): pl.pallas_call(conv_back_kernel, grid=(BLOCKS,), in_specs=[columns(rows,...  16.3 us
    unnamed x174, local copies, waits for them, and re-layouts  14.5 us
  transfers between devices with their start and end apart: 77, of which 31 were waited for; matrix products, arithmetic and copies ran while one was open for 27% of the time, Pallas kernels for 15%

profile of v2, /device:TPU:0, one launch (start us, length us, event | category | flops | bytes accessed | tf_op | source)
XLA Modules:
  0.0 630.8 jit_solution(6559171646329565019)
XLA Ops:
  8.8 4.1 concatenate.130
  12.9 3.0 collective-permute-start.1
  22.4 10.4 %collective-permute-done.4 = bf16[256,768]{1,0:T(8,128)(2,1)} collective-permute-done((bf16[256,768]{1,0:T(8,128)(2,1)}, bf16[256,768]{1,0:T(8,128)(2,1)}, u32[]{:S(2)}, u32[]{:S(2)}) %collective-permute-start.4) | collective-permute-done | bytes 393248 | tf_op jit(solution)/shard_map/ppermute | solution.py:42
  40.1 4.7 collective-permute-start.6
  44.7 4.6 collective-permute-start.7
  50.0 4.8 collective-permute-done.11
  54.8 3.6 collective-permute-start.8
  58.4 3.5 collective-permute-start.9
  67.5 2.7 pad_maximum_fusion
  70.2 8.0 %all-gather.4.cloned.1.call-done = bf16[1024,3352]{0,1:T(8,128)(2,1)} async-done(((bf16[256,3352]{0,1:T(8,128)(2,1)}), bf16[1024,3352]{0,1:T(8,128)(2,1)}) %all-gather.4.cloned.1.call-update) | async-done | bytes 6864912 | tf_op jit(solution)/shard_map/all_gather | solution.py:791
  78.3 5.0 fusion.88
  85.5 3.4 collective-permute-start.13
  91.9 5.1 copy.55.mixed_ref.z_ref
  101.3 8.9 %conv.1.x_ref.b_ref.c_ref = f32[256,1792]{1,0:T(8,128)} custom-call(f32[256,3352]{1,0:T(8,128)} %copy.55.mixed_ref.z_ref, bf16[8,1792]{1,0:T(8,128)(2,1)} %copy-done.52, f32[4,1792]{1,0:T(4,128)} %reshape.178.taps_ref), custom_call_target="tpu_custom_call" | custom-call | tf_op jit(solution)/shard_map/conv/pallas_call | solution.py:595
  110.2 11.0 %scan.1 = (f32[256,1536]{1,0:T(8,128)}, f32[1536,128]{1,0:T(8,128)}) custom-call(f32[256,1792]{1,0:T(8,128)} %conv.1.x_ref.b_ref.c_ref, f32[256,1792]{1,0:T(8,128)} %conv.1.x_ref.b_ref.c_ref, f32[256,1792]{1,0:T(8,128)} %conv.1.x_ref.b_ref.c_ref, f32[256,24]{1,0:T(8,128)} %get-tuple-element.56.step_ref, f32[256,24]{1,0:T(8,128)} %get-tuple-element.57.cum_ref, ...), custom_call_target="tpu_custom_call" | custom-call | tf_op jit(solution)/shard_map/scan/pallas_call | solution.py:607
  123.2 3.4 collective-permute-start.16
  127.5 8.0 %collective-permute-done.16 = bf16[1536,128]{1,0:T(8,128)(2,1)S(1)} collective-permute-done((bf16[1536,128]{1,0:T(8,128)(2,1)}, bf16[1536,128]{1,0:T(8,128)(2,1)S(1)}, u32[]{:S(2)}, u32[]{:S(2)}) %collective-permute-start.16) | collective-permute-done | bytes 393248 | tf_op jit(solution)/shard_map/ppermute | solution.py:37
  137.6 6.0 collective-permute-start.17
  145.7 4.5 collective-permute-start.14
  155.6 5.7 collective-permute-start.18
  161.9 8.7 %attend.1 = (bf16[256,512]{1,0:T(8,128)(2,1)}, f32[4,256,2]{2,1,0:T(8,128)}) custom-call(bf16[256,512]{1,0:T(8,128)(2,1)} %get-tuple-element.51.q_ref, bf16[1280,256]{1,0:T(8,128)(2,1)} %constant_dynamic-update-slice_fusion.kv_ref, s32[256,1]{1,0:T(8,128)} %copy.52.pos_ref), custom_call_target="tpu_custom_call" | custom-call | tf_op jit(solution)/shard_map/attend/pallas_call | solution.py:237
  171.9 4.3 slice.106
  183.6 5.5 finish.1
  189.1 3.5 multiply_reduce_fusion.2
  213.5 2.9 fusion.73
  216.3 2.6 fusion.72
  225.2 3.3 fusion.83
  229.1 3.5 convolution_convert_fusion.2
  232.6 3.5 convolution_convert_fusion.1
  243.0 9.2 %collective-permute-done.27 = bf16[256,1024]{1,0:T(8,128)(2,1)} collective-permute-done((bf16[256,1024]{1,0:T(8,128)(2,1)}, bf16[256,1024]{1,0:T(8,128)(2,1)}, u32[]{:S(2)}, u32[]{:S(2)}) %collective-permute-start.27) | collective-permute-done | bytes 524320 | tf_op jit(solution)/shard_map/ppermute | solution.py:42
  254.3 8.1 %collective-permute-done.24 = bf16[256,1024]{1,0:T(8,128)(2,1)S(1)} collective-permute-done((bf16[256,1024]{1,0:T(8,128)(2,1)S(1)}, bf16[256,1024]{1,0:T(8,128)(2,1)S(1)}, u32[]{:S(2)}, u32[]{:S(2)}) %collective-permute-start.24) | collective-permute-done | bytes 524320 | tf_op jit(solution)/shard_map/ppermute | solution.py:42
  262.4 3.0 bitcast_add_fusion
  269.0 12.0 %attend_back.1 = (bf16[256,512]{1,0:T(8,128)(2,1)}, bf16[1280,256]{1,0:T(8,128)(2,1)}) custom-call(bf16[256,512]{1,0:T(8,128)(2,1)} %get-tuple-element.51.q_ref, bf16[1280,256]{1,0:T(8,128)(2,1)} %constant_dynamic-update-slice_fusion.kv_ref, s32[256,1]{1,0:T(8,128)} %copy.52.pos_ref, bf16[256,512]{1,0:T(8,128)(2,1)} %get-tuple-element.54.o_ref, ...), custom_call_target="tpu_custom_call" | custom-call | tf_op jit(solution)/shard_map/attend_back/pallas_call | solution.py:264
  288.2 5.9 gate_back.1
  296.9 4.7 fusion.85
  301.6 3.7 fusion.87
  308.0 20.2 %scan_back.1 = (f32[256,1536]{1,0:T(8,128)}, f32[256,256]{1,0:T(8,128)}, f32[256,24]{1,0:T(8,128)}, f32[256,24]{1,0:T(8,128)}, f32[1,1536]{1,0:T(1,128)}) custom-call(f32[256,1792]{1,0:T(8,128)} %conv.1.x_ref.b_ref.c_ref, f32[256,1792]{1,0:T(8,128)} %conv.1.x_ref.b_ref.c_ref, f32[256,1792]{1,0:T(8,128)} %conv.1.x_ref.b_ref.c_ref, ...), custom_call_target="tpu_custom_call" | custom-call | tf_op jit(solution)/shard_map/scan_back/pallas_call | solution.py:667
  340.7 16.2 %collective-permute-done.31 = bf16[1536,128]{1,0:T(8,128)(2,1)S(1)} collective-permute-done((bf16[1536,128]{1,0:T(8,128)(2,1)S(1)}, bf16[1536,128]{1,0:T(8,128)(2,1)S(1)}, u32[]{:S(2)}, u32[]{:S(2)}) %collective-permute-start.31) | collective-permute-done | bytes 393248 | tf_op jit(solution)/shard_map/ppermute | solution.py:37
  358.7 2.8 fusion.12
  363.0 24.7 %collective-permute-done.32 = bf16[1536,128]{1,0:T(8,128)(2,1)S(1)} collective-permute-done((bf16[1536,128]{1,0:T(8,128)(2,1)S(1)}, bf16[1536,128]{1,0:T(8,128)(2,1)S(1)}, u32[]{:S(2)}, u32[]{:S(2)}) %collective-permute-start.32) | collective-permute-done | bytes 393248 | tf_op jit(solution)/shard_map/ppermute | solution.py:37
  389.1 16.3 %conv_back.1 = (f32[256,1792]{1,0:T(8,128)}, f32[8,1792]{1,0:T(8,128)}, f32[4,1792]{1,0:T(4,128)}, f32[256,24]{1,0:T(8,128)}, f32[256,24]{1,0:T(8,128)}) custom-call(f32[256,3352]{1,0:T(8,128)} %copy.55.mixed_ref.z_ref, bf16[8,1792]{1,0:T(8,128)(2,1)} %copy-done.52, f32[4,1792]{1,0:T(4,128)} %reshape.178.taps_ref, f32[256,1792]{1,0:T(8,128)} %conv.1.x_ref.b_ref.c_ref, ...), custom_call_target="tpu_custom_call" | custom-call | tf_op jit(solution)/shard_map/conv_back/pallas_call | solution.py:704
  406.9 3.2 fusion
  425.8 6.2 fusion.86
  432.1 6.2 fusion.32
  445.0 3.6 collective-permute-start.59
  450.0 7.9 %collective-permute-done.59 = bf16[128,1536]{1,0:T(8,128)(2,1)S(1)} collective-permute-done((bf16[128,1536]{1,0:T(8,128)(2,1)S(1)}, bf16[128,1536]{1,0:T(8,128)(2,1)S(1)}, u32[]{:S(2)}, u32[]{:S(2)}) %collective-permute-start.59) | collective-permute-done | bytes 393248 | tf_op jit(solution)/shard_map/ppermute | solution.py:42
  458.7 10.0 %collective-permute-done.40 = bf16[264,768]{1,0:T(8,128)(2,1)S(1)} collective-permute-done((bf16[264,768]{1,0:T(8,128)(2,1)S(1)}, bf16[264,768]{1,0:T(8,128)(2,1)S(1)}, u32[]{:S(2)}, u32[]{:S(2)}) %collective-permute-start.40) | collective-permute-done | bytes 405536 | tf_op jit(solution)/shard_map/ppermute | solution.py:42
  470.4 2.6 fusion.1
  473.3 6.0 collective-permute-done.60
  481.1 4.9 collective-permute-done.42
  492.6 3.8 collective-permute-start.63
  497.3 2.7 fusion.2
  500.6 5.8 collective-permute-done.45
  509.8 4.8 collective-permute-done.46
  515.7 10.7 %collective-permute-done.51 = bf16[128,1024]{1,0:T(8,128)(2,1)S(1)} collective-permute-done((bf16[128,1024]{1,0:T(8,128)(2,1)}, bf16[128,1024]{1,0:T(8,128)(2,1)S(1)}, u32[]{:S(2)}, u32[]{:S(2)}) %collective-permute-start.51) | collective-permute-done | bytes 262176 | tf_op jit(solution)/shard_map/ppermute | solution.py:42
  530.5 8.0 %collective-permute-done.52 = bf16[64,1024]{1,0:T(8,128)(2,1)S(1)} collective-permute-done((bf16[64,1024]{1,0:T(8,128)(2,1)S(1)}, bf16[64,1024]{1,0:T(8,128)(2,1)S(1)}, u32[]{:S(2)}, u32[]{:S(2)}) %collective-permute-start.52) | collective-permute-done | bytes 131104 | tf_op jit(solution)/shard_map/ppermute | solution.py:42
  540.7 3.9 collective-permute-done.53
  544.7 10.9 %collective-permute-done.69 = bf16[64,1816]{0,1:T(8,128)(2,1)S(1)} collective-permute-done((bf16[64,1816]{0,1:T(8,128)(2,1)S(1)}, bf16[64,1816]{0,1:T(8,128)(2,1)S(1)}, u32[]{:S(2)}, u32[]{:S(2)}) %collective-permute-start.69) | collective-permute-done | bytes 232480 | tf_op jit(solution)/shard_map/ppermute | solution.py:42
  556.2 5.0 collective-permute-done.54
  562.0 22.5 %collective-permute-done.70 = bf16[32,1816]{0,1:T(8,128)(2,1)S(1)} collective-permute-done((bf16[32,1816]{0,1:T(8,128)(2,1)S(1)}, bf16[32,1816]{0,1:T(8,128)(2,1)S(1)}, u32[]{:S(2)}, u32[]{:S(2)}) %collective-permute-start.70) | collective-permute-done | bytes 116256 | tf_op jit(solution)/shard_map/ppermute | solution.py:42
  586.1 8.3 %collective-permute-done.71 = bf16[32,1816]{0,1:T(8,128)(2,1)S(1)} collective-permute-done((bf16[32,1816]{0,1:T(8,128)(2,1)S(1)}, bf16[32,1816]{0,1:T(8,128)(2,1)S(1)}, u32[]{:S(2)}, u32[]{:S(2)}) %collective-permute-start.71) | collective-permute-done | bytes 116256 | tf_op jit(solution)/shard_map/ppermute | solution.py:42
  596.9 2.9 convert_element_type.405
  606.3 8.6 %collective-permute-start.73 = (bf16[128,1816]{0,1:T(8,128)(2,1)S(1)}, bf16[128,1816]{0,1:T(8,128)(2,1)S(1)}, u32[]{:S(2)}, u32[]{:S(2)}) collective-permute-start(bf16[128,1816]{0,1:T(8,128)(2,1)S(1)} %maximum_select_fusion.5), channel_id=1, source_target_pairs={{0,4},{4,0},{8,12},{12,8},{16,20},{20,16},{24,28},{28,24},{1,5},{5... | collective-permute-start | bytes 1394696 | tf_op jit(solution)/shard_map/ppermute | solution.py:42
  617.1 4.4 collective-permute-done.73
  (469 shorter events, 187.1 us)
Async XLA Ops:
  7.2 71.1 %all-gather.4.cloned.1.call-start = ((), (), s32[]{:S(2)}) async-start(), calls=%async_computation | async-start | bytes 8581120 | tf_op jit(solution)/shard_map/all_gather | solution.py:791
  8.0 162.6 %all-gather.6.cloned.1.call-start = ((), (), s32[]{:S(2)}) async-start(), calls=%async_computation.1 | async-start | bytes 5242880 | tf_op jit(solution)/shard_map/all_gather | solution.py:793
  12.9 7.9 %collective-permute-start.1 = (bf16[2706]{0:T(1024)(128)(2,1)S(1)}, bf16[2706]{0:T(1024)(128)(2,1)S(1)}, u32[]{:S(2)}, u32[]{:S(2)}) collective-permute-start(bf16[2706]{0:T(1024)(128)(2,1)S(1)} %concatenate.130), channel_id=1, source_target_pairs={{0,2},{1,3},{2,0},{3,1},{4,6},{5,7},{6,4},{7,5},{8,10},{9,11},{10,... | collective-permute-start | bytes 16244 | tf_op jit(solution)/shard_map/ppermute | solution.py:42
  15.9 16.9 %collective-permute-start.4 = (bf16[256,768]{1,0:T(8,128)(2,1)}, bf16[256,768]{1,0:T(8,128)(2,1)}, u32[]{:S(2)}, u32[]{:S(2)}) collective-permute-start(bf16[256,768]{1,0:T(8,128)(2,1)} %param.20), channel_id=1, source_target_pairs={{0,2},{1,3},{2,0},{3,1},{4,6},{5,7},{6,4},{7,5},{8,10},{9,11},{10,... | collective-permute-start | bytes 1179656 | tf_op jit(solution)/shard_map/ppermute | solution.py:42
  16.0 18.4 %collective-permute-start.3 = (bf16[256,768]{1,0:T(8,128)(2,1)}, bf16[256,768]{1,0:T(8,128)(2,1)}, u32[]{:S(2)}, u32[]{:S(2)}) collective-permute-start(bf16[256,768]{1,0:T(8,128)(2,1)} %param.20), channel_id=1, source_target_pairs={{0,1},{1,0},{2,3},{3,2},{4,5},{5,4},{6,7},{7,6},{8,9},{9,8},{10,11... | collective-permute-start | bytes 1179656 | tf_op jit(solution)/shard_map/ppermute | solution.py:42
  16.5 38.3 %collective-permute-start.11 = (bf16[256,1024]{1,0:T(8,128)(2,1)S(1)}, bf16[256,1024]{1,0:T(8,128)(2,1)}, u32[]{:S(2)}, u32[]{:S(2)}) collective-permute-start(bf16[256,1024]{1,0:T(8,128)(2,1)S(1)} %bitcast_convert_fusion), channel_id=1, source_target_pairs={{0,2},{1,3},{2,0},{3,1},{4,6},{5,7},{6,4},{7,5},{8,10},{9,11},{10,... | collective-permute-start | bytes 1572872 | tf_op jit(solution)/shard_map/ppermute | solution.py:42
  19.4 577.5 %all-reduce.4.cloned.1.call-start = ((), (), s32[]{:S(2)}) async-start(), calls=%async_computation.2 | async-start | bytes 6291456 | tf_op jit(solution)/shard_map/psum | solution.py:850
  21.5 46.0 %collective-permute-start.10 = (bf16[256,1024]{1,0:T(8,128)(2,1)S(1)}, bf16[256,1024]{1,0:T(8,128)(2,1)}, u32[]{:S(2)}, u32[]{:S(2)}) collective-permute-start(bf16[256,1024]{1,0:T(8,128)(2,1)S(1)} %bitcast_convert_fusion), channel_id=1, source_target_pairs={{0,1},{1,0},{2,3},{3,2},{4,5},{5,4},{6,7},{7,6},{8,9},{9,8},{10,11... | collective-permute-start | bytes 1572872 | tf_op jit(solution)/shard_map/ppermute | solution.py:42
  40.1 18.3 %collective-permute-start.6 = (bf16[256,256]{1,0:T(8,128)(2,1)}, bf16[256,256]{1,0:T(8,128)(2,1)S(1)}, u32[]{:S(2)}, u32[]{:S(2)}) collective-permute-start(bf16[256,256]{1,0:T(8,128)(2,1)} %get-tuple-element.52), channel_id=1, source_target_pairs={{0,16},{4,20},{8,24},{12,28},{1,17},{5,21},{9,25},{13,29},{2,18},{... | collective-permute-start | bytes 393224 | tf_op jit(solution)/shard_map/ppermute | solution.py:37
  44.7 17.8 %collective-permute-start.7 = (bf16[256,256]{1,0:T(8,128)(2,1)}, bf16[256,256]{1,0:T(8,128)(2,1)S(1)}, u32[]{:S(2)}, u32[]{:S(2)}) collective-permute-start(bf16[256,256]{1,0:T(8,128)(2,1)} %get-tuple-element.52), channel_id=1, source_target_pairs={{0,12},{4,16},{8,20},{12,24},{16,28},{1,13},{5,17},{9,21},{13,25},... | collective-permute-start | bytes 393224 | tf_op jit(solution)/shard_map/ppermute | solution.py:37
  54.8 12.7 %collective-permute-start.12 = (bf16[256,1024]{1,0:T(8,128)(2,1)}, bf16[256,1024]{1,0:T(8,128)(2,1)S(1)}, u32[]{:S(2)}, u32[]{:S(2)}) collective-permute-start(bf16[256,1024]{1,0:T(8,128)(2,1)} %collective-permute-done.11), channel_id=1, source_target_pairs={{0,1},{1,0},{2,3},{3,2},{4,5},{5,4},{6,7},{7,6},{8,9},{9,8},{10,11... | collective-permute-start | bytes 1572872 | tf_op jit(solution)/shard_map/ppermute | solution.py:42
  54.8 8.4 %collective-permute-start.8 = (bf16[256,256]{1,0:T(8,128)(2,1)}, bf16[256,256]{1,0:T(8,128)(2,1)S(1)}, u32[]{:S(2)}, u32[]{:S(2)}) collective-permute-start(bf16[256,256]{1,0:T(8,128)(2,1)} %get-tuple-element.52), channel_id=1, source_target_pairs={{0,8},{4,12},{8,16},{12,20},{16,24},{20,28},{1,9},{5,13},{9,17},{1... | collective-permute-start | bytes 393224 | tf_op jit(solution)/shard_map/ppermute | solution.py:37
  58.4 6.9 %collective-permute-start.9 = (bf16[256,256]{1,0:T(8,128)(2,1)}, bf16[256,256]{1,0:T(8,128)(2,1)S(1)}, u32[]{:S(2)}, u32[]{:S(2)}) collective-permute-start(bf16[256,256]{1,0:T(8,128)(2,1)} %get-tuple-element.52), channel_id=1, source_target_pairs={{0,4},{4,8},{8,12},{12,16},{16,20},{20,24},{24,28},{1,5},{5,9},{9,... | collective-permute-start | bytes 393224 | tf_op jit(solution)/shard_map/ppermute | solution.py:37
  85.5 15.2 %collective-permute-start.13 = (bf16[8,1792]{1,0:T(8,128)(2,1)S(1)}, bf16[8,1792]{1,0:T(8,128)(2,1)S(1)}, u32[]{:S(2)}, u32[]{:S(2)}) collective-permute-start(bf16[8,1792]{1,0:T(8,128)(2,1)S(1)} %copy.63), channel_id=1, source_target_pairs={{0,4},{4,8},{8,12},{12,16},{16,20},{20,24},{24,28},{1,5},{5,9},{9,... | collective-permute-start | bytes 86024 | tf_op jit(solution)/shard_map/ppermute | solution.py:37
  123.2 12.2 %collective-permute-start.16 = (bf16[1536,128]{1,0:T(8,128)(2,1)}, bf16[1536,128]{1,0:T(8,128)(2,1)S(1)}, u32[]{:S(2)}, u32[]{:S(2)}) collective-permute-start(bf16[1536,128]{1,0:T(8,128)(2,1)} %convert_element_type.319), channel_id=1, source_target_pairs={{0,4},{4,8},{8,12},{12,16},{16,20},{20,24},{24,28},{1,5},{5,9},{9,... | collective-permute-start | bytes 1179656 | tf_op jit(solution)/shard_map/ppermute | solution.py:37
  137.6 15.8 %collective-permute-start.17 = (bf16[1536,128]{1,0:T(8,128)(2,1)}, bf16[1536,128]{1,0:T(8,128)(2,1)}, u32[]{:S(2)}, u32[]{:S(2)}) collective-permute-start(bf16[1536,128]{1,0:T(8,128)(2,1)} %fusion.50), channel_id=1, source_target_pairs={{0,8},{4,12},{8,16},{12,20},{16,24},{20,28},{1,9},{5,13},{9,17},{1... | collective-permute-start | bytes 1179656 | tf_op jit(solution)/shard_map/ppermute | solution.py:37
  155.6 25.7 %collective-permute-start.18 = (bf16[1536,128]{1,0:T(8,128)(2,1)}, bf16[1536,128]{1,0:T(8,128)(2,1)S(1)}, u32[]{:S(2)}, u32[]{:S(2)}) collective-permute-start(bf16[1536,128]{1,0:T(8,128)(2,1)} %fusion.44), channel_id=1, source_target_pairs={{0,16},{4,20},{8,24},{12,28},{1,17},{5,21},{9,25},{13,29},{2,18},{... | collective-permute-start | bytes 1179656 | tf_op jit(solution)/shard_map/ppermute | solution.py:37
  194.1 12.7 %collective-permute-start.20 = (bf16[256,1024]{1,0:T(8,128)(2,1)}, bf16[256,1024]{1,0:T(8,128)(2,1)}, u32[]{:S(2)}, u32[]{:S(2)}) collective-permute-start(bf16[256,1024]{1,0:T(8,128)(2,1)} %multiply_convert_fusion.3), channel_id=1, source_target_pairs={{0,2},{1,3},{2,0},{3,1},{4,6},{5,7},{6,4},{7,5},{8,10},{9,11},{10,... | collective-permute-start | bytes 1572872 | tf_op jit(solution)/shard_map/ppermute | solution.py:42
  204.5 8.9 %collective-permute-start.19 = (bf16[256,1024]{1,0:T(8,128)(2,1)}, bf16[256,1024]{1,0:T(8,128)(2,1)S(1)}, u32[]{:S(2)}, u32[]{:S(2)}) collective-permute-start(bf16[256,1024]{1,0:T(8,128)(2,1)} %multiply_convert_fusion.3), channel_id=1, source_target_pairs={{0,1},{1,0},{2,3},{3,2},{4,5},{5,4},{6,7},{7,6},{8,9},{9,8},{10,11... | collective-permute-start | bytes 1572872 | tf_op jit(solution)/shard_map/ppermute | solution.py:42
  206.8 6.7 %collective-permute-start.21 = (bf16[256,1024]{1,0:T(8,128)(2,1)}, bf16[256,1024]{1,0:T(8,128)(2,1)S(1)}, u32[]{:S(2)}, u32[]{:S(2)}) collective-permute-start(bf16[256,1024]{1,0:T(8,128)(2,1)} %collective-permute-done.20), channel_id=1, source_target_pairs={{0,1},{1,0},{2,3},{3,2},{4,5},{5,4},{6,7},{7,6},{8,9},{9,8},{10,11... | collective-permute-start | bytes 1572872 | tf_op jit(solution)/shard_map/ppermute | solution.py:42
  224.7 11.4 %collective-permute-start.26 = (bf16[256,1024]{1,0:T(8,128)(2,1)S(1)}, bf16[256,1024]{1,0:T(8,128)(2,1)S(1)}, u32[]{:S(2)}, u32[]{:S(2)}) collective-permute-start(bf16[256,1024]{1,0:T(8,128)(2,1)S(1)} %get-tuple-element.105), channel_id=1, source_target_pairs={{0,1},{1,0},{2,3},{3,2},{4,5},{5,4},{6,7},{7,6},{8,9},{9,8},{10,11... | collective-permute-start | bytes 1572872 | tf_op jit(solution)/shard_map/ppermute | solution.py:42
  224.7 18.3 %collective-permute-start.25 = (bf16[256,1024]{1,0:T(8,128)(2,1)}, bf16[256,1024]{1,0:T(8,128)(2,1)}, u32[]{:S(2)}, u32[]{:S(2)}) collective-permute-start(bf16[256,1024]{1,0:T(8,128)(2,1)} %get-tuple-element.104), channel_id=1, source_target_pairs={{0,1},{1,0},{2,3},{3,2},{4,5},{5,4},{6,7},{7,6},{8,9},{9,8},{10,11... | collective-permute-start | bytes 1572872 | tf_op jit(solution)/shard_map/ppermute | solution.py:42
  228.6 12.2 %collective-permute-start.23 = (bf16[256,1024]{1,0:T(8,128)(2,1)S(1)}, bf16[256,1024]{1,0:T(8,128)(2,1)}, u32[]{:S(2)}, u32[]{:S(2)}) collective-permute-start(bf16[256,1024]{1,0:T(8,128)(2,1)S(1)} %get-tuple-element.107), channel_id=1, source_target_pairs={{0,1},{1,0},{2,3},{3,2},{4,5},{5,4},{6,7},{7,6},{8,9},{9,8},{10,11... | collective-permute-start | bytes 1572872 | tf_op jit(solution)/shard_map/ppermute | solution.py:42
  228.6 25.7 %collective-permute-start.22 = (bf16[256,1024]{1,0:T(8,128)(2,1)S(1)}, bf16[256,1024]{1,0:T(8,128)(2,1)}, u32[]{:S(2)}, u32[]{:S(2)}) collective-permute-start(bf16[256,1024]{1,0:T(8,128)(2,1)S(1)} %get-tuple-element.106), channel_id=1, source_target_pairs={{0,1},{1,0},{2,3},{3,2},{4,5},{5,4},{6,7},{7,6},{8,9},{9,8},{10,11... | collective-permute-start | bytes 1572872 | tf_op jit(solution)/shard_map/ppermute | solution.py:42
  237.1 15.1 %collective-permute-start.27 = (bf16[256,1024]{1,0:T(8,128)(2,1)}, bf16[256,1024]{1,0:T(8,128)(2,1)}, u32[]{:S(2)}, u32[]{:S(2)}) collective-permute-start(bf16[256,1024]{1,0:T(8,128)(2,1)} %fusion.17), channel_id=1, source_target_pairs={{0,2},{1,3},{2,0},{3,1},{4,6},{5,7},{6,4},{7,5},{8,10},{9,11},{10,... | collective-permute-start | bytes 1572872 | tf_op jit(solution)/shard_map/ppermute | solution.py:42
  242.4 20.1 %collective-permute-start.24 = (bf16[256,1024]{1,0:T(8,128)(2,1)S(1)}, bf16[256,1024]{1,0:T(8,128)(2,1)S(1)}, u32[]{:S(2)}, u32[]{:S(2)}) collective-permute-start(bf16[256,1024]{1,0:T(8,128)(2,1)S(1)} %fusion.19), channel_id=1, source_target_pairs={{0,2},{1,3},{2,0},{3,1},{4,6},{5,7},{6,4},{7,5},{8,10},{9,11},{10,... | collective-permute-start | bytes 1572872 | tf_op jit(solution)/shard_map/ppermute | solution.py:42
  283.0 46.9 %collective-permute-start.34 = (bf16[256,256]{1,0:T(8,128)(2,1)}, bf16[256,256]{1,0:T(8,128)(2,1)}, u32[]{:S(2)}, u32[]{:S(2)}) collective-permute-start(bf16[256,256]{1,0:T(8,128)(2,1)} %get-tuple-element.119), channel_id=1, source_target_pairs={{4,0},{8,4},{12,8},{16,12},{20,16},{24,20},{28,24},{5,1},{9,5},{13... | collective-permute-start | bytes 393224 | tf_op jit(solution)/shard_map/ppermute | solution.py:37
  284.3 45.6 %collective-permute-start.35 = (bf16[256,256]{1,0:T(8,128)(2,1)}, bf16[256,256]{1,0:T(8,128)(2,1)}, u32[]{:S(2)}, u32[]{:S(2)}) collective-permute-start(bf16[256,256]{1,0:T(8,128)(2,1)} %get-tuple-element.118), channel_id=1, source_target_pairs={{8,0},{12,4},{16,8},{20,12},{24,16},{28,20},{9,1},{13,5},{17,9},{2... | collective-permute-start | bytes 393224 | tf_op jit(solution)/shard_map/ppermute | solution.py:37
  285.6 44.8 %collective-permute-start.36 = (bf16[256,256]{1,0:T(8,128)(2,1)}, bf16[256,256]{1,0:T(8,128)(2,1)}, u32[]{:S(2)}, u32[]{:S(2)}) collective-permute-start(bf16[256,256]{1,0:T(8,128)(2,1)} %get-tuple-element.117), channel_id=1, source_target_pairs={{12,0},{16,4},{20,8},{24,12},{28,16},{13,1},{17,5},{21,9},{25,13},... | collective-permute-start | bytes 393224 | tf_op jit(solution)/shard_map/ppermute | solution.py:37
  286.9 43.6 %collective-permute-start.37 = (bf16[256,256]{1,0:T(8,128)(2,1)}, bf16[256,256]{1,0:T(8,128)(2,1)}, u32[]{:S(2)}, u32[]{:S(2)}) collective-permute-start(bf16[256,256]{1,0:T(8,128)(2,1)} %get-tuple-element.116), channel_id=1, source_target_pairs={{16,0},{20,4},{24,8},{28,12},{17,1},{21,5},{25,9},{29,13},{18,2},{... | collective-permute-start | bytes 393224 | tf_op jit(solution)/shard_map/ppermute | solution.py:37
  295.4 40.3 %collective-permute-start.30 = (bf16[1536,128]{1,0:T(8,128)(2,1)S(1)}, bf16[1536,128]{1,0:T(8,128)(2,1)S(1)}, u32[]{:S(2)}, u32[]{:S(2)}) collective-permute-start(bf16[1536,128]{1,0:T(8,128)(2,1)S(1)} %convert_element_type.341), channel_id=1, source_target_pairs={{4,0},{8,4},{12,8},{16,12},{20,16},{24,20},{28,24},{5,1},{9,5},{13... | collective-permute-start | bytes 1179656 | tf_op jit(solution)/shard_map/ppermute | solution.py:37
  329.9 77.0 %collective-permute-start.48 = (bf16[512,1024]{1,0:T(8,128)(2,1)}, bf16[512,1024]{1,0:T(8,128)(2,1)}, u32[]{:S(2)}, u32[]{:S(2)}) collective-permute-start(bf16[512,1024]{1,0:T(8,128)(2,1)} %get-tuple-element.94), channel_id=1, source_target_pairs={{0,1},{1,0},{2,3},{3,2},{4,5},{5,4},{6,7},{7,6},{8,9},{9,8},{10,11... | collective-permute-start | bytes 3145736 | tf_op jit(solution)/shard_map/ppermute | solution.py:42
  329.9 139.0 %collective-permute-start.47 = (bf16[512,1024]{1,0:T(8,128)(2,1)}, bf16[512,1024]{1,0:T(8,128)(2,1)}, u32[]{:S(2)}, u32[]{:S(2)}) collective-permute-start(bf16[512,1024]{1,0:T(8,128)(2,1)} %get-tuple-element.93), channel_id=1, source_target_pairs={{0,1},{1,0},{2,3},{3,2},{4,5},{5,4},{6,7},{7,6},{8,9},{9,8},{10,11... | collective-permute-start | bytes 3145736 | tf_op jit(solution)/shard_map/ppermute | solution.py:42
  330.4 28.3 %collective-permute-start.57 = (bf16[256,1536]{1,0:T(8,128)(2,1)}, bf16[256,1536]{1,0:T(8,128)(2,1)}, u32[]{:S(2)}, u32[]{:S(2)}) collective-permute-start(bf16[256,1536]{1,0:T(8,128)(2,1)} %get-tuple-element.101), channel_id=1, source_target_pairs={{0,1},{1,0},{2,3},{3,2},{4,5},{5,4},{6,7},{7,6},{8,9},{9,8},{10,11... | collective-permute-start | bytes 2359304 | tf_op jit(solution)/shard_map/ppermute | solution.py:42
  330.5 111.7 %collective-permute-start.56 = (bf16[256,1536]{1,0:T(8,128)(2,1)}, bf16[256,1536]{1,0:T(8,128)(2,1)}, u32[]{:S(2)}, u32[]{:S(2)}) collective-permute-start(bf16[256,1536]{1,0:T(8,128)(2,1)} %get-tuple-element.100), channel_id=1, source_target_pairs={{0,1},{1,0},{2,3},{3,2},{4,5},{5,4},{6,7},{7,6},{8,9},{9,8},{10,11... | collective-permute-start | bytes 2359304 | tf_op jit(solution)/shard_map/ppermute | solution.py:42
  336.5 20.4 %collective-permute-start.31 = (bf16[1536,128]{1,0:T(8,128)(2,1)S(1)}, bf16[1536,128]{1,0:T(8,128)(2,1)S(1)}, u32[]{:S(2)}, u32[]{:S(2)}) collective-permute-start(bf16[1536,128]{1,0:T(8,128)(2,1)S(1)} %fusion.49), channel_id=1, source_target_pairs={{8,0},{12,4},{16,8},{20,12},{24,16},{28,20},{9,1},{13,5},{17,9},{2... | collective-permute-start | bytes 1179656 | tf_op jit(solution)/shard_map/ppermute | solution.py:37
  357.4 30.3 %collective-permute-start.32 = (bf16[1536,128]{1,0:T(8,128)(2,1)S(1)}, bf16[1536,128]{1,0:T(8,128)(2,1)S(1)}, u32[]{:S(2)}, u32[]{:S(2)}) collective-permute-start(bf16[1536,128]{1,0:T(8,128)(2,1)S(1)} %fusion.48), channel_id=1, source_target_pairs={{16,0},{20,4},{24,8},{28,12},{17,1},{21,5},{25,9},{29,13},{18,2},{... | collective-permute-start | bytes 1179656 | tf_op jit(solution)/shard_map/ppermute | solution.py:37
  361.5 81.3 %collective-permute-start.58 = (bf16[256,1536]{1,0:T(8,128)(2,1)}, bf16[256,1536]{1,0:T(8,128)(2,1)}, u32[]{:S(2)}, u32[]{:S(2)}) collective-permute-start(bf16[256,1536]{1,0:T(8,128)(2,1)} %fusion.12), channel_id=1, source_target_pairs={{0,2},{1,3},{2,0},{3,1},{4,6},{5,7},{6,4},{7,5},{8,10},{9,11},{10,... | collective-permute-start | bytes 2359304 | tf_op jit(solution)/shard_map/ppermute | solution.py:42
  405.4 19.5 %collective-permute-start.33 = (f32[8,1792]{1,0:T(8,128)}, f32[8,1792]{1,0:T(8,128)}, u32[]{:S(2)}, u32[]{:S(2)}) collective-permute-start(f32[8,1792]{1,0:T(8,128)} %get-tuple-element.74), channel_id=1, source_target_pairs={{4,0},{8,4},{12,8},{16,12},{20,16},{24,20},{28,24},{5,1},{9,5},{13... | collective-permute-start | bytes 172040 | tf_op jit(solution)/shard_map/ppermute | solution.py:37
  410.1 60.3 %collective-permute-start.49 = (bf16[512,1024]{1,0:T(8,128)(2,1)}, bf16[512,1024]{1,0:T(8,128)(2,1)}, u32[]{:S(2)}, u32[]{:S(2)}) collective-permute-start(bf16[512,1024]{1,0:T(8,128)(2,1)} %fusion), channel_id=1, source_target_pairs={{0,2},{1,3},{2,0},{3,1},{4,6},{5,7},{6,4},{7,5},{8,10},{9,11},{10,... | collective-permute-start | bytes 3145736 | tf_op jit(solution)/shard_map/ppermute | solution.py:42
  439.5 10.3 %collective-permute-start.39 = (bf16[264,768]{1,0:T(8,128)(2,1)S(1)}, bf16[264,768]{1,0:T(8,128)(2,1)S(1)}, u32[]{:S(2)}, u32[]{:S(2)}) collective-permute-start(bf16[264,768]{1,0:T(8,128)(2,1)S(1)} %pad_maximum_fusion.7), channel_id=1, source_target_pairs={{0,1},{1,0},{2,3},{3,2},{4,5},{5,4},{6,7},{7,6},{8,9},{9,8},{10,11... | collective-permute-start | bytes 1216520 | tf_op jit(solution)/shard_map/ppermute | solution.py:42
  442.2 16.4 %collective-permute-start.38 = (bf16[264,768]{1,0:T(8,128)(2,1)S(1)}, bf16[264,768]{1,0:T(8,128)(2,1)S(1)}, u32[]{:S(2)}, u32[]{:S(2)}) collective-permute-start(bf16[264,768]{1,0:T(8,128)(2,1)S(1)} %pad_maximum_fusion.6), channel_id=1, source_target_pairs={{0,1},{1,0},{2,3},{3,2},{4,5},{5,4},{6,7},{7,6},{8,9},{9,8},{10,11... | collective-permute-start | bytes 1216520 | tf_op jit(solution)/shard_map/ppermute | solution.py:42
  445.0 12.9 %collective-permute-start.59 = (bf16[128,1536]{1,0:T(8,128)(2,1)S(1)}, bf16[128,1536]{1,0:T(8,128)(2,1)S(1)}, u32[]{:S(2)}, u32[]{:S(2)}) collective-permute-start(bf16[128,1536]{1,0:T(8,128)(2,1)S(1)} %select_convert_fusion.4), channel_id=1, source_target_pairs={{0,8},{4,12},{8,0},{12,4},{16,24},{20,28},{24,16},{28,20},{1,9},{5... | collective-permute-start | bytes 1179656 | tf_op jit(solution)/shard_map/ppermute | solution.py:42
  449.8 47.5 %collective-permute-start.66 = (bf16[256,1816]{0,1:T(8,128)(2,1)S(1)}, bf16[256,1816]{0,1:T(8,128)(2,1)S(1)}, u32[]{:S(2)}, u32[]{:S(2)}) collective-permute-start(bf16[256,1816]{0,1:T(8,128)(2,1)S(1)} %get-tuple-element.99), channel_id=1, source_target_pairs={{0,1},{1,0},{2,3},{3,2},{4,5},{5,4},{6,7},{7,6},{8,9},{9,8},{10,11... | collective-permute-start | bytes 2789384 | tf_op jit(solution)/shard_map/ppermute | solution.py:42
  457.9 10.8 %collective-permute-start.40 = (bf16[264,768]{1,0:T(8,128)(2,1)S(1)}, bf16[264,768]{1,0:T(8,128)(2,1)S(1)}, u32[]{:S(2)}, u32[]{:S(2)}) collective-permute-start(bf16[264,768]{1,0:T(8,128)(2,1)S(1)} %fusion.40), channel_id=1, source_target_pairs={{0,2},{1,3},{2,0},{3,1},{4,6},{5,7},{6,4},{7,5},{8,10},{9,11},{10,... | collective-permute-start | bytes 1216520 | tf_op jit(solution)/shard_map/ppermute | solution.py:42
  458.7 67.9 %collective-permute-start.65 = (bf16[256,1816]{0,1:T(8,128)(2,1)}, bf16[256,1816]{0,1:T(8,128)(2,1)S(1)}, u32[]{:S(2)}, u32[]{:S(2)}) collective-permute-start(bf16[256,1816]{0,1:T(8,128)(2,1)} %get-tuple-element.98), channel_id=1, source_target_pairs={{0,1},{1,0},{2,3},{3,2},{4,5},{5,4},{6,7},{7,6},{8,9},{9,8},{10,11... | collective-permute-start | bytes 2789384 | tf_op jit(solution)/shard_map/ppermute | solution.py:42
  468.7 10.6 %collective-permute-start.60 = (bf16[64,1536]{1,0:T(8,128)(2,1)S(1)}, bf16[64,1536]{1,0:T(8,128)(2,1)S(1)}, u32[]{:S(2)}, u32[]{:S(2)}) collective-permute-start(bf16[64,1536]{1,0:T(8,128)(2,1)S(1)} %select_convert_fusion.7), channel_id=1, source_target_pairs={{0,16},{4,20},{8,24},{12,28},{16,0},{20,4},{24,8},{28,12},{1,17},{... | collective-permute-start | bytes 589832 | tf_op jit(solution)/shard_map/ppermute | solution.py:42
  468.9 10.5 %collective-permute-start.41 = (bf16[132,768]{1,0:T(8,128)(2,1)S(1)}, bf16[132,768]{1,0:T(8,128)(2,1)S(1)}, u32[]{:S(2)}, u32[]{:S(2)}) collective-permute-start(bf16[132,768]{1,0:T(8,128)(2,1)S(1)} %select_convert_fusion.6), channel_id=1, source_target_pairs={{0,8},{4,12},{8,0},{12,4},{16,24},{20,28},{24,16},{28,20},{1,9},{5... | collective-permute-start | bytes 608264 | tf_op jit(solution)/shard_map/ppermute | solution.py:42
  473.2 35.6 %collective-permute-start.50 = (bf16[256,1024]{1,0:T(8,128)(2,1)S(1)}, bf16[256,1024]{1,0:T(8,128)(2,1)S(1)}, u32[]{:S(2)}, u32[]{:S(2)}) collective-permute-start(bf16[256,1024]{1,0:T(8,128)(2,1)S(1)} %select_convert_fusion), channel_id=1, source_target_pairs={{0,4},{4,0},{8,12},{12,8},{16,20},{20,16},{24,28},{28,24},{1,5},{5... | collective-permute-start | bytes 1572872 | tf_op jit(solution)/shard_map/ppermute | solution.py:42
  492.6 14.0 %collective-permute-start.63 = (bf16[64,1536]{1,0:T(8,128)(2,1)S(1)}, bf16[64,1536]{1,0:T(8,128)(2,1)S(1)}, u32[]{:S(2)}, u32[]{:S(2)}) collective-permute-start(bf16[64,1536]{1,0:T(8,128)(2,1)S(1)} %maximum_select_fusion.10), channel_id=1, source_target_pairs={{0,16},{4,20},{8,24},{12,28},{16,0},{20,4},{24,8},{28,12},{1,17},{... | collective-permute-start | bytes 589832 | tf_op jit(solution)/shard_map/ppermute | solution.py:42
  496.5 10.0 %collective-permute-start.45 = (bf16[66,768]{1,0:T(8,128)(2,1)S(1)}, bf16[66,768]{1,0:T(8,128)(2,1)S(1)}, u32[]{:S(2)}, u32[]{:S(2)}) collective-permute-start(bf16[66,768]{1,0:T(8,128)(2,1)S(1)} %maximum_select_fusion.11), channel_id=1, source_target_pairs={{0,16},{4,20},{8,24},{12,28},{16,0},{20,4},{24,8},{28,12},{1,17},{... | collective-permute-start | bytes 304136 | tf_op jit(solution)/shard_map/ppermute | solution.py:42
  500.1 26.5 %collective-permute-start.67 = (bf16[256,1816]{0,1:T(8,128)(2,1)}, bf16[256,1816]{0,1:T(8,128)(2,1)}, u32[]{:S(2)}, u32[]{:S(2)}) collective-permute-start(bf16[256,1816]{0,1:T(8,128)(2,1)} %fusion.2), channel_id=1, source_target_pairs={{0,2},{1,3},{2,0},{3,1},{4,6},{5,7},{6,4},{7,5},{8,10},{9,11},{10,... | collective-permute-start | bytes 2789384 | tf_op jit(solution)/shard_map/ppermute | solution.py:42
  506.5 8.1 %collective-permute-start.46 = (bf16[132,768]{1,0:T(8,128)(2,1)S(1)}, bf16[132,768]{1,0:T(8,128)(2,1)S(1)}, u32[]{:S(2)}, u32[]{:S(2)}) collective-permute-start(bf16[132,768]{1,0:T(8,128)(2,1)S(1)} %maximum_select_fusion.9), channel_id=1, source_target_pairs={{0,8},{4,12},{8,0},{12,4},{16,24},{20,28},{24,16},{28,20},{1,9},{5... | collective-permute-start | bytes 608264 | tf_op jit(solution)/shard_map/ppermute | solution.py:42
  506.7 88.5 %collective-permute-start.64 = (bf16[128,1536]{1,0:T(8,128)(2,1)S(1)}, bf16[128,1536]{1,0:T(8,128)(2,1)}, u32[]{:S(2)}, u32[]{:S(2)}) collective-permute-start(bf16[128,1536]{1,0:T(8,128)(2,1)S(1)} %maximum_select_fusion.7), channel_id=1, source_target_pairs={{0,8},{4,12},{8,0},{12,4},{16,24},{20,28},{24,16},{28,20},{1,9},{5... | collective-permute-start | bytes 1179656 | tf_op jit(solution)/shard_map/ppermute | solution.py:42
  509.8 16.6 %collective-permute-start.51 = (bf16[128,1024]{1,0:T(8,128)(2,1)}, bf16[128,1024]{1,0:T(8,128)(2,1)S(1)}, u32[]{:S(2)}, u32[]{:S(2)}) collective-permute-start(bf16[128,1024]{1,0:T(8,128)(2,1)} %select_convert_fusion.5), channel_id=1, source_target_pairs={{0,8},{4,12},{8,0},{12,4},{16,24},{20,28},{24,16},{28,20},{1,9},{5... | collective-permute-start | bytes 786440 | tf_op jit(solution)/shard_map/ppermute | solution.py:42
  528.7 10.5 %collective-permute-start.68 = (bf16[128,1816]{0,1:T(8,128)(2,1)S(1)}, bf16[128,1816]{0,1:T(8,128)(2,1)S(1)}, u32[]{:S(2)}, u32[]{:S(2)}) collective-permute-start(bf16[128,1816]{0,1:T(8,128)(2,1)S(1)} %select_convert_fusion.3), channel_id=1, source_target_pairs={{0,4},{4,0},{8,12},{12,8},{16,20},{20,16},{24,28},{28,24},{1,5},{5... | collective-permute-start | bytes 1394696 | tf_op jit(solution)/shard_map/ppermute | solution.py:42
  529.8 8.6 %collective-permute-start.52 = (bf16[64,1024]{1,0:T(8,128)(2,1)S(1)}, bf16[64,1024]{1,0:T(8,128)(2,1)S(1)}, u32[]{:S(2)}, u32[]{:S(2)}) collective-permute-start(bf16[64,1024]{1,0:T(8,128)(2,1)S(1)} %select_convert_fusion.8), channel_id=1, source_target_pairs={{0,16},{4,20},{8,24},{12,28},{16,0},{20,4},{24,8},{28,12},{1,17},{... | collective-permute-start | bytes 393224 | tf_op jit(solution)/shard_map/ppermute | solution.py:42
  539.5 16.1 %collective-permute-start.69 = (bf16[64,1816]{0,1:T(8,128)(2,1)S(1)}, bf16[64,1816]{0,1:T(8,128)(2,1)S(1)}, u32[]{:S(2)}, u32[]{:S(2)}) collective-permute-start(bf16[64,1816]{0,1:T(8,128)(2,1)S(1)} %select_convert_fusion.2), channel_id=1, source_target_pairs={{0,8},{4,12},{8,0},{12,4},{16,24},{20,28},{24,16},{28,20},{1,9},{5... | collective-permute-start | bytes 697352 | tf_op jit(solution)/shard_map/ppermute | solution.py:42
  544.6 16.6 %collective-permute-start.54 = (bf16[128,1024]{1,0:T(8,128)(2,1)S(1)}, bf16[128,1024]{1,0:T(8,128)(2,1)S(1)}, u32[]{:S(2)}, u32[]{:S(2)}) collective-permute-start(bf16[128,1024]{1,0:T(8,128)(2,1)S(1)} %maximum_select_fusion.8), channel_id=1, source_target_pairs={{0,8},{4,12},{8,0},{12,4},{16,24},{20,28},{24,16},{28,20},{1,9},{5... | collective-permute-start | bytes 786440 | tf_op jit(solution)/shard_map/ppermute | solution.py:42
  556.1 28.3 %collective-permute-start.70 = (bf16[32,1816]{0,1:T(8,128)(2,1)S(1)}, bf16[32,1816]{0,1:T(8,128)(2,1)S(1)}, u32[]{:S(2)}, u32[]{:S(2)}) collective-permute-start(bf16[32,1816]{0,1:T(8,128)(2,1)S(1)} %select_convert_fusion.1), channel_id=1, source_target_pairs={{0,16},{4,20},{8,24},{12,28},{16,0},{20,4},{24,8},{28,12},{1,17},{... | collective-permute-start | bytes 348680 | tf_op jit(solution)/shard_map/ppermute | solution.py:42
  561.4 41.6 %collective-permute-start.55 = (bf16[256,1024]{1,0:T(8,128)(2,1)S(1)}, bf16[256,1024]{1,0:T(8,128)(2,1)}, u32[]{:S(2)}, u32[]{:S(2)}) collective-permute-start(bf16[256,1024]{1,0:T(8,128)(2,1)S(1)} %maximum_select_fusion.3), channel_id=1, source_target_pairs={{0,4},{4,0},{8,12},{12,8},{16,20},{20,16},{24,28},{28,24},{1,5},{5... | collective-permute-start | bytes 1572872 | tf_op jit(solution)/shard_map/ppermute | solution.py:42
  584.8 9.6 %collective-permute-start.71 = (bf16[32,1816]{0,1:T(8,128)(2,1)S(1)}, bf16[32,1816]{0,1:T(8,128)(2,1)S(1)}, u32[]{:S(2)}, u32[]{:S(2)}) collective-permute-start(bf16[32,1816]{0,1:T(8,128)(2,1)S(1)} %add_convert_fusion), channel_id=1, source_target_pairs={{0,16},{4,20},{8,24},{12,28},{16,0},{20,4},{24,8},{28,12},{1,17},{... | collective-permute-start | bytes 348680 | tf_op jit(solution)/shard_map/ppermute | solution.py:42
  595.1 9.5 %collective-permute-start.72 = (bf16[64,1816]{0,1:T(8,128)(2,1)S(1)}, bf16[64,1816]{0,1:T(8,128)(2,1)}, u32[]{:S(2)}, u32[]{:S(2)}) collective-permute-start(bf16[64,1816]{0,1:T(8,128)(2,1)S(1)} %maximum_select_fusion.4), channel_id=1, source_target_pairs={{0,8},{4,12},{8,0},{12,4},{16,24},{20,28},{24,16},{28,20},{1,9},{5... | collective-permute-start | bytes 697352 | tf_op jit(solution)/shard_map/ppermute | solution.py:42
  606.3 15.1 %collective-permute-start.73 = (bf16[128,1816]{0,1:T(8,128)(2,1)S(1)}, bf16[128,1816]{0,1:T(8,128)(2,1)S(1)}, u32[]{:S(2)}, u32[]{:S(2)}) collective-permute-start(bf16[128,1816]{0,1:T(8,128)(2,1)S(1)} %maximum_select_fusion.5), channel_id=1, source_target_pairs={{0,4},{4,0},{8,12},{12,8},{16,20},{20,16},{24,28},{28,24},{1,5},{5... | collective-permute-start | bytes 1394696 | tf_op jit(solution)/shard_map/ppermute | solution.py:42
  (92 other events, 1013.4 us)
Sparse Core Ops, SparseCore 0:
  9.6 68.6 all-gather.3
  80.4 34.7 all-gather.5
  269.1 159.1 all-reduce.3
